TPU v7x, 32 devices: a whole 2x2x4 slice. The times are simulated.
32 devices in a mesh: px: 16 (over z, y, x), py: 2 (over core).
Axes of the slice: x: 2, y: 2, z: 4, core: 2. Of those that a mesh axis runs over, the one named last changes fastest.
Arguments:
- start_value: float32 [128, 256, 256], P(None, 'px', 'py'), may hold values from -6 to 6
- prior: float32 [128, 256, 256], P('px', None, 'py'), may hold values from -6 to 6
- reach: float32 [256, 256], P('px', 'py'), may hold values from -6 to 6
- avoid: float32 [256, 256], P('px', 'py'), may hold values from -3 to 0.5
Outputs:
- final_value: float32 [128, 256, 256], P(None, 'px', 'py')
All inputs are finite; a program needn't handle non-finite values.
Results may differ from a plain program's by a relative error of at most 0.00002.
Values sent between devices are 32-bit elements; how exact they have to be, the bound alone decides.
No kernel may reach another device: no remote copies, remote signals or barrier semaphores. Data moves between devices by JAX's collectives and lax.ppermute only.
A program may use at most 64 MiB of HBM per device.

v0:
```python
import math

import jax
import jax.numpy as jnp
from jax import lax
from jax.sharding import PartitionSpec as P

epsilon = 1e-06
spacing = 1.0 / 64.0
speed = 1.0
turn_rate = 2.0
courant = 0.5


def extended_2(block, sides, width):
    for axis, dim in sides:
        count = lax.axis_size(axis)
        forward = [(i, i + 1) for i in range(count - 1)]
        backward = [(target, source) for source, target in forward]
        low = lax.ppermute(
            lax.slice_in_dim(block, block.shape[dim] - width, None, axis=dim), axis, forward
        )
        high = lax.ppermute(lax.slice_in_dim(block, 0, width, axis=dim), axis, backward)
        block = jnp.concatenate([low, block, high], axis=dim)
    return block


def upwind_blend(first, second, third, fourth, fifth):
    stencil_one = first / 3.0 - 7.0 * second / 6.0 + 11.0 * third / 6.0
    stencil_two = -second / 6.0 + 5.0 * third / 6.0 + fourth / 3.0
    stencil_three = third / 3.0 + 5.0 * fourth / 6.0 - fifth / 6.0
    smooth_one = 13.0 / 12.0 * jnp.square(first - 2.0 * second + third) + 0.25 * jnp.square(
        first - 4.0 * second + 3.0 * third
    )
    smooth_two = 13.0 / 12.0 * jnp.square(second - 2.0 * third + fourth) + 0.25 * jnp.square(
        second - fourth
    )
    smooth_three = 13.0 / 12.0 * jnp.square(third - 2.0 * fourth + fifth) + 0.25 * jnp.square(
        3.0 * third - 4.0 * fourth + fifth
    )
    weight_one = 0.1 / jnp.square(epsilon + smooth_one)
    weight_two = 0.6 / jnp.square(epsilon + smooth_two)
    weight_three = 0.3 / jnp.square(epsilon + smooth_three)
    total = weight_one * stencil_one + weight_two * stencil_two + weight_three * stencil_three
    return total / (weight_one + weight_two + weight_three)


def one_sided(padded, along, length, width):
    slopes = (
        lax.slice_in_dim(padded, 1, length + 6, axis=along)
        - lax.slice_in_dim(padded, 0, length + 5, axis=along)
    ) / width
    pieces = [lax.slice_in_dim(slopes, offset, offset + length, axis=along) for offset in range(6)]
    backward = upwind_blend(pieces[0], pieces[1], pieces[2], pieces[3], pieces[4])
    forward = upwind_blend(pieces[5], pieces[4], pieces[3], pieces[2], pieces[1])
    return (backward, forward)


def change_rate(extended):
    headings = extended.shape[0]
    row_count = extended.shape[1] - 6
    col_count = extended.shape[2] - 6
    heading_gap = 2.0 * math.pi / headings
    center = extended[:, 3 : 3 + row_count, 3 : 3 + col_count]
    west_slope, east_slope = one_sided(extended[:, :, 3 : 3 + col_count], 1, row_count, spacing)
    south_slope, north_slope = one_sided(extended[:, 3 : 3 + row_count, :], 2, col_count, spacing)
    wrapped = jnp.concatenate([center[headings - 3 :], center, center[:3]], axis=0)
    right_slope, left_slope = one_sided(wrapped, 0, headings, heading_gap)
    angles = heading_gap * jnp.arange(headings, dtype=jnp.float32)
    cosine = jnp.cos(angles)[:, None, None]
    sine_value = jnp.sin(angles)[:, None, None]
    result = cosine * speed * 0.5 * (west_slope + east_slope) + sine_value * speed * 0.5 * (
        south_slope + north_slope
    )
    result = result - turn_rate * jnp.abs(0.5 * (right_slope + left_slope))
    result = result + speed * jnp.abs(cosine) * 0.5 * (east_slope - west_slope)
    result = result + speed * jnp.abs(sine_value) * 0.5 * (north_slope - south_slope)
    return result + turn_rate * 0.5 * (left_slope - right_slope)


def section_update(extended):
    headings = extended.shape[0]
    heading_gap = 2.0 * math.pi / headings
    time_step = courant / (2.0 * speed / spacing + turn_rate / heading_gap)
    center = extended[:, 3 : extended.shape[1] - 3, 3 : extended.shape[2] - 3]
    return center + time_step * change_rate(extended)


def trim(field, margin):
    return field[:, margin : field.shape[1] - margin, margin : field.shape[2] - margin]


def on_device(start_value, prior, reach, avoid):
    regrouped = lax.all_to_all(prior, "px", split_axis=1, concat_axis=0, tiled=True)
    tile_rows = start_value.shape[1]
    tile_cols = start_value.shape[2]
    values = start_value
    row_pos = lax.axis_index("px") * tile_rows - 9 + jnp.arange(tile_rows + 18, dtype=jnp.int32)
    col_pos = lax.axis_index("py") * tile_cols - 9 + jnp.arange(tile_cols + 18, dtype=jnp.int32)
    row_inside = (row_pos >= 0) & (row_pos < tile_rows * lax.axis_size("px"))
    col_inside = (col_pos >= 0) & (col_pos < tile_cols * lax.axis_size("py"))
    inside = (row_inside[:, None] & col_inside[None, :]).astype(jnp.float32)[None]
    extended = extended_2(values, (("px", 1), ("py", 2)), 9)
    first = section_update(extended) * trim(inside, 3)
    second = (0.75 * trim(extended, 6) + 0.25 * section_update(first)) * trim(inside, 6)
    third = trim(extended, 9) / 3.0 + 2.0 / 3.0 * section_update(second)
    values = jnp.minimum(regrouped, jnp.maximum(avoid[None], jnp.minimum(reach[None], third)))
    return values


def solution(mesh):
    return jax.shard_map(
        on_device,
        mesh=mesh,
        in_specs=(P(None, "px", "py"), P("px", None, "py"), P("px", "py"), P("px", "py")),
        out_specs=P(None, "px", "py"),
        check_vma=False,
    )
```

profile of v0, /device:TPU:10, one launch (start us, length us, event | category | flops | bytes accessed | tf_op | source)
XLA Modules:
  0.0 142.2 jit_solution(3829122154147356272)
XLA Ops:
  0.0 1.7 %fusion.18 = (f32[128,9,128]{2,1,0:T(8,128)S(1)}, f32[128,9,128]{2,1,0:T(8,128)S(1)}) fusion(f32[128,16,128]{2,1,0:T(8,128)} %param.4), kind=kLoop, calls=%fused_computation.45 | loop fusion | bytes 2359296 | tf_op jit(solution)/shard_map/slice | solution.py:21
  1.9 3.5 %collective-permute-start = (f32[128,9,128]{2,0,1:T(8,128)S(1)}, f32[128,9,128]{2,0,1:T(8,128)}, u32[]{:S(2)}, u32[]{:S(2)}) collective-permute-start(f32[128,9,128]{2,0,1:T(8,128)S(1)} %copy.53), channel_id=1, source_target_pairs={{0,2},{2,4},{4,6},{6,8},{8,10},{10,12},{12,14},{14,16},{16,18},{18... | collective-permute-start | bytes 1769480 | tf_op jit(solution)/shard_map/ppermute | solution.py:20
  5.7 2.6 %collective-permute-start.1 = (f32[128,9,128]{2,0,1:T(8,128)S(1)}, f32[128,9,128]{2,0,1:T(8,128)}, u32[]{:S(2)}, u32[]{:S(2)}) collective-permute-start(f32[128,9,128]{2,0,1:T(8,128)S(1)} %copy.54), channel_id=1, source_target_pairs={{2,0},{4,2},{6,4},{8,6},{10,8},{12,10},{14,12},{16,14},{18,16},{20... | collective-permute-start | bytes 1769480 | tf_op jit(solution)/shard_map/ppermute | solution.py:23
  8.3 1.6 %copy.37 = f32[8,256,128]{2,0,1:T(8,128)} copy(f32[8,256,128]{2,1,0:T(8,128)S(1)} %copy-done.2) | data formatting | bytes 2097152 | tf_op args[1]
  9.9 8.0 %all-to-all-start = ((f32[8,256,128]{2,0,1:T(8,128)}), f32[8,256,128]{2,0,1:T(8,128)}, u32[]{:S(2)}, u32[]{:S(2)}) async-start(f32[8,256,128]{2,0,1:T(8,128)} %copy.37), calls=%async_computation | async-start | bytes 2097152 | tf_op jit(solution)/shard_map/all_to_all | solution.py:94
  18.6 17.1 %collective-permute-done = f32[128,9,128]{2,0,1:T(8,128)} collective-permute-done((f32[128,9,128]{2,0,1:T(8,128)S(1)}, f32[128,9,128]{2,0,1:T(8,128)}, u32[]{:S(2)}, u32[]{:S(2)}) %collective-permute-start) | collective-permute-done | bytes 589856 | tf_op jit(solution)/shard_map/ppermute | solution.py:20
  35.7 1.3 copy.43
  37.0 8.0 %collective-permute-done.1 = f32[128,9,128]{2,0,1:T(8,128)} collective-permute-done((f32[128,9,128]{2,0,1:T(8,128)S(1)}, f32[128,9,128]{2,0,1:T(8,128)}, u32[]{:S(2)}, u32[]{:S(2)}) %collective-permute-start.1) | collective-permute-done | bytes 589856 | tf_op jit(solution)/shard_map/ppermute | solution.py:23
  45.0 1.3 copy.45
  46.4 1.3 collective-permute-start.2
  47.8 1.3 collective-permute-start.3
  49.2 1.9 %collective-permute-done.3 = f32[128,34,9]{0,1,2:T(8,128)S(1)} collective-permute-done((f32[128,34,9]{0,1,2:T(8,128)S(1)}, f32[128,34,9]{0,1,2:T(8,128)S(1)}, u32[]{:S(2)}, u32[]{:S(2)}) %collective-permute-start.3) | collective-permute-done | bytes 156704 | tf_op jit(solution)/shard_map/ppermute | solution.py:23
  52.8 1.7 %pad_maximum_fusion = f32[134,28,140]{0,2,1:T(8,128)S(1)} fusion(f32[3,28,140]{0,2,1:T(8,128)S(1)} %get-tuple-element.6, f32[128,28,140]{0,2,1:T(8,128)S(1)} %slice.380, f32[3,28,140]{0,2,1:T(8,128)S(1)} %get-tuple-element.5), kind=kLoop, calls=%fused_computation.2 | loop fusion | flops 1050560 | bytes 4202240 | tf_op jit(solution)/shard_map/concatenate | solution.py:67
  54.5 1.1 fusion
  55.6 29.6 %add_multiply_fusion = f32[128,28,140]{0,2,1:T(8,128)S(1)} fusion(f32[133,28,140]{0,2,1:T(8,128)S(1)} %fusion, f32[128,28,145]{0,2,1:T(8,128)S(1)} %fusion.3, f32[128,33,140]{0,2,1:T(8,128)S(1)} %fusion.2, f32[28,140]{1,0:T(8,128)S(1)} %slice_bitcast_fusion, f32[128]{0:T(128)S(1)} %get-tuple-element.15, f32[128]{0:T(128)S(1)} %get-tuple-element.16, ...), kind=kLoop, calls=%fused_computation.14 | loop fusion | flops 197191680 | bytes 40158528 | tf_op jit(solution)/shard_map/mul | solution.py:104
  86.4 1.3 pad_maximum_fusion.1
  88.5 22.1 %fusion.8 = f32[128,22,134]{0,2,1:T(8,128)S(1)} fusion(f32[128,34,146]{0,2,1:T(8,128)S(1)} %pad_maximum_fusion.2, f32[133,22,134]{0,2,1:T(8,128)S(1)} %fusion.1, f32[128,22,139]{0,2,1:T(8,128)S(1)} %fusion.6, f32[128,27,134]{0,2,1:T(8,128)S(1)} %fusion.5, f32[22,134]{1,0:T(8,128)S(1)} %slice_bitcast_fusion.1, f32[128]{0:T(128)S(1)} %get-tuple-element.15, ...), kind=kLoop, calls=%fused_computation.21 | loop fusion | flops 149428224 | bytes 31710736 | tf_op jit(solution)/shard_map/mul | solution.py:105
  111.1 0.9 pad_maximum_fusion.3
  112.2 1.3 fusion.9
  113.5 2.0 %fusion.4 = f32[133,16,128]{0,2,1:T(8,128)} fusion(f32[134,16,128]{0,2,1:T(8,128)S(1)} %pad_maximum_fusion.3), kind=kLoop, calls=%fused_computation.12 | loop fusion | flops 544768 | bytes 3268608 | tf_op jit(solution)/shard_map/div | solution.py:49
  115.4 2.4 %copy.39 = f32[16,8,16,128]{3,2,1,0:T(8,128)} copy(f32[16,8,16,128]{3,1,2,0:T(8,128)} %bitcast.2) | data formatting | bytes 2097152 | tf_op jit(solution)/shard_map/all_to_all | solution.py:94
  117.8 2.6 %copy.50 = f32[128,16,128]{0,2,1:T(8,128)} copy(f32[128,16,128]{2,1,0:T(8,128)} %bitcast.8) | data formatting | bytes 2097152 | tf_op jit(solution)/shard_map/all_to_all | solution.py:94
  120.4 19.2 %maximum_minimum_fusion = f32[128,16,128]{0,2,1:T(8,128)} fusion(f32[128,16,128]{0,2,1:T(8,128)} %copy.50, f32[133,16,128]{0,2,1:T(8,128)} %fusion.4, f32[128,16,133]{0,2,1:T(8,128)S(1)} %fusion.10, f32[128,21,128]{0,2,1:T(8,128)} %fusion.9, f32[128,16,128]{0,2,1:T(8,128)} %copy-done, f32[128]{0:T(128)S(1)} %get-tuple-element.15, ...), kind=kLoop, calls=%fused_computation.26 | loop fusion | flops 104333312 | bytes 23087104 | tf_op jit(solution)/shard_map/min | solution.py:107
  139.6 2.6 %copy.51 = f32[128,16,128]{2,1,0:T(8,128)} copy(f32[128,16,128]{0,2,1:T(8,128)} %maximum_minimum_fusion) | data formatting | bytes 2097152 | tf_op jit(solution)/shard_map/min | solution.py:107
  (40 shorter events, 5.6 us)
Async XLA Ops:
  1.7 6.5 %copy-start.2 = (f32[8,256,128]{2,1,0:T(8,128)S(1)}, f32[8,256,128]{2,1,0:T(8,128)}, u32[]{:S(2)}) copy-start(f32[8,256,128]{2,1,0:T(8,128)} %param.5) | copy-start | bytes 3145732
  1.9 33.8 %collective-permute-start = (f32[128,9,128]{2,0,1:T(8,128)S(1)}, f32[128,9,128]{2,0,1:T(8,128)}, u32[]{:S(2)}, u32[]{:S(2)}) collective-permute-start(f32[128,9,128]{2,0,1:T(8,128)S(1)} %copy.53), channel_id=1, source_target_pairs={{0,2},{2,4},{4,6},{6,8},{8,10},{10,12},{12,14},{14,16},{16,18},{18... | collective-permute-start | bytes 1769480 | tf_op jit(solution)/shard_map/ppermute | solution.py:20
  5.7 12.2 %copy-start.1 = (f32[128,16,128]{2,1,0:T(8,128)S(1)}, f32[128,16,128]{2,1,0:T(8,128)}, u32[]{:S(2)}) copy-start(f32[128,16,128]{2,1,0:T(8,128)} %param.4) | copy-start | bytes 3145732
  5.7 39.3 %collective-permute-start.1 = (f32[128,9,128]{2,0,1:T(8,128)S(1)}, f32[128,9,128]{2,0,1:T(8,128)}, u32[]{:S(2)}, u32[]{:S(2)}) collective-permute-start(f32[128,9,128]{2,0,1:T(8,128)S(1)} %copy.54), channel_id=1, source_target_pairs={{2,0},{4,2},{6,4},{8,6},{10,8},{12,10},{14,12},{16,14},{18,16},{20... | collective-permute-start | bytes 1769480 | tf_op jit(solution)/shard_map/ppermute | solution.py:23
  9.9 105.6 %all-to-all-start = ((f32[8,256,128]{2,0,1:T(8,128)}), f32[8,256,128]{2,0,1:T(8,128)}, u32[]{:S(2)}, u32[]{:S(2)}) async-start(f32[8,256,128]{2,0,1:T(8,128)} %copy.37), calls=%async_computation | async-start | bytes 2097152 | tf_op jit(solution)/shard_map/all_to_all | solution.py:94
  18.3 32.8 %copy-start = (f32[128,16,128]{0,2,1:T(8,128)}, f32[128,16,128]{0,2,1:T(8,128)S(1)}, u32[]{:S(2)}) copy-start(f32[128,16,128]{0,2,1:T(8,128)S(1)} %copy.40) | copy-start | bytes 3145732
  46.4 2.8 %collective-permute-start.2 = (f32[128,34,9]{0,1,2:T(8,128)S(1)}, f32[128,34,9]{0,1,2:T(8,128)S(1)}, u32[]{:S(2)}, u32[]{:S(2)}) collective-permute-start(f32[128,34,9]{0,1,2:T(8,128)S(1)} %copy.46), channel_id=1, source_target_pairs={{0,1},{2,3},{4,5},{6,7},{8,9},{10,11},{12,13},{14,15},{16,17},{18,... | collective-permute-start | bytes 470024 | tf_op jit(solution)/shard_map/ppermute | solution.py:20
  47.8 3.3 %collective-permute-start.3 = (f32[128,34,9]{0,1,2:T(8,128)S(1)}, f32[128,34,9]{0,1,2:T(8,128)S(1)}, u32[]{:S(2)}, u32[]{:S(2)}) collective-permute-start(f32[128,34,9]{0,1,2:T(8,128)S(1)} %copy.47), channel_id=1, source_target_pairs={{1,0},{3,2},{5,4},{7,6},{9,8},{11,10},{13,12},{15,14},{17,16},{19,... | collective-permute-start | bytes 470024 | tf_op jit(solution)/shard_map/ppermute | solution.py:23
  115.4 5.0 %copy-start.3 = (f32[16,128]{1,0:T(8,128)S(1)}, f32[16,128]{1,0:T(8,128)}, u32[]{:S(2)}) copy-start(f32[16,128]{1,0:T(8,128)} %param.6) | copy-start | bytes 24580
  115.4 5.0 %copy-start.4 = (f32[16,128]{1,0:T(8,128)S(1)}, f32[16,128]{1,0:T(8,128)}, u32[]{:S(2)}) copy-start(f32[16,128]{1,0:T(8,128)} %param.7) | copy-start | bytes 24580
where the time goes:
time: 143 us; the launch traced here: 142 us
  other arithmetic  81.6 us (57%)
  waiting for transfers between devices  27 us (19%)
  starting transfers between devices  16.7 us (12%)
  local copies, waits for them, and re-layouts  16.6 us (12%)
    mul x1, other arithmetic, on_device(): first = section_update(extended) * trim(inside, 3)  29.6 us
    mul x1, other arithmetic, on_device(): (0.75 * trim(extended, 6) + 0.25 * section_update(first)) * trim(inside, 6)  22.1 us
    min x1, other arithmetic, on_device(): jnp.minimum(regrouped, jnp.maximum(avoid[None], jnp.minimum(reach[None],...  19.2 us
    ppermute x2, waiting for transfers between devices, extended_2(): lax.ppermute(lax.slice_in_dim(block, block.shape[dim] - width, None, axis...  17.1 us
    ppermute x2, waiting for transfers between devices, extended_2(): lax.ppermute(lax.slice_in_dim(block, 0, width, axis=dim), axis, backward)  9.82 us
    all_to_all x1, starting transfers between devices, on_device(): lax.all_to_all(prior, 'px', split_axis=1, concat_axis=0, tiled=True)  8.01 us
    div x9, other arithmetic, one_sided(): (lax.slice_in_dim(padded, 1, length + 6, axis=along) - lax.slice_in_dim(p...  6.45 us
    all_to_all x2, local copies, waits for them, and re-layouts, on_device(): lax.all_to_all(prior, 'px', split_axis=1, concat_axis=0, tiled=True)  5.01 us
  transfers between devices with their start and end apart: 5, of which 3 were waited for; matrix products, arithmetic and copies ran while one was open for 49% of the time, Pallas kernels for 0%

commit v1 on v0

v1 whole, which is shorter than its diff:
```python
import functools
import math

import jax
import jax.numpy as jnp
import numpy as np
from jax import lax
from jax.experimental import pallas as pl
from jax.experimental.pallas import tpu as pltpu
from jax.sharding import PartitionSpec as P

EPS = 1e-06
SPACING = 1.0 / 64.0
SPEED = 1.0
TURN = 2.0
COURANT = 0.5
SCALE = 16.0
LANES = 128
SUB = 8
DEPTH = 9
OFF = 16


def ceil_div(a, b):
    return -(-a // b)


def stage_constants(headings, share):
    gap = 2.0 * math.pi / headings
    dt = COURANT / (2.0 * SPEED / SPACING + TURN / gap)
    angles = (np.float32(gap) * np.arange(headings, dtype=np.float32)).astype(np.float64)
    rows = []
    for wave in (np.cos(angles), np.sin(angles)):
        g = share * dt * SPEED * wave / SPACING
        ahead = wave >= 0
        rows += [
            g,
            np.where(ahead, -g / 3, g / 6),
            np.where(ahead, -g / 6, g / 3),
            np.where(ahead, 0.5, 1.0 / 6.0),
            np.where(ahead, 1.0 / 6.0, 0.5),
            np.where(ahead, g / 6, -g / 3),
            np.where(ahead, g / 3, -g / 6),
            np.where(ahead, 1.0, 0.0),
        ]
    turn = share * dt * TURN / (6.0 * gap)
    return np.stack(rows).astype(np.float32), float(turn)


def indicators(a, b, d, eps):
    bd = b * d
    ad = a * d
    ab = a * b
    mid = (bd - ad) * (2.0 / 3.0) + (ab * 0.5 + eps)
    return mid + bd, mid, mid - ad


def inverse(x):
    r = pl.reciprocal(x, approx=True)
    return r * (2.0 - x * r)


def sided(vals, coef, eps):
    n = len(vals)
    g, r2, r3, n1c, n3c, k1, k3 = coef
    u = [vals[i + 1] - vals[i] for i in range(n - 1)]
    w = [None] + [u[i] - u[i - 1] for i in range(1, n - 1)]
    d = [None] + [w[i + 1] - w[i] for i in range(1, n - 2)]
    tri = [None] + [indicators(w[i], w[i + 1], d[i], eps) for i in range(1, n - 2)]
    third = [None, None] + [d[i] - d[i - 1] for i in range(2, n - 2)]
    faces = {}
    for k in range(2, n - 3):
        low = tri[k - 1][0]
        mid = tri[k][1]
        high = tri[k + 1][2]
        mh = mid * high
        lh = low * high
        lm = low * mid
        m1 = (mh * mh) * n1c
        m2 = lh * lh
        m3 = (lm * lm) * n3c
        den = (m1 + m3) + m2
        num = m1 * (k1 * third[k]) + m3 * (k3 * third[k + 1])
        smooth = g * u[k] + r2 * w[k] + r3 * w[k + 1]
        faces[k] = smooth + num * inverse(den)
    return faces


def turning(v, eps):
    ahead = lambda x: pltpu.roll(x, LANES - 1, x.ndim - 1)
    behind = lambda x: pltpu.roll(x, 1, x.ndim - 1)
    u = ahead(v) - v
    w = u - behind(u)
    wn = ahead(w)
    d = wn - w
    low, mid, high = indicators(w, wn, d, eps)
    low = behind(low)
    high = ahead(high)
    g1 = d - behind(d)
    g2 = ahead(g1)
    mh = mid * high
    lh = low * high
    lm = low * mid
    m1 = mh * mh
    m2 = lh * lh
    m3 = lm * lm
    v0 = (m1 + m3) * 0.5 + m2 * 3.0
    a1 = m1 * g1
    a3 = m3 * g2
    s = w + wn
    top = u * 6.0 + wn + s
    back = (a1 + 1.5 * a3) * inverse(v0 + m3) - top
    fore = (top - 3.0 * s) + (a3 + 1.5 * a1) * inverse(v0 + m1)
    return jnp.minimum(behind(back), fore)


def prep_kernel(x_ref, o_ref):
    rows = o_ref.shape[0]
    for r in range(rows):
        o_ref[r] = x_ref[pl.ds(r, LANES, stride=rows), :].T * SCALE


def stage(src, dst, part, base, const_ref, lo, hi, seg, start, turn, eps_xy, eps_t, weights, row_of, rows_dst):
    def column(ref, row, j):
        return ref[row, pl.ds(OFF + start + j, SUB, stride=seg), :]

    def const(i):
        return const_ref[pl.ds(i, SUB, stride=0), :]

    xcoef = [const(i) for i in range(7)]
    ycoef = [const(i) for i in range(8, 15)]
    xmask = const(7) > 0.5
    ymask = const(15) > 0.5

    @pl.loop(0, seg)
    def _(j):
        vals = [column(src, row_of(r), j) for r in range(lo - 3, hi + 3)]
        faces = sided(vals, xcoef, eps_xy)
        for r in range(lo, hi):
            i = r - lo + 3
            move = jnp.where(xmask, faces[i], faces[i - 1])
            here = vals[i]
            if weights is not None:
                here = here * weights[0] + column(base, r + DEPTH, j) * weights[1]
            part[r - lo, j] = here + move

    @pl.loop(0, hi - lo)
    def _(r):
        vals = [column(src, row_of(lo) + r, j) for j in range(-3, seg + 3)]
        faces = sided(vals, ycoef, eps_xy)
        for j in range(seg):
            i = j + 3
            move = jnp.where(ymask, faces[i], faces[i - 1])
            out = part[r, j] + move + turn * turning(vals[i], eps_t)
            dst[r, pl.ds(OFF + start + j, SUB, stride=seg), :] = out


def main_kernel(edge_ref, const_ref, mid_ref, low_ref, high_ref, ylow_ref, yhigh_ref, o_ref, field, one, two, part, *, consts, sizes):
    rows, cols, headings = sizes
    gap = 2.0 * math.pi / headings
    eps_xy = 0.5 * EPS * (SCALE * SPACING) ** 2
    eps_t = 0.5 * EPS * (SCALE * gap) ** 2
    first_row = edge_ref[0] == 1
    last_row = edge_ref[1] == 1
    first_col = edge_ref[2] == 1
    last_col = edge_ref[3] == 1

    body = pl.ds(OFF, cols)
    field[pl.ds(0, DEPTH), body, :] = low_ref[...]
    field[pl.ds(DEPTH, rows), body, :] = mid_ref[...]
    field[pl.ds(DEPTH + rows, DEPTH), body, :] = high_ref[...]
    field[:, pl.ds(0, OFF), :] = ylow_ref[...]
    field[:, pl.ds(OFF + cols, OFF), :] = yhigh_ref[...]

    @pl.when(first_col)
    def _():
        field[:, pl.ds(0, OFF), :] = jnp.zeros((rows + 2 * DEPTH, OFF, LANES), jnp.float32)

    @pl.when(last_col)
    def _():
        field[:, pl.ds(OFF + cols, OFF), :] = jnp.zeros((rows + 2 * DEPTH, OFF, LANES), jnp.float32)

    def clear(ref, margin):
        count = rows + 2 * margin

        @pl.when(first_row)
        def _():
            ref[pl.ds(0, margin)] = jnp.zeros((margin,) + ref.shape[1:], jnp.float32)

        @pl.when(last_row)
        def _():
            ref[pl.ds(margin + rows, margin)] = jnp.zeros((margin,) + ref.shape[1:], jnp.float32)

        @pl.when(first_col)
        def _():
            ref[pl.ds(0, count), pl.ds(0, OFF), :] = jnp.zeros((count, OFF, LANES), jnp.float32)

        @pl.when(last_col)
        def _():
            ref[pl.ds(0, count), pl.ds(OFF + cols, OFF), :] = jnp.zeros((count, OFF, LANES), jnp.float32)

    def run(index, src, src_depth, dst, margin):
        seg = ceil_div(cols + 2 * margin, SUB)
        start = -((seg * SUB - cols) // 2)
        weights = (None, (0.25, 0.75), (2.0 / 3.0, 1.0 / 3.0))[index]
        stage(src, dst, part, field, const_ref.at[index], -margin, rows + margin, seg, start, consts[index],
              eps_xy, eps_t, weights, lambda r: r + src_depth, None)

    run(0, field, DEPTH, one, 6)
    clear(one, 6)
    run(1, one, 6, two, 3)
    clear(two, 3)
    run(2, two, 3, one, 0)
    for r in range(rows):
        o_ref[pl.ds(r, LANES, stride=rows), :] = one[r, pl.ds(OFF, cols), :].T * (1.0 / SCALE)


def on_device(start_value, prior, reach, avoid):
    headings, rows, cols = start_value.shape
    assert headings == LANES and cols == LANES
    regrouped = lax.all_to_all(prior, "px", split_axis=1, concat_axis=0, tiled=True)
    nx, ny = lax.axis_size("px"), lax.axis_size("py")
    px, py = lax.axis_index("px"), lax.axis_index("py")
    vmem = pl.BlockSpec(memory_space=pltpu.VMEM)
    f32 = jnp.float32
    mid = pl.pallas_call(
        prep_kernel,
        out_shape=jax.ShapeDtypeStruct((rows, cols, headings), f32),
        in_specs=[vmem],
        out_specs=vmem,
    )(start_value.reshape(headings * rows, cols))
    up = [(i, i + 1) for i in range(nx - 1)]
    down = [(b, a) for a, b in up]
    low = lax.ppermute(mid[rows - DEPTH :], "px", up)
    high = lax.ppermute(mid[:DEPTH], "px", down)
    if ny == 2:
        swap = [(0, 1), (1, 0)]
        first = py == 0
        column = lambda x: jnp.where(first, x[:, cols - OFF :], x[:, :OFF])
        slab = jnp.concatenate([column(low), column(mid), column(high)], axis=0)
        ylow = yhigh = lax.ppermute(slab, "py", swap)
    else:
        yup = [(i, i + 1) for i in range(ny - 1)]
        ydown = [(b, a) for a, b in yup]
        full = jnp.concatenate([low, mid, high], axis=0)
        ylow = lax.ppermute(full[:, cols - OFF :], "py", yup)
        yhigh = lax.ppermute(full[:, :OFF], "py", ydown)
    edges = jnp.stack([px == 0, px == nx - 1, py == 0, py == ny - 1]).astype(jnp.int32)
    tables = [stage_constants(headings, share) for share in (1.0, 0.25, 2.0 / 3.0)]
    table = jnp.asarray(np.stack([t[0] for t in tables]))
    seg = ceil_div(cols + 12, SUB)
    tall = rows + 2 * DEPTH
    wide = cols + 2 * OFF
    third = pl.pallas_call(
        functools.partial(main_kernel, consts=[t[1] for t in tables], sizes=(rows, cols, headings)),
        out_shape=jax.ShapeDtypeStruct((headings * rows, cols), f32),
        in_specs=[pl.BlockSpec(memory_space=pltpu.SMEM)] + [vmem] * 6,
        out_specs=vmem,
        scratch_shapes=[
            pltpu.VMEM((tall, wide, LANES), f32),
            pltpu.VMEM((rows + 12, wide, LANES), f32),
            pltpu.VMEM((rows + 6, wide, LANES), f32),
            pltpu.VMEM((rows + 12, seg, SUB, LANES), f32),
        ],
        compiler_params=pltpu.CompilerParams(vmem_limit_bytes=40 * 2**20),
    )(edges, table, mid, low, high, ylow, yhigh).reshape(headings, rows, cols)
    return jnp.minimum(regrouped, jnp.maximum(avoid[None], jnp.minimum(reach[None], third)))


def solution(mesh):
    return jax.shard_map(
        on_device,
        mesh=mesh,
        in_specs=(P(None, "px", "py"), P("px", None, "py"), P("px", "py"), P("px", "py")),
        out_specs=P(None, "px", "py"),
        check_vma=False,
    )
```

time: 143 us -> 101 us (0.71)
  the two profiles are of different devices: /device:TPU:10 before, /device:TPU:19 now
where the time goes in v1:
time: 101 us
  Pallas kernels  43.8 us (43%)
  waiting for transfers between devices  35.5 us (35%)
  starting transfers between devices  13.7 us (14%)
  local copies, waits for them, and re-layouts  6.38 us (6%)
  other arithmetic  1.24 us (1%)
    pallas_call x1, Pallas kernels, on_device(): pl.pallas_call(functools.partial(main_kernel, consts=[t[1] for t in table...  41.2 us
    ppermute x1, waiting for transfers between devices, on_device(): high = lax.ppermute(mid[:DEPTH], 'px', down)  20.7 us
    ppermute x1, waiting for transfers between devices, on_device(): low = lax.ppermute(mid[rows - DEPTH:], 'px', up)  13.6 us
    all_to_all x1, starting transfers between devices, on_device(): lax.all_to_all(prior, 'px', split_axis=1, concat_axis=0, tiled=True)  6.52 us
    ppermute x1, starting transfers between devices, on_device(): low = lax.ppermute(mid[rows - DEPTH:], 'px', up)  3.99 us
    unnamed x9, local copies, waits for them, and re-layouts  3.56 us
    pallas_call x1, Pallas kernels, on_device(): pl.pallas_call(prep_kernel, out_shape=jax.ShapeDtypeStruct((rows, cols, h...  2.62 us
    ppermute x1, starting transfers between devices, on_device(): high = lax.ppermute(mid[:DEPTH], 'px', down)  2.19 us
  transfers between devices with their start and end apart: 4, of which 3 were waited for; matrix products, arithmetic and copies ran while one was open for 2% of the time, Pallas kernels for 44%

profile of v1, /device:TPU:19, one launch (start us, length us, event | category | flops | bytes accessed | tf_op | source)
XLA Modules:
  0.0 100.7 jit_solution(8369014974832975930)
XLA Ops:
  0.0 2.8 %copy.7 = f32[8,256,128]{2,0,1:T(8,128)} copy(f32[8,256,128]{2,1,0:T(8,128)} %param.6) | data formatting | bytes 2097152 | tf_op args[1]
  2.8 6.5 %all-to-all-start = ((f32[8,256,128]{2,0,1:T(8,128)}), f32[8,256,128]{2,0,1:T(8,128)}, u32[]{:S(2)}, u32[]{:S(2)}) async-start(f32[8,256,128]{2,0,1:T(8,128)} %copy.7), calls=%async_computation | async-start | bytes 2097152 | tf_op jit(solution)/shard_map/all_to_all | solution.py:221
  9.3 2.6 %shard_map.55.mid_ref = f32[16,128,128]{2,1,0:T(8,128)} custom-call(f32[2048,128]{1,0:T(8,128)} %bitcast.12), custom_call_target="tpu_custom_call" | custom-call | tf_op jit(solution)/shard_map/pallas_call | solution.py:226
  12.0 0.0 copy-start
  12.0 1.4 %fusion = (f32[9,128,128]{2,1,0:T(8,128)S(1)}, f32[9,128,128]{2,1,0:T(8,128)S(1)}) fusion(f32[16,128,128]{2,1,0:T(8,128)} %shard_map.55.mid_ref), kind=kLoop, calls=%fused_computation.6 | loop fusion | bytes 2359296 | tf_op jit(solution)/shard_map/slice | solution.py:235
  13.4 2.2 %collective-permute-start.1 = (f32[9,128,128]{2,1,0:T(8,128)S(1)}, f32[9,128,128]{2,1,0:T(8,128)S(1)}, u32[]{:S(2)}, u32[]{:S(2)}) collective-permute-start(f32[9,128,128]{2,1,0:T(8,128)S(1)} %get-tuple-element.5), channel_id=1, source_target_pairs={{2,0},{4,2},{6,4},{8,6},{10,8},{12,10},{14,12},{16,14},{18,16},{20... | collective-permute-start | bytes 1769480 | tf_op jit(solution)/shard_map/ppermute | solution.py:235
  15.6 4.0 %collective-permute-start = (f32[9,128,128]{2,1,0:T(8,128)S(1)}, f32[9,128,128]{2,1,0:T(8,128)S(1)}, u32[]{:S(2)}, u32[]{:S(2)}) collective-permute-start(f32[9,128,128]{2,1,0:T(8,128)S(1)} %get-tuple-element.6), channel_id=1, source_target_pairs={{0,2},{2,4},{4,6},{6,8},{8,10},{10,12},{12,14},{14,16},{16,18},{18... | collective-permute-start | bytes 1769480 | tf_op jit(solution)/shard_map/ppermute | solution.py:234
  19.6 0.0 copy-done
  19.6 20.7 %collective-permute-done.1.high_ref = f32[9,128,128]{2,1,0:T(8,128)S(1)} collective-permute-done((f32[9,128,128]{2,1,0:T(8,128)S(1)}, f32[9,128,128]{2,1,0:T(8,128)S(1)}, u32[]{:S(2)}, u32[]{:S(2)}) %collective-permute-start.1) | collective-permute-done | bytes 589856 | tf_op jit(solution)/shard_map/ppermute | solution.py:235
  40.4 13.6 %collective-permute-done.low_ref = f32[9,128,128]{2,1,0:T(8,128)S(1)} collective-permute-done((f32[9,128,128]{2,1,0:T(8,128)S(1)}, f32[9,128,128]{2,1,0:T(8,128)S(1)}, u32[]{:S(2)}, u32[]{:S(2)}) %collective-permute-start) | collective-permute-done | bytes 589856 | tf_op jit(solution)/shard_map/ppermute | solution.py:234
  54.0 1.0 collective-permute-start.2
  55.0 0.1 add_convert_fusion.edge_ref
  55.1 1.1 %collective-permute-done.2.ylow_ref.yhigh_ref = f32[34,16,128]{2,1,0:T(8,128)S(1)} collective-permute-done((f32[34,16,128]{2,1,0:T(8,128)S(1)}, f32[34,16,128]{2,1,0:T(8,128)S(1)}, u32[]{:S(2)}, u32[]{:S(2)}) %collective-permute-start.2) | collective-permute-done | bytes 278560 | tf_op jit(solution)/shard_map/ppermute | solution.py:241
  56.2 0.0 copy-start.1
  56.2 0.7 copy-done.1
  56.9 41.2 %shard_map.56 = f32[2048,128]{1,0:T(8,128)S(1)} custom-call(s32[4]{0:T(128)S(1)} %add_convert_fusion.edge_ref, f32[3,16,128]{2,1,0:T(8,128)S(1)} %copy-done.1, f32[16,128,128]{2,1,0:T(8,128)S(1)} %copy-done, f32[9,128,128]{2,1,0:T(8,128)S(1)} %collective-permute-done.low_ref, f32[9,128,128]{2,1,0:T(8,128)S(1)} %collective-permute-done.1.high_ref, ...), custom_call_target="tpu_custom_call" | custom-call | tf_op jit(solution)/shard_map/pallas_call | solution.py:254
  98.1 0.0 all-to-all-done
  98.2 0.0 copy-start.2
  98.2 0.0 copy-start.3
  98.2 1.4 %copy.8 = f32[16,8,16,128]{3,2,1,0:T(8,128)S(1)} copy(f32[16,8,16,128]{3,1,2,0:T(8,128)} %bitcast.1) | data formatting | bytes 2097152 | tf_op jit(solution)/shard_map/all_to_all | solution.py:221
  99.6 0.0 copy-done.2
  99.6 0.0 copy-done.3
  99.6 1.1 %bitcast_minimum_fusion = f32[128,16,128]{2,1,0:T(8,128)} fusion(f32[16,8,16,128]{3,2,1,0:T(8,128)S(1)} %copy.8, f32[128,16,128]{2,1,0:T(8,128)S(1)} %bitcast.11, f32[16,128]{1,0:T(8,128)S(1)} %copy-done.2, f32[16,128]{1,0:T(8,128)S(1)} %copy-done.3), kind=kLoop, calls=%fused_computation | loop fusion | flops 786432 | bytes 3162112 | tf_op jit(solution)/shard_map/min | solution.py:267
  (4 shorter events, 0.1 us)
Async XLA Ops:
  2.8 95.3 %all-to-all-start = ((f32[8,256,128]{2,0,1:T(8,128)}), f32[8,256,128]{2,0,1:T(8,128)}, u32[]{:S(2)}, u32[]{:S(2)}) async-start(f32[8,256,128]{2,0,1:T(8,128)} %copy.7), calls=%async_computation | async-start | bytes 2097152 | tf_op jit(solution)/shard_map/all_to_all | solution.py:221
  12.0 7.6 %copy-start = (f32[16,128,128]{2,1,0:T(8,128)S(1)}, f32[16,128,128]{2,1,0:T(8,128)}, u32[]{:S(2)}) copy-start(f32[16,128,128]{2,1,0:T(8,128)} %shard_map.55.mid_ref) | copy-start | bytes 3145732
  13.4 27.0 %collective-permute-start.1 = (f32[9,128,128]{2,1,0:T(8,128)S(1)}, f32[9,128,128]{2,1,0:T(8,128)S(1)}, u32[]{:S(2)}, u32[]{:S(2)}) collective-permute-start(f32[9,128,128]{2,1,0:T(8,128)S(1)} %get-tuple-element.5), channel_id=1, source_target_pairs={{2,0},{4,2},{6,4},{8,6},{10,8},{12,10},{14,12},{16,14},{18,16},{20... | collective-permute-start | bytes 1769480 | tf_op jit(solution)/shard_map/ppermute | solution.py:235
  15.6 38.4 %collective-permute-start = (f32[9,128,128]{2,1,0:T(8,128)S(1)}, f32[9,128,128]{2,1,0:T(8,128)S(1)}, u32[]{:S(2)}, u32[]{:S(2)}) collective-permute-start(f32[9,128,128]{2,1,0:T(8,128)S(1)} %get-tuple-element.6), channel_id=1, source_target_pairs={{0,2},{2,4},{4,6},{6,8},{8,10},{10,12},{12,14},{14,16},{16,18},{18... | collective-permute-start | bytes 1769480 | tf_op jit(solution)/shard_map/ppermute | solution.py:234
  54.0 2.2 %collective-permute-start.2 = (f32[34,16,128]{2,1,0:T(8,128)S(1)}, f32[34,16,128]{2,1,0:T(8,128)S(1)}, u32[]{:S(2)}, u32[]{:S(2)}) collective-permute-start(f32[34,16,128]{2,1,0:T(8,128)S(1)} %pad_maximum_fusion), channel_id=1, source_target_pairs={{0,1},{1,0},{2,3},{3,2},{4,5},{5,4},{6,7},{7,6},{8,9},{9,8},{10,11... | collective-permute-start | bytes 835592 | tf_op jit(solution)/shard_map/ppermute | solution.py:241
  56.2 0.7 copy-start.1
  98.2 1.4 %copy-start.2 = (f32[16,128]{1,0:T(8,128)S(1)}, f32[16,128]{1,0:T(8,128)}, u32[]{:S(2)}) copy-start(f32[16,128]{1,0:T(8,128)} %param.7) | copy-start | bytes 24580
  98.2 1.4 %copy-start.3 = (f32[16,128]{1,0:T(8,128)S(1)}, f32[16,128]{1,0:T(8,128)}, u32[]{:S(2)}) copy-start(f32[16,128]{1,0:T(8,128)} %param.8) | copy-start | bytes 24580

commit v2 on v1

v2 whole, which is shorter than its diff:
```python
import functools
import math

import jax
import jax.numpy as jnp
import numpy as np
from jax import lax
from jax.experimental import pallas as pl
from jax.experimental.pallas import tpu as pltpu
from jax.sharding import PartitionSpec as P

EPS = 1e-06
SPACING = 1.0 / 64.0
SPEED = 1.0
TURN = 2.0
COURANT = 0.5
LANES = 128
SUB = 8
DEPTH = 9
OFF = 16


def ceil_div(a, b):
    return -(-a // b)


def stage_constants(headings, share):
    gap = 2.0 * math.pi / headings
    dt = COURANT / (2.0 * SPEED / SPACING + TURN / gap)
    angles = (np.float32(gap) * np.arange(headings, dtype=np.float32)).astype(np.float64)
    rows = []
    for wave in (np.cos(angles), np.sin(angles)):
        g = share * dt * SPEED * wave / SPACING
        ahead = wave >= 0
        rows += [
            g,
            np.where(ahead, -g / 3, g / 6),
            np.where(ahead, -g / 6, g / 3),
            np.where(ahead, 0.5, 1.0 / 6.0),
            np.where(ahead, 1.0 / 6.0, 0.5),
            np.where(ahead, g / 6, -g / 3),
            np.where(ahead, g / 3, -g / 6),
            np.where(ahead, 1.0, 0.0),
        ]
    turn = share * dt * TURN / (6.0 * gap)
    return np.stack(rows).astype(np.float32), float(turn)


def weights_of(a, b, d, eps, want):
    bd = b * d
    ad = a * d
    ab = a * b
    mid = (bd - ad) * (2.0 / 3.0) + (ab * 0.5 + eps)
    out = []
    for name in want:
        x = {"L": mid + bd if "L" in want else None, "C": mid, "R": mid - ad if "R" in want else None}[name]
        r = inverse(x)
        out.append(r * r)
    return out


def inverse(x):
    return 1.0 / x


def sided(vals, coef, eps):
    n = len(vals)
    g, r2, r3, n1c, n3c, k1, k3 = coef
    u = [vals[i + 1] - vals[i] for i in range(n - 1)]
    w = [None] + [u[i] - u[i - 1] for i in range(1, n - 1)]
    d = [None] + [w[i + 1] - w[i] for i in range(1, n - 2)]
    tri = [None] + [weights_of(w[i], w[i + 1], d[i], eps, "LCR") for i in range(1, n - 2)]
    third = [None, None] + [d[i] - d[i - 1] for i in range(2, n - 2)]
    faces = {}
    for k in range(2, n - 3):
        m1 = tri[k - 1][0] * n1c
        m2 = tri[k][1]
        m3 = tri[k + 1][2] * n3c
        den = (m1 + m3) + m2
        num = m1 * (k1 * third[k]) + m3 * (k3 * third[k + 1])
        smooth = g * u[k] + r2 * w[k] + r3 * w[k + 1]
        faces[k] = smooth + num * inverse(den)
    return faces


def turning(v, eps):
    ahead = lambda x: pltpu.roll(x, LANES - 1, x.ndim - 1)
    behind = lambda x: pltpu.roll(x, 1, x.ndim - 1)
    u = ahead(v) - v
    w = u - behind(u)
    wn = ahead(w)
    d = wn - w
    low, mid, high = weights_of(w, wn, d, eps, "LCR")
    m1 = behind(low)
    m3 = ahead(high)
    g1 = d - behind(d)
    g2 = ahead(g1)
    v0 = (m1 + m3) * 0.5 + mid * 3.0
    a1 = m1 * g1
    a3 = m3 * g2
    s = w + wn
    top = u * 6.0 + wn + s
    back = (a1 + 1.5 * a3) * inverse(v0 + m3) - top
    fore = (top - 3.0 * s) + (a3 + 1.5 * a1) * inverse(v0 + m1)
    return jnp.minimum(behind(back), fore)


def lanes_of(shape):
    return lax.broadcasted_iota(jnp.int32, shape, len(shape) - 1)


def fold(rows, shift):
    half = rows.shape[0] // 2
    low = pltpu.roll(rows[:half], (-shift) % LANES, 1)
    high = pltpu.roll(rows[half:], shift % LANES, 1)
    return jnp.where(lanes_of(low.shape) < LANES // 2, low, high)


def unfold(packed, shift):
    return pltpu.roll(packed, shift % LANES, 1), pltpu.roll(packed, (-shift) % LANES, 1)


QUARTER = LANES // 4
FULL = 6


def prep_kernel(x_ref, mid_ref, one_ref, two_ref):
    rows, cols = mid_ref.shape[:2]
    half = cols // 2
    for r in range(rows):
        mid_ref[r] = x_ref[pl.ds(r, LANES, stride=rows), :].T

    def upper(ref):
        for i in range(FULL):
            ref[pl.ds(i * cols, cols), :] = mid_ref[rows - FULL + i]
        for i in range(3):
            ref[pl.ds(FULL * cols + i * half, half), :] = fold(mid_ref[rows - FULL - 3 + i], QUARTER)

    def lower(ref):
        for i in range(FULL):
            ref[pl.ds(i * cols, cols), :] = mid_ref[i]
        for i in range(3):
            ref[pl.ds(FULL * cols + i * half, half), :] = fold(mid_ref[FULL + i], -QUARTER)

    even = lax.rem(lax.axis_index("px"), 2) == 0

    @pl.when(even)
    def _():
        upper(one_ref)
        lower(two_ref)

    @pl.when(jnp.logical_not(even))
    def _():
        lower(one_ref)
        upper(two_ref)


def halo_parts(low, one_ref, two_ref, rows, cols, write):
    half = cols // 2

    def emit(ref):
        for i in range(FULL):
            write(3 + i if low else DEPTH + rows + i, 0, ref[pl.ds(i * cols, cols), :])
        for i in range(3):
            packed = ref[pl.ds(FULL * cols + i * half, half), :]
            row = i if low else DEPTH + rows + FULL + i
            a, b = unfold(packed, QUARTER if low else -QUARTER)
            write(row, 0, a)
            write(row, half, b)

    even = lax.rem(lax.axis_index("px"), 2) == 0
    first, second = (two_ref, one_ref) if low else (one_ref, two_ref)

    @pl.when(even)
    def _():
        emit(first)

    @pl.when(jnp.logical_not(even))
    def _():
        emit(second)


def edge_kernel(mid_ref, one_ref, two_ref, *slabs, sides):
    rows, cols = mid_ref.shape[:2]

    def fill(ref, right):
        begin = cols - OFF if right else 0
        ref[pl.ds(DEPTH, rows)] = mid_ref[:, pl.ds(begin, OFF), :]

        def write(row, col, values):
            count = values.shape[0]
            if col <= begin and begin + OFF <= col + count:
                ref[row] = values[begin - col : begin - col + OFF]

        halo_parts(True, one_ref, two_ref, rows, cols, write)
        halo_parts(False, one_ref, two_ref, rows, cols, write)

    if sides == 1:
        at_left = lax.axis_index("py") == 0

        @pl.when(at_left)
        def _():
            fill(slabs[0], True)

        @pl.when(jnp.logical_not(at_left))
        def _():
            fill(slabs[0], False)
    else:
        fill(slabs[0], True)
        fill(slabs[1], False)


def zpack_kernel(p_ref, *outs, inner):
    z = lax.axis_index("px") // inner
    rows = outs[0].shape[2]
    for k, out in enumerate(outs):
        for q in range(inner):
            start = ((z ^ k) * inner + q) * rows
            out[q] = p_ref[:, pl.ds(pl.multiple_of(start, rows), rows), :]


def qpack_kernel(*refs, inner, outer):
    ins, outs = refs[:outer], refs[outer:]
    q = lax.rem(lax.axis_index("px"), inner)
    for m, out in enumerate(outs):
        for k in range(outer):
            out[k] = ins[k][q ^ m]


def final_kernel(third_ref, reach_ref, avoid_ref, *refs, inner, outer):
    ins, o_ref = refs[:inner], refs[inner]
    px = lax.axis_index("px")
    z, q = px // inner, lax.rem(px, inner)
    count = ins[0].shape[1]
    reach, avoid = reach_ref[...], avoid_ref[...]
    for m in range(inner):
        for k in range(outer):
            block = pl.ds(((z ^ k) * inner + (q ^ m)) * count, count)
            kept = jnp.maximum(avoid[None], jnp.minimum(reach[None], third_ref[block]))
            o_ref[block] = jnp.minimum(ins[m][k], kept)


def stage(src, dst, part, base, const_ref, lo, hi, seg, start, turn, eps_xy, eps_t, weights, depth):
    def column(ref, row, j):
        return ref[row, pl.ds(OFF + start + j, SUB, stride=seg), :]

    def const(i):
        return const_ref[pl.ds(i, SUB, stride=0), :]

    xcoef = [const(i) for i in range(7)]
    ycoef = [const(i) for i in range(8, 15)]
    xmask = const(7) > 0.5
    ymask = const(15) > 0.5

    @pl.loop(0, seg)
    def _(j):
        vals = [column(src, r + depth, j) for r in range(lo - 3, hi + 3)]
        faces = sided(vals, xcoef, eps_xy)
        for r in range(lo, hi):
            i = r - lo + 3
            move = jnp.where(xmask, faces[i], faces[i - 1])
            here = vals[i]
            if weights is not None:
                here = here * weights[0] + column(base, r + DEPTH, j) * weights[1]
            part[r - lo, j] = here + move

    @pl.loop(0, hi - lo)
    def _(r):
        vals = [column(src, lo + depth + r, j) for j in range(-3, seg + 3)]
        faces = sided(vals, ycoef, eps_xy)
        for j in range(seg):
            i = j + 3
            move = jnp.where(ymask, faces[i], faces[i - 1])
            out = part[r, j] + move + turn * turning(vals[i], eps_t)
            dst[r, pl.ds(OFF + start + j, SUB, stride=seg), :] = out


def main_kernel(const_ref, mid_ref, recv1_ref, recv2_ref, ylow_ref, yhigh_ref, o_ref, field, one, two, part, *, consts, sizes):
    rows, cols, headings = sizes
    gap = 2.0 * math.pi / headings
    eps_xy = 0.5 * EPS * SPACING**2
    eps_t = 0.5 * EPS * gap**2
    px, py = lax.axis_index("px"), lax.axis_index("py")
    first_row = px == 0
    last_row = px == lax.axis_size("px") - 1
    first_col = py == 0
    last_col = py == lax.axis_size("py") - 1
    tall = rows + 2 * DEPTH

    def write(row, col, values):
        field[row, pl.ds(OFF + col, values.shape[0]), :] = values

    field[pl.ds(DEPTH, rows), pl.ds(OFF, cols), :] = mid_ref[...]
    halo_parts(True, recv1_ref, recv2_ref, rows, cols, write)
    halo_parts(False, recv1_ref, recv2_ref, rows, cols, write)
    for at_edge, begin, slab in ((first_col, 0, ylow_ref), (last_col, OFF + cols, yhigh_ref)):

        @pl.when(at_edge)
        def _():
            field[:, pl.ds(begin, OFF), :] = jnp.zeros((tall, OFF, LANES), jnp.float32)

        @pl.when(jnp.logical_not(at_edge))
        def _():
            field[:, pl.ds(begin, OFF), :] = slab[...]

    def clear(ref, margin):
        count = rows + 2 * margin

        @pl.when(first_row)
        def _():
            ref[pl.ds(0, margin)] = jnp.zeros((margin,) + ref.shape[1:], jnp.float32)

        @pl.when(last_row)
        def _():
            ref[pl.ds(margin + rows, margin)] = jnp.zeros((margin,) + ref.shape[1:], jnp.float32)

        @pl.when(first_col)
        def _():
            ref[pl.ds(0, count), pl.ds(0, OFF), :] = jnp.zeros((count, OFF, LANES), jnp.float32)

        @pl.when(last_col)
        def _():
            ref[pl.ds(0, count), pl.ds(OFF + cols, OFF), :] = jnp.zeros((count, OFF, LANES), jnp.float32)

    def run(index, src, src_depth, dst, margin):
        seg = ceil_div(cols + 2 * margin, SUB)
        start = -((seg * SUB - cols) // 2)
        weights = (None, (0.25, 0.75), (2.0 / 3.0, 1.0 / 3.0))[index]
        stage(src, dst, part, field, const_ref.at[index], -margin, rows + margin, seg, start, consts[index],
              eps_xy, eps_t, weights, src_depth)

    run(0, field, DEPTH, one, 6)
    clear(one, 6)
    run(1, one, 6, two, 3)
    clear(two, 3)
    run(2, two, 3, one, 0)
    for r in range(rows):
        o_ref[pl.ds(r, LANES, stride=rows), :] = one[r, pl.ds(OFF, cols), :].T


def on_device(start_value, prior, reach, avoid):
    headings, rows, cols = start_value.shape
    nx, ny = lax.axis_size("px"), lax.axis_size("py")
    inner = 4 if nx % 4 == 0 else 1
    outer = nx // inner
    assert headings == LANES and cols == LANES and rows >= DEPTH
    assert nx % 2 == 0 and outer & (outer - 1) == 0
    f32 = jnp.float32
    vmem = pl.BlockSpec(memory_space=pltpu.VMEM)

    def call(kernel, outs, *args, **kw):
        return pl.pallas_call(
            kernel,
            out_shape=[jax.ShapeDtypeStruct(o, f32) for o in outs],
            in_specs=[vmem] * len(args),
            out_specs=[vmem] * len(outs),
            **kw,
        )(*args)

    message = (FULL * cols + 3 * cols // 2, headings)
    mid, send1, send2 = call(
        prep_kernel, [(rows, cols, headings), message, message], start_value.reshape(headings * rows, cols)
    )
    pairs1 = [(i, i ^ 1) for i in range(nx)]
    pairs2 = [(i, j) for i in range(nx) for j in [((i + 1) ^ 1) - 1] if 0 <= j < nx]
    recv1 = lax.ppermute(send1, "px", pairs1)
    recv2 = lax.ppermute(send2, "px", pairs2)

    share = (inner, headings // nx, rows, cols)
    zsend = call(functools.partial(zpack_kernel, inner=inner), [share] * outer, prior)
    zrecv = [zsend[0]] + [
        lax.ppermute(zsend[k], "px", [(i, ((i // inner) ^ k) * inner + i % inner) for i in range(nx)])
        for k in range(1, outer)
    ]

    sides = 1 if ny == 2 else 2
    slabs = call(
        functools.partial(edge_kernel, sides=sides), [(rows + 2 * DEPTH, OFF, headings)] * sides, mid, recv1, recv2
    )
    if sides == 1:
        ylow = yhigh = lax.ppermute(slabs[0], "py", [(0, 1), (1, 0)])
    else:
        ylow = lax.ppermute(slabs[0], "py", [(i, i + 1) for i in range(ny - 1)])
        yhigh = lax.ppermute(slabs[1], "py", [(i + 1, i) for i in range(ny - 1)])

    share = (outer, headings // nx, rows, cols)
    qsend = call(functools.partial(qpack_kernel, inner=inner, outer=outer), [share] * inner, *zrecv)
    qrecv = [qsend[0]] + [
        lax.ppermute(qsend[m], "px", [(i, (i // inner) * inner + ((i % inner) ^ m)) for i in range(nx)])
        for m in range(1, inner)
    ]

    tables = [stage_constants(headings, part) for part in (1.0, 0.25, 2.0 / 3.0)]
    table = jnp.asarray(np.stack([t[0] for t in tables]))
    seg = ceil_div(cols + 12, SUB)
    wide = cols + 2 * OFF
    (third,) = call(
        functools.partial(main_kernel, consts=[t[1] for t in tables], sizes=(rows, cols, headings)),
        [(headings * rows, cols)],
        table, mid, recv1, recv2, ylow, yhigh,
        scratch_shapes=[
            pltpu.VMEM((rows + 2 * DEPTH, wide, LANES), f32),
            pltpu.VMEM((rows + 12, wide, LANES), f32),
            pltpu.VMEM((rows + 6, wide, LANES), f32),
            pltpu.VMEM((rows + 12, seg, SUB, LANES), f32),
        ],
        compiler_params=pltpu.CompilerParams(vmem_limit_bytes=40 * 2**20),
    )
    (out,) = call(
        functools.partial(final_kernel, inner=inner, outer=outer),
        [(headings, rows, cols)],
        third.reshape(headings, rows, cols), reach, avoid, *qrecv,
    )
    return out


def solution(mesh):
    return jax.shard_map(
        on_device,
        mesh=mesh,
        in_specs=(P(None, "px", "py"), P("px", None, "py"), P("px", "py"), P("px", "py")),
        out_specs=P(None, "px", "py"),
        check_vma=False,
    )
```

time: 101 us -> 96.1 us (0.951)
  the two profiles are of different devices: /device:TPU:19 before, /device:TPU:10 now
where the time goes in v2:
time: 96.1 us; the launch traced here: 94.2 us
  Pallas kernels  52.5 us (55%)
  waiting for transfers between devices  19.1 us (20%)
  starting transfers between devices  17.1 us (18%)
  local copies, waits for them, and re-layouts  5.38 us (6%)
    pallas_call x6, Pallas kernels, call(): pl.pallas_call(kernel, out_shape=[jax.ShapeDtypeStruct(o, f32) for o in o...  52.5 us
    ppermute x1, waiting for transfers between devices, on_device(): recv1 = lax.ppermute(send1, 'px', pairs1)  13.1 us
    ppermute x3, starting transfers between devices, on_device(): lax.ppermute(qsend[m], 'px', [(i, i // inner * inner + (i % inner ^ m)) f...  8.78 us
    unnamed x26, local copies, waits for them, and re-layouts  5.38 us
    ppermute x3, waiting for transfers between devices, on_device(): lax.ppermute(zsend[k], 'px', [(i, (i // inner ^ k) * inner + i % inner) f...  5.08 us
    ppermute x1, starting transfers between devices, on_device(): recv2 = lax.ppermute(send2, 'px', pairs2)  4.39 us
    ppermute x3, starting transfers between devices, on_device(): lax.ppermute(zsend[k], 'px', [(i, (i // inner ^ k) * inner + i % inner) f...  3.49 us
  transfers between devices with their start and end apart: 9, of which 4 were waited for; matrix products, arithmetic and copies ran while one was open for 0% of the time, Pallas kernels for 50%

profile of v2, /device:TPU:10, one launch (start us, length us, event | category | flops | bytes accessed | tf_op | source)
XLA Modules:
  0.0 94.2 jit_solution(955679732155167659)
XLA Ops:
  0.0 3.0 %shard_map.55 = (f32[16,128,128]{2,1,0:T(8,128)}, f32[960,128]{1,0:T(8,128)}, f32[960,128]{1,0:T(8,128)}) custom-call(f32[2048,128]{1,0:T(8,128)} %bitcast.3), custom_call_target="tpu_custom_call" | custom-call | tf_op jit(solution)/shard_map/pallas_call | solution.py:352
  3.0 0.5 collective-permute-start
  3.5 4.4 %collective-permute-start.1 = (f32[960,128]{1,0:T(8,128)}, f32[960,128]{1,0:T(8,128)S(1)}, u32[]{:S(2)}, u32[]{:S(2)}) collective-permute-start(f32[960,128]{1,0:T(8,128)} %get-tuple-element.18), channel_id=1, source_target_pairs={{2,4},{4,2},{6,8},{8,6},{10,12},{12,10},{14,16},{16,14},{18,20},{2... | collective-permute-start | bytes 1474568 | tf_op jit(solution)/shard_map/ppermute | solution.py:367
  7.9 2.3 %shard_map.58 = (f32[4,8,16,128]{3,2,1,0:T(8,128)}, f32[4,8,16,128]{3,2,1,0:T(8,128)}, f32[4,8,16,128]{3,2,1,0:T(8,128)}, f32[4,8,16,128]{3,2,1,0:T(8,128)}) custom-call(f32[8,256,128]{2,1,0:T(8,128)} %p_ref.1), custom_call_target="tpu_custom_call" | custom-call | tf_op jit(solution)/shard_map/pallas_call | solution.py:352
  10.2 0.4 collective-permute-start.3
  10.7 2.6 %collective-permute-start.4 = (f32[4,8,16,128]{3,2,1,0:T(8,128)}, f32[4,8,16,128]{3,2,1,0:T(8,128)S(1)}, u32[]{:S(2)}, u32[]{:S(2)}) collective-permute-start(f32[4,8,16,128]{3,2,1,0:T(8,128)} %get-tuple-element.21), channel_id=1, source_target_pairs={{0,16},{2,18},{4,20},{6,22},{8,24},{10,26},{12,28},{14,30},{16,0},... | collective-permute-start | bytes 786440 | tf_op jit(solution)/shard_map/ppermute | solution.py:372
  13.2 0.5 collective-permute-start.5
  13.7 13.1 %collective-permute-done.one_ref.recv1_ref = f32[960,128]{1,0:T(8,128)S(1)} collective-permute-done((f32[960,128]{1,0:T(8,128)}, f32[960,128]{1,0:T(8,128)S(1)}, u32[]{:S(2)}, u32[]{:S(2)}) %collective-permute-start) | collective-permute-done | bytes 491552 | tf_op jit(solution)/shard_map/ppermute | solution.py:366
  26.8 1.0 %collective-permute-done.1.two_ref.recv2_ref = f32[960,128]{1,0:T(8,128)S(1)} collective-permute-done((f32[960,128]{1,0:T(8,128)}, f32[960,128]{1,0:T(8,128)S(1)}, u32[]{:S(2)}, u32[]{:S(2)}) %collective-permute-start.1) | collective-permute-done | bytes 491552 | tf_op jit(solution)/shard_map/ppermute | solution.py:367
  27.7 0.8 copy-done.4
  28.5 2.4 %shard_map.56 = f32[34,16,128]{2,1,0:T(8,128)} custom-call(f32[16,128,128]{2,1,0:T(8,128)} %get-tuple-element.16.mid_ref, f32[960,128]{1,0:T(8,128)} %copy-done.2, f32[960,128]{1,0:T(8,128)} %copy-done.4), custom_call_target="tpu_custom_call" | custom-call | tf_op jit(solution)/shard_map/pallas_call | solution.py:352
  30.9 0.6 collective-permute-done.4.refs_2_
  31.5 4.5 %collective-permute-done.5.refs_3_ = f32[4,8,16,128]{3,2,1,0:T(8,128)S(1)} collective-permute-done((f32[4,8,16,128]{3,2,1,0:T(8,128)}, f32[4,8,16,128]{3,2,1,0:T(8,128)S(1)}, u32[]{:S(2)}, u32[]{:S(2)}) %collective-permute-start.5) | collective-permute-done | bytes 262176 | tf_op jit(solution)/shard_map/ppermute | solution.py:372
  36.0 0.7 copy-done.12
  36.7 2.2 %shard_map.59 = (f32[4,8,16,128]{3,2,1,0:T(8,128)}, f32[4,8,16,128]{3,2,1,0:T(8,128)}, f32[4,8,16,128]{3,2,1,0:T(8,128)}, f32[4,8,16,128]{3,2,1,0:T(8,128)}) custom-call(f32[4,8,16,128]{3,2,1,0:T(8,128)} %get-tuple-element.19.refs_0_, f32[4,8,16,128]{3,2,1,0:T(8,128)} %copy-done.10, f32[4,8,16,128]{3,2,1,0:T(8,128)} %copy-done.11, f32[4,8,16,128]{3,2,1,0:T(8,128)} %copy-done.12), custom_call_target="tpu_custom_call" | custom-call | tf_op jit(solution)/shard_map/pallas_call | solution.py:352
  38.9 7.3 %collective-permute-start.6 = (f32[4,8,16,128]{3,2,1,0:T(8,128)}, f32[4,8,16,128]{3,2,1,0:T(8,128)S(1)}, u32[]{:S(2)}, u32[]{:S(2)}) collective-permute-start(f32[4,8,16,128]{3,2,1,0:T(8,128)} %get-tuple-element.24), channel_id=1, source_target_pairs={{0,2},{2,0},{4,6},{6,4},{8,10},{10,8},{12,14},{14,12},{16,18},{18,... | collective-permute-start | bytes 786440 | tf_op jit(solution)/shard_map/ppermute | solution.py:389
  46.2 1.5 %collective-permute-start.8 = (f32[4,8,16,128]{3,2,1,0:T(8,128)}, f32[4,8,16,128]{3,2,1,0:T(8,128)S(1)}, u32[]{:S(2)}, u32[]{:S(2)}) collective-permute-start(f32[4,8,16,128]{3,2,1,0:T(8,128)} %get-tuple-element.26), channel_id=1, source_target_pairs={{0,6},{2,4},{4,2},{6,0},{8,14},{10,12},{12,10},{14,8},{16,22},{18,... | collective-permute-start | bytes 786440 | tf_op jit(solution)/shard_map/ppermute | solution.py:389
  47.7 1.0 %copy-done.3 = f32[960,128]{1,0:T(8,128)S(1)} copy-done((f32[960,128]{1,0:T(8,128)S(1)}, f32[960,128]{1,0:T(8,128)}, u32[]{:S(2)}) %copy-start.3) | copy-done | bytes 491544
  48.7 1.0 %copy-done.5 = f32[960,128]{1,0:T(8,128)S(1)} copy-done((f32[960,128]{1,0:T(8,128)S(1)}, f32[960,128]{1,0:T(8,128)}, u32[]{:S(2)}) %copy-start.5) | copy-done | bytes 491544
  49.7 39.8 %shard_map.57 = f32[2048,128]{1,0:T(8,128)S(1)} custom-call(f32[3,16,128]{2,1,0:T(8,128)S(1)} %copy-done.6, f32[16,128,128]{2,1,0:T(8,128)S(1)} %copy-done.1, f32[960,128]{1,0:T(8,128)S(1)} %copy-done.3, f32[960,128]{1,0:T(8,128)S(1)} %copy-done.5, f32[34,16,128]{2,1,0:T(8,128)S(1)} %collective-permute-done.2.ylow_ref.yhigh_ref, ...), custom_call_target="tpu_custom_call" | custom-call | tf_op jit(solution)/shard_map/pallas_call | solution.py:352
  89.6 1.0 %copy-done = f32[2048,128]{1,0:T(8,128)} copy-done((f32[2048,128]{1,0:T(8,128)}, f32[2048,128]{1,0:T(8,128)S(1)}, u32[]{:S(2)}) %copy-start) | copy-done | bytes 1048600
  90.6 0.7 copy-done.7
  91.3 0.1 copy-done.8
  91.5 2.7 %shard_map.60 = f32[128,16,128]{2,1,0:T(8,128)} custom-call(f32[128,16,128]{2,1,0:T(8,128)} %bitcast.2, f32[16,128]{1,0:T(8,128)} %reach_ref.1, f32[16,128]{1,0:T(8,128)} %avoid_ref.1, f32[4,8,16,128]{3,2,1,0:T(8,128)} %get-tuple-element.23.refs_0_, f32[4,8,16,128]{3,2,1,0:T(8,128)} %copy-done.7, f32[4,8,16,128]{3,2,1,0:T(8,128)} %copy-done.8, ...), custom_call_target="tpu_custom_call" | custom-call | tf_op jit(solution)/shard_map/pallas_call | solution.py:352
  (26 shorter events, 0.1 us)
Async XLA Ops:
  3.0 23.7 %collective-permute-start = (f32[960,128]{1,0:T(8,128)}, f32[960,128]{1,0:T(8,128)S(1)}, u32[]{:S(2)}, u32[]{:S(2)}) collective-permute-start(f32[960,128]{1,0:T(8,128)} %get-tuple-element.17), channel_id=1, source_target_pairs={{0,2},{2,0},{4,6},{6,4},{8,10},{10,8},{12,14},{14,12},{16,18},{18,... | collective-permute-start | bytes 1474568 | tf_op jit(solution)/shard_map/ppermute | solution.py:366
  3.5 24.2 %collective-permute-start.1 = (f32[960,128]{1,0:T(8,128)}, f32[960,128]{1,0:T(8,128)S(1)}, u32[]{:S(2)}, u32[]{:S(2)}) collective-permute-start(f32[960,128]{1,0:T(8,128)} %get-tuple-element.18), channel_id=1, source_target_pairs={{2,4},{4,2},{6,8},{8,6},{10,12},{12,10},{14,16},{16,14},{18,20},{2... | collective-permute-start | bytes 1474568 | tf_op jit(solution)/shard_map/ppermute | solution.py:367
  10.2 20.7 %collective-permute-start.3 = (f32[4,8,16,128]{3,2,1,0:T(8,128)}, f32[4,8,16,128]{3,2,1,0:T(8,128)S(1)}, u32[]{:S(2)}, u32[]{:S(2)}) collective-permute-start(f32[4,8,16,128]{3,2,1,0:T(8,128)} %get-tuple-element.20), channel_id=1, source_target_pairs={{0,8},{2,10},{4,12},{6,14},{8,0},{10,2},{12,4},{14,6},{16,24},{18,... | collective-permute-start | bytes 786440 | tf_op jit(solution)/shard_map/ppermute | solution.py:372
  10.7 20.8 %collective-permute-start.4 = (f32[4,8,16,128]{3,2,1,0:T(8,128)}, f32[4,8,16,128]{3,2,1,0:T(8,128)S(1)}, u32[]{:S(2)}, u32[]{:S(2)}) collective-permute-start(f32[4,8,16,128]{3,2,1,0:T(8,128)} %get-tuple-element.21), channel_id=1, source_target_pairs={{0,16},{2,18},{4,20},{6,22},{8,24},{10,26},{12,28},{14,30},{16,0},... | collective-permute-start | bytes 786440 | tf_op jit(solution)/shard_map/ppermute | solution.py:372
  13.2 22.7 %collective-permute-start.5 = (f32[4,8,16,128]{3,2,1,0:T(8,128)}, f32[4,8,16,128]{3,2,1,0:T(8,128)S(1)}, u32[]{:S(2)}, u32[]{:S(2)}) collective-permute-start(f32[4,8,16,128]{3,2,1,0:T(8,128)} %get-tuple-element.22), channel_id=1, source_target_pairs={{0,24},{2,26},{4,28},{6,30},{8,16},{10,18},{12,20},{14,22},{16,8},... | collective-permute-start | bytes 786440 | tf_op jit(solution)/shard_map/ppermute | solution.py:372
  26.8 1.0 %copy-start.2 = (f32[960,128]{1,0:T(8,128)}, f32[960,128]{1,0:T(8,128)S(1)}, u32[]{:S(2)}) copy-start(f32[960,128]{1,0:T(8,128)S(1)} %collective-permute-done.one_ref.recv1_ref) | copy-start | bytes 1474564
  27.7 0.8 copy-start.4
  28.5 19.2 %copy-start.6 = (f32[3,16,128]{2,1,0:T(8,128)S(1)}, f32[3,16,128]{2,1,0:T(8,128)}, u32[]{:S(2)}) copy-start(f32[3,16,128]{2,1,0:T(8,128)} %constant.2.clone.const_ref) | copy-start | bytes 73732
  30.9 16.8 %copy-start.1 = (f32[16,128,128]{2,1,0:T(8,128)S(1)}, f32[16,128,128]{2,1,0:T(8,128)}, u32[]{:S(2)}) copy-start(f32[16,128,128]{2,1,0:T(8,128)} %get-tuple-element.16.mid_ref) | copy-start | bytes 3145732
  30.9 16.8 %collective-permute-start.2 = (f32[34,16,128]{2,1,0:T(8,128)}, f32[34,16,128]{2,1,0:T(8,128)S(1)}, u32[]{:S(2)}, u32[]{:S(2)}) collective-permute-start(f32[34,16,128]{2,1,0:T(8,128)} %shard_map.56), channel_id=1, source_target_pairs={{0,1},{1,0},{2,3},{3,2},{4,5},{5,4},{6,7},{7,6},{8,9},{9,8},{10,11... | collective-permute-start | bytes 835592 | tf_op jit(solution)/shard_map/ppermute | solution.py:381
  30.9 5.1 %copy-start.10 = (f32[4,8,16,128]{3,2,1,0:T(8,128)}, f32[4,8,16,128]{3,2,1,0:T(8,128)S(1)}, u32[]{:S(2)}) copy-start(f32[4,8,16,128]{3,2,1,0:T(8,128)S(1)} %collective-permute-done.3.refs_1_) | copy-start | bytes 786436
  31.5 4.5 %copy-start.11 = (f32[4,8,16,128]{3,2,1,0:T(8,128)}, f32[4,8,16,128]{3,2,1,0:T(8,128)S(1)}, u32[]{:S(2)}) copy-start(f32[4,8,16,128]{3,2,1,0:T(8,128)S(1)} %collective-permute-done.4.refs_2_) | copy-start | bytes 786436
  36.0 0.7 copy-start.12
  38.9 51.7 %collective-permute-start.6 = (f32[4,8,16,128]{3,2,1,0:T(8,128)}, f32[4,8,16,128]{3,2,1,0:T(8,128)S(1)}, u32[]{:S(2)}, u32[]{:S(2)}) collective-permute-start(f32[4,8,16,128]{3,2,1,0:T(8,128)} %get-tuple-element.24), channel_id=1, source_target_pairs={{0,2},{2,0},{4,6},{6,4},{8,10},{10,8},{12,14},{14,12},{16,18},{18,... | collective-permute-start | bytes 786440 | tf_op jit(solution)/shard_map/ppermute | solution.py:389
  46.2 44.4 %collective-permute-start.7 = (f32[4,8,16,128]{3,2,1,0:T(8,128)}, f32[4,8,16,128]{3,2,1,0:T(8,128)S(1)}, u32[]{:S(2)}, u32[]{:S(2)}) collective-permute-start(f32[4,8,16,128]{3,2,1,0:T(8,128)} %get-tuple-element.25), channel_id=1, source_target_pairs={{0,4},{2,6},{4,0},{6,2},{8,12},{10,14},{12,8},{14,10},{16,20},{18,... | collective-permute-start | bytes 786440 | tf_op jit(solution)/shard_map/ppermute | solution.py:389
  46.2 44.4 %collective-permute-start.8 = (f32[4,8,16,128]{3,2,1,0:T(8,128)}, f32[4,8,16,128]{3,2,1,0:T(8,128)S(1)}, u32[]{:S(2)}, u32[]{:S(2)}) collective-permute-start(f32[4,8,16,128]{3,2,1,0:T(8,128)} %get-tuple-element.26), channel_id=1, source_target_pairs={{0,6},{2,4},{4,2},{6,0},{8,14},{10,12},{12,10},{14,8},{16,22},{18,... | collective-permute-start | bytes 786440 | tf_op jit(solution)/shard_map/ppermute | solution.py:389
  47.7 1.0 %copy-start.3 = (f32[960,128]{1,0:T(8,128)S(1)}, f32[960,128]{1,0:T(8,128)}, u32[]{:S(2)}) copy-start(f32[960,128]{1,0:T(8,128)} %copy-done.2) | copy-start | bytes 1474564
  48.7 1.0 %copy-start.5 = (f32[960,128]{1,0:T(8,128)S(1)}, f32[960,128]{1,0:T(8,128)}, u32[]{:S(2)}) copy-start(f32[960,128]{1,0:T(8,128)} %copy-done.4) | copy-start | bytes 1474564
  89.6 1.0 %copy-start = (f32[2048,128]{1,0:T(8,128)}, f32[2048,128]{1,0:T(8,128)S(1)}, u32[]{:S(2)}) copy-start(f32[2048,128]{1,0:T(8,128)S(1)} %shard_map.57) | copy-start | bytes 3145732
  90.6 0.7 copy-start.7
  90.6 0.8 copy-start.8
  90.6 0.9 copy-start.9

commit v3 on v1

v3 whole, which is shorter than its diff:
```python
import functools
import math

import jax
import jax.numpy as jnp
import numpy as np
from jax import lax
from jax.experimental import pallas as pl
from jax.experimental.pallas import tpu as pltpu
from jax.sharding import PartitionSpec as P

EPS = 1e-06
SPACING = 1.0 / 64.0
SPEED = 1.0
TURN = 2.0
COURANT = 0.5
LANES = 128
SUB = 8
DEPTH = 6
OFF = 16


LIMIT = 12


def ceil_div(a, b):
    return -(-a // b)


def stage_constants(headings, share):
    gap = 2.0 * math.pi / headings
    dt = COURANT / (2.0 * SPEED / SPACING + TURN / gap)
    angles = (np.float32(gap) * np.arange(headings, dtype=np.float32)).astype(np.float64)
    rows = []
    for wave in (np.cos(angles), np.sin(angles)):
        g = share * dt * SPEED * wave / SPACING
        ahead = wave >= 0
        rows += [
            g,
            np.where(ahead, -g / 3, g / 6),
            np.where(ahead, -g / 6, g / 3),
            np.where(ahead, 0.5, 1.0 / 6.0),
            np.where(ahead, 1.0 / 6.0, 0.5),
            np.where(ahead, g / 6, -g / 3),
            np.where(ahead, g / 3, -g / 6),
            np.where(ahead, 1.0, 0.0),
        ]
    turn = share * dt * TURN / (6.0 * gap)
    return np.stack(rows).astype(np.float32), float(turn)


def weights_of(a, b, d, eps, want):
    bd = b * d
    ad = a * d
    ab = a * b
    mid = (bd - ad) * (2.0 / 3.0) + (ab * 0.5 + eps)
    out = []
    for name in want:
        x = {"L": mid + bd if "L" in want else None, "C": mid, "R": mid - ad if "R" in want else None}[name]
        r = inverse(x)
        out.append(r * r)
    return out


def inverse(x):
    return 1.0 / x


def sided(vals, coef, eps):
    n = len(vals)
    g, r2, r3, n1c, n3c, k1, k3 = coef
    u = [vals[i + 1] - vals[i] for i in range(n - 1)]
    w = [None] + [u[i] - u[i - 1] for i in range(1, n - 1)]
    d = [None] + [w[i + 1] - w[i] for i in range(1, n - 2)]
    tri = [None] + [weights_of(w[i], w[i + 1], d[i], eps, "LCR") for i in range(1, n - 2)]
    third = [None, None] + [d[i] - d[i - 1] for i in range(2, n - 2)]
    faces = {}
    for k in range(2, n - 3):
        m1 = tri[k - 1][0] * n1c
        m2 = tri[k][1]
        m3 = tri[k + 1][2] * n3c
        den = (m1 + m3) + m2
        num = m1 * (k1 * third[k]) + m3 * (k3 * third[k + 1])
        smooth = g * u[k] + r2 * w[k] + r3 * w[k + 1]
        faces[k] = smooth + num * inverse(den)
    return faces


def turning(v, eps):
    ahead = lambda x: pltpu.roll(x, LANES - 1, x.ndim - 1)
    behind = lambda x: pltpu.roll(x, 1, x.ndim - 1)
    u = ahead(v) - v
    w = u - behind(u)
    wn = ahead(w)
    d = wn - w
    low, mid, high = weights_of(w, wn, d, eps, "LCR")
    m1 = behind(low)
    m3 = ahead(high)
    g1 = d - behind(d)
    g2 = ahead(g1)
    v0 = (m1 + m3) * 0.5 + mid * 3.0
    a1 = m1 * g1
    a3 = m3 * g2
    s = w + wn
    top = u * 6.0 + wn + s
    back = (a1 + 1.5 * a3) * inverse(v0 + m3) - top
    fore = (top - 3.0 * s) + (a3 + 1.5 * a1) * inverse(v0 + m1)
    return jnp.minimum(behind(back), fore)


def lanes_of(shape):
    return lax.broadcasted_iota(jnp.int32, shape, len(shape) - 1)


def fold(rows, shift):
    half = rows.shape[0] // 2
    low = pltpu.roll(rows[:half], (-shift) % LANES, 1)
    high = pltpu.roll(rows[half:], shift % LANES, 1)
    return jnp.where(lanes_of(low.shape) < LANES // 2, low, high)


def unfold(packed, shift):
    return pltpu.roll(packed, shift % LANES, 1), pltpu.roll(packed, (-shift) % LANES, 1)


QUARTER = LANES // 4
FULL1, HALF1 = 4, 2
FULL2, HALF2 = 2, 1


def even_tile():
    return lax.rem(lax.axis_index("px"), 2) == 0


def pack(ref, read, count, full, half):
    for i in range(full):
        ref[pl.ds(i * count, count), :] = read(i)[0]
    for i in range(half):
        values, shift = read(full + i)
        ref[pl.ds(full * count + i * (count // 2), count // 2), :] = fold(values, shift)


def pack_pair(one_ref, two_ref, row, rows, count, full, half):
    upper = lambda i: (row(rows - 1 - i), QUARTER)
    lower = lambda i: (row(i), -QUARTER)

    @pl.when(even_tile())
    def _():
        pack(one_ref, upper, count, full, half)
        pack(two_ref, lower, count, full, half)

    @pl.when(jnp.logical_not(even_tile()))
    def _():
        pack(one_ref, lower, count, full, half)
        pack(two_ref, upper, count, full, half)


def unpack_pair(one_ref, two_ref, write, rows, count, full, half):
    def unpack(ref, low):
        at = lambda i: -1 - i if low else rows + i
        for i in range(full):
            write(at(i), 0, ref[pl.ds(i * count, count), :])
        for i in range(half):
            packed = ref[pl.ds(full * count + i * (count // 2), count // 2), :]
            first, second = unfold(packed, QUARTER if low else -QUARTER)
            write(at(full + i), 0, first)
            write(at(full + i), count // 2, second)

    @pl.when(even_tile())
    def _():
        unpack(one_ref, False)
        unpack(two_ref, True)

    @pl.when(jnp.logical_not(even_tile()))
    def _():
        unpack(one_ref, True)
        unpack(two_ref, False)


def prep_kernel(x_ref, mid_ref, one_ref, two_ref, *slabs):
    rows, cols = mid_ref.shape[:2]
    for r in range(rows):
        mid_ref[r] = x_ref[pl.ds(r, LANES, stride=rows), :].T
    pack_pair(one_ref, two_ref, lambda r: mid_ref[r], rows, cols, FULL1, HALF1)
    right = lambda ref: ref.__setitem__(Ellipsis, mid_ref[:, pl.ds(cols - OFF, OFF), :])
    left = lambda ref: ref.__setitem__(Ellipsis, mid_ref[:, pl.ds(0, OFF), :])
    if len(slabs) == 1:
        pl.when(lax.axis_index("py") == 0)(lambda: right(slabs[0]))
        pl.when(lax.axis_index("py") != 0)(lambda: left(slabs[0]))
    else:
        right(slabs[0])
        left(slabs[1])


def spread_kernel(p_ref, o_ref):
    rows = o_ref.shape[2]
    for i in range(o_ref.shape[0]):
        o_ref[i] = p_ref[:, pl.ds(i * rows, rows), :]


def columns_of(cols, margin):
    seg = ceil_div(cols + 2 * margin, SUB)
    return seg, -((seg * SUB - cols) // 2)


def stage(index, src, dst, base, part, const_ref, parts, sizes, turn):
    cols, margin, gap = sizes
    seg, start = columns_of(cols, margin)
    eps_xy = 0.5 * EPS * SPACING**2
    eps_t = 0.5 * EPS * gap**2
    weights = (None, (0.25, 0.75), (2.0 / 3.0, 1.0 / 3.0))[index]

    def column(array, row, j):
        return array[0][row + array[1], pl.ds(OFF + start + j, SUB, stride=seg), :]

    def const(i):
        return const_ref[index, pl.ds(i, SUB, stride=0), :]

    xcoef = [const(i) for i in range(7)]
    ycoef = [const(i) for i in range(8, 15)]
    xmask = const(7) > 0.5
    ymask = const(15) > 0.5

    @pl.loop(0, seg)
    def _(j):
        at = 0
        for lo, hi in parts:
            vals = [column(src, r, j) for r in range(lo - 3, hi + 3)]
            faces = sided(vals, xcoef, eps_xy)
            for r in range(lo, hi):
                i = r - lo + 3
                move = jnp.where(xmask, faces[i], faces[i - 1])
                here = vals[i]
                if weights is not None:
                    here = here * weights[0] + column(base, r, j) * weights[1]
                part[at, j] = here + move
                at += 1

    counts = [hi - lo for lo, hi in parts]

    @pl.loop(0, sum(counts))
    def _(t):
        row = t + parts[0][0]
        if len(parts) == 2:
            row = jnp.where(t < counts[0], row, t - counts[0] + parts[1][0])
        vals = [column(src, row, j) for j in range(-3, seg + 3)]
        faces = sided(vals, ycoef, eps_xy)
        for j in range(seg):
            i = j + 3
            move = jnp.where(ymask, faces[i], faces[i - 1])
            out = part[t, j] + move + turn * turning(vals[i], eps_t)
            dst[0][row + dst[1], pl.ds(OFF + start + j, SUB, stride=seg), :] = out


def clear_columns(dst, parts, cols):
    py = lax.axis_index("py")
    for edge, begin in ((0, 0), (lax.axis_size("py") - 1, OFF + cols)):

        @pl.when(py == edge)
        def _():
            for lo, hi in parts:
                dst[0][pl.ds(lo + dst[1], hi - lo), pl.ds(begin, OFF), :] = jnp.zeros((hi - lo, OFF, LANES), jnp.float32)


def inner_kernel(const_ref, mid_ref, ylow_ref, yhigh_ref, field, one, part, *, turns, gap):
    rows, cols = mid_ref.shape[:2]
    own = pl.ds(DEPTH, rows)
    field[own, pl.ds(OFF, cols), :] = mid_ref[...]
    field[own, pl.ds(0, OFF), :] = ylow_ref[...]
    field[own, pl.ds(OFF + cols, OFF), :] = yhigh_ref[...]
    clear_columns((field, DEPTH), [(0, rows)], cols)
    parts = [(3, rows - 3)]
    stage(0, (field, DEPTH), (one, 3), None, part, const_ref, parts, (cols, 6, gap), turns[0])
    clear_columns((one, 3), parts, cols)


def outer_kernel(const_ref, recv1_ref, recv2_ref, side1_ref, side2_ref, field_in, one_in, field, one, two, send1, send2, part, *, turns, gap, rows, cols):
    del field_in, one_in

    def write(row, col, values):
        field[row + DEPTH, pl.ds(OFF + col, values.shape[0]), :] = values

    unpack_pair(recv1_ref, recv2_ref, write, rows, cols, FULL1, HALF1)
    low, high = pl.ds(0, DEPTH), pl.ds(DEPTH + rows, DEPTH)

    def sides(ref, where):
        field[where, pl.ds(0, OFF), :] = ref[0]
        field[where, pl.ds(OFF + cols, OFF), :] = ref[ref.shape[0] - 1]

    @pl.when(even_tile())
    def _():
        sides(side1_ref, high)
        sides(side2_ref, low)

    @pl.when(jnp.logical_not(even_tile()))
    def _():
        sides(side1_ref, low)
        sides(side2_ref, high)

    clear_columns((field, DEPTH), [(-DEPTH, 0), (rows, rows + DEPTH)], cols)
    parts = [(-3, 3), (rows - 3, rows + 3)]
    stage(0, (field, DEPTH), (one, 3), None, part, const_ref, parts, (cols, 6, gap), turns[0])
    clear_columns((one, 3), parts, cols)
    px = lax.axis_index("px")
    for edge, begin in ((0, 0), (lax.axis_size("px") - 1, 3 + rows)):

        @pl.when(px == edge)
        def _():
            one[pl.ds(begin, 3)] = jnp.zeros((3,) + one.shape[1:], jnp.float32)

    parts = [(0, 3), (rows - 3, rows)]
    stage(1, (one, 3), (two, 3), (field, DEPTH), part, const_ref, parts, (cols, 3, gap), turns[1])
    clear_columns((two, 3), parts, cols)
    seg, start = columns_of(cols, 3)
    count = seg * SUB
    pack_pair(send1, send2, lambda r: two[r + 3, pl.ds(OFF + start, count), :], rows, count, FULL2, HALF2)


def middle_kernel(const_ref, field, one, two_in, two, three, part, *, turns, gap, rows, cols):
    del two_in
    parts = [(3, rows - 3)]
    stage(1, (one, 3), (two, 3), (field, DEPTH), part, const_ref, parts, (cols, 3, gap), turns[1])
    clear_columns((two, 3), parts, cols)
    stage(2, (two, 3), (three, 0), (field, DEPTH), part, const_ref, parts, (cols, 0, gap), turns[2])


def last_kernel(const_ref, recv1_ref, recv2_ref, field, two_in, three_in, prior_ref, reach_ref, avoid_ref, o_ref, two, three, part, *, turns, gap, rows, cols):
    del two_in, three_in
    seg, start = columns_of(cols, 3)

    def write(row, col, values):
        two[row + 3, pl.ds(OFF + start + col, values.shape[0]), :] = values

    unpack_pair(recv1_ref, recv2_ref, write, rows, seg * SUB, FULL2, HALF2)
    parts = [(0, 3), (rows - 3, rows)]
    stage(2, (two, 3), (three, 0), (field, DEPTH), part, const_ref, parts, (cols, 0, gap), turns[2])
    for r in range(rows):
        lines = pl.ds(r, LANES, stride=rows)
        value = three[r, pl.ds(OFF, cols), :].T
        kept = jnp.maximum(avoid_ref[pl.ds(r, LANES, stride=0), :], jnp.minimum(reach_ref[pl.ds(r, LANES, stride=0), :], value))
        o_ref[lines, :] = jnp.minimum(prior_ref[lines, :], kept)


def on_device(start_value, prior, reach, avoid):
    headings, rows, cols = start_value.shape
    nx, ny = lax.axis_size("px"), lax.axis_size("py")
    assert headings == LANES and cols == LANES and rows >= 2 * DEPTH and nx % 2 == 0
    gap = 2.0 * math.pi / headings
    f32 = jnp.float32
    vmem = pl.BlockSpec(memory_space=pltpu.VMEM)

    def call(kernel, outs, *args, limit=LIMIT, aliases={}, scratch=(), **kw):
        return pl.pallas_call(
            functools.partial(kernel, **kw) if kw else kernel,
            out_shape=[jax.ShapeDtypeStruct(o, f32) for o in outs],
            in_specs=[vmem] * len(args),
            out_specs=[vmem] * len(outs),
            input_output_aliases=aliases,
            scratch_shapes=[pltpu.VMEM(shape, f32) for shape in scratch],
            compiler_params=pltpu.CompilerParams(vmem_limit_bytes=limit * 2**20),
        )(*args)

    sides = 1 if ny == 2 else 2
    message = (FULL1 * cols + HALF1 * cols // 2, headings)
    mid, send1, send2, *slabs = call(
        prep_kernel,
        [(rows, cols, headings), message, message] + [(rows, OFF, headings)] * sides,
        start_value.reshape(headings * rows, cols),
    )
    pairs1 = [(i, i ^ 1) for i in range(nx)]
    pairs2 = [(i, j) for i in range(nx) for j in [((i + 1) ^ 1) - 1] if 0 <= j < nx]
    if sides == 1:
        yslabs = [lax.ppermute(slabs[0], "py", [(0, 1), (1, 0)])]
    else:
        yslabs = [
            lax.ppermute(slabs[0], "py", [(i, i + 1) for i in range(ny - 1)]),
            lax.ppermute(slabs[1], "py", [(i + 1, i) for i in range(ny - 1)]),
        ]
    recv1 = lax.ppermute(send1, "px", pairs1)
    recv2 = lax.ppermute(send2, "px", pairs2)
    corners = jnp.stack(yslabs)
    even = lax.rem(lax.axis_index("px"), 2) == 0
    top = lax.slice_in_dim(corners, rows - DEPTH, rows, axis=1)
    bottom = lax.slice_in_dim(corners, 0, DEPTH, axis=1)
    side1 = lax.ppermute(jnp.where(even, top, bottom), "px", pairs1)
    side2 = lax.ppermute(jnp.where(even, bottom, top), "px", pairs2)

    tables = [stage_constants(headings, part) for part in (1.0, 0.25, 2.0 / 3.0)]
    table = jnp.asarray(np.stack([t[0] for t in tables]))
    common = dict(turns=[t[1] for t in tables], gap=gap)
    seg = columns_of(cols, 6)[0]
    wide = cols + 2 * OFF
    tall = (rows + 2 * DEPTH, wide, headings)
    short = (rows + 6, wide, headings)
    scratch = [(max(rows - 6, 12), seg, SUB, LANES)]
    field, one = call(inner_kernel, [tall, short], table, mid, yslabs[0], yslabs[-1], scratch=scratch, **common)

    blocks = call(spread_kernel, [(nx, headings // nx, rows, cols)], prior)[0]
    regrouped = lax.all_to_all(blocks, "px", split_axis=0, concat_axis=0, tiled=True)

    common = dict(common, rows=rows, cols=cols)
    count = columns_of(cols, 3)[0] * SUB
    message = (FULL2 * count + HALF2 * count // 2, headings)
    field, one, two, send1, send2 = call(
        outer_kernel, [tall, short, short, message, message],
        table, recv1, recv2, side1, side2, field, one, aliases={5: 0, 6: 1}, scratch=scratch, **common,
    )
    recv1 = lax.ppermute(send1, "px", pairs1)
    recv2 = lax.ppermute(send2, "px", pairs2)
    two, three = call(
        middle_kernel, [short, (rows, wide, headings)], table, field, one, two, aliases={3: 0}, scratch=scratch, **common
    )
    out = call(
        last_kernel, [(headings * rows, cols), short, (rows, wide, headings)],
        table, recv1, recv2, field, two, three, regrouped.reshape(headings * rows, cols), reach, avoid,
        aliases={4: 1, 5: 2}, scratch=scratch, **common,
    )[0]
    return out.reshape(headings, rows, cols)


def solution(mesh):
    return jax.shard_map(
        on_device,
        mesh=mesh,
        in_specs=(P(None, "px", "py"), P("px", None, "py"), P("px", "py"), P("px", "py")),
        out_specs=P(None, "px", "py"),
        check_vma=False,
    )
```

time: 101 us -> 86.9 us (0.86)
  the two profiles are of different devices: /device:TPU:19 before, /device:TPU:10 now
where the time goes in v3:
time: 86.9 us; the launch traced here: 86.5 us
  Pallas kernels  39.9 us (46%)
  starting transfers between devices  23 us (26%)
  local copies, waits for them, and re-layouts  11.7 us (13%)
  waiting for transfers between devices  11.7 us (13%)
    pallas_call x6, Pallas kernels, call(): pl.pallas_call(functools.partial(kernel, **kw) if kw else kernel, out_sha...  39.9 us
    unnamed x30, local copies, waits for them, and re-layouts  11.7 us
    ppermute x2, starting transfers between devices, on_device(): recv2 = lax.ppermute(send2, 'px', pairs2)  10.2 us
    ppermute x1, waiting for transfers between devices, on_device(): side1 = lax.ppermute(jnp.where(even, top, bottom), 'px', pairs1)  8.73 us
    all_to_all x1, starting transfers between devices, on_device(): lax.all_to_all(blocks, 'px', split_axis=0, concat_axis=0, tiled=True)  7.33 us
    ppermute x1, starting transfers between devices, on_device(): side2 = lax.ppermute(jnp.where(even, bottom, top), 'px', pairs2)  4.29 us
    ppermute x1, waiting for transfers between devices, on_device(): side2 = lax.ppermute(jnp.where(even, bottom, top), 'px', pairs2)  2.97 us
  transfers between devices with their start and end apart: 8, of which 2 were waited for; matrix products, arithmetic and copies ran while one was open for 0% of the time, Pallas kernels for 38%

profile of v3, /device:TPU:10, one launch (start us, length us, event | category | flops | bytes accessed | tf_op | source)
XLA Modules:
  0.0 86.5 jit_solution(11569651415604970036)
XLA Ops:
  0.0 1.2 %copy-done.4 = f32[8,256,128]{2,1,0:T(8,128)S(1)} copy-done((f32[8,256,128]{2,1,0:T(8,128)S(1)}, f32[8,256,128]{2,1,0:T(8,128)}, u32[]{:S(2)}) %copy-start.4) | copy-done | bytes 1048600
  1.2 1.0 %shard_map.59 = f32[16,8,16,128]{3,2,1,0:T(8,128)} custom-call(f32[8,256,128]{2,1,0:T(8,128)S(1)} %copy-done.4), custom_call_target="tpu_custom_call" | custom-call | tf_op jit(solution)/shard_map/pallas_call | solution.py:353
  2.3 7.3 %all-to-all-start = ((f32[16,8,16,128]{3,2,1,0:T(8,128)}), f32[16,8,16,128]{3,2,1,0:T(8,128)S(1)}, u32[]{:S(2)}, u32[]{:S(2)}) async-start(f32[16,8,16,128]{3,2,1,0:T(8,128)} %shard_map.59), calls=%async_computation | async-start | bytes 2097152 | tf_op jit(solution)/shard_map/all_to_all | solution.py:399
  9.6 1.3 %shard_map.55 = (f32[16,128,128]{2,1,0:T(8,128)S(1)}, f32[640,128]{1,0:T(8,128)}, f32[640,128]{1,0:T(8,128)}, f32[16,16,128]{2,1,0:T(8,128)S(1)}) custom-call(f32[2048,128]{1,0:T(8,128)S(1)} %bitcast.5), custom_call_target="tpu_custom_call" | custom-call | tf_op jit(solution)/shard_map/pallas_call | solution.py:353
  10.9 1.0 %copy-done.6 = f32[16,128,128]{2,1,0:T(8,128)} copy-done((f32[16,128,128]{2,1,0:T(8,128)}, f32[16,128,128]{2,1,0:T(8,128)S(1)}, u32[]{:S(2)}) %copy-start.6) | copy-done | bytes 1048600
  12.4 4.3 %collective-permute-start.1 = (f32[640,128]{1,0:T(8,128)}, f32[640,128]{1,0:T(8,128)}, u32[]{:S(2)}, u32[]{:S(2)}) collective-permute-start(f32[640,128]{1,0:T(8,128)} %get-tuple-element.20), channel_id=1, source_target_pairs={{2,4},{4,2},{6,8},{8,6},{10,12},{12,10},{14,16},{16,14},{18,20},{2... | collective-permute-start | bytes 983048 | tf_op jit(solution)/shard_map/ppermute | solution.py:380
  16.8 0.6 collective-permute-start.3
  17.4 4.3 %collective-permute-start.4 = (f32[1,6,16,128]{3,2,1,0:T(8,128)S(1)}, f32[1,6,16,128]{3,2,1,0:T(8,128)S(1)}, u32[]{:S(2)}, u32[]{:S(2)}) collective-permute-start(f32[1,6,16,128]{3,2,1,0:T(8,128)S(1)} %get-tuple-element.33), channel_id=1, source_target_pairs={{2,4},{4,2},{6,8},{8,6},{10,12},{12,10},{14,16},{16,14},{18,20},{2... | collective-permute-start | bytes 147464 | tf_op jit(solution)/shard_map/ppermute | solution.py:386
  21.7 1.2 %copy-done.7 = f32[16,128,128]{2,1,0:T(8,128)S(1)} copy-done((f32[16,128,128]{2,1,0:T(8,128)S(1)}, f32[16,128,128]{2,1,0:T(8,128)}, u32[]{:S(2)}) %copy-start.7) | copy-done | bytes 1048600
  22.9 6.2 %shard_map.56 = (f32[28,160,128]{2,1,0:T(8,128)S(1)}, f32[22,160,128]{2,1,0:T(8,128)S(1)}) custom-call(f32[3,16,128]{2,1,0:T(8,128)S(1)} %copy-done.8, f32[16,128,128]{2,1,0:T(8,128)S(1)} %copy-done.7, f32[16,16,128]{2,1,0:T(8,128)S(1)} %collective-permute-done.2.ylow_ref.yhigh_ref, f32[16,16,128]{2,1,0:T(8,128)S(1)} %collective-permute-done.2.ylow_ref.yhigh_ref), custom_call_target="tpu_custom_call" | custom-call | tf_op jit(solution)/shard_map/pallas_call | solution.py:353
  29.2 8.7 %collective-permute-done.3.side1_ref = f32[1,6,16,128]{3,2,1,0:T(8,128)S(1)} collective-permute-done((f32[1,6,16,128]{3,2,1,0:T(8,128)S(1)}, f32[1,6,16,128]{3,2,1,0:T(8,128)S(1)}, u32[]{:S(2)}, u32[]{:S(2)}) %collective-permute-start.3) | collective-permute-done | bytes 49184 | tf_op jit(solution)/shard_map/ppermute | solution.py:385
  37.9 3.0 %collective-permute-done.4.side2_ref = f32[1,6,16,128]{3,2,1,0:T(8,128)S(1)} collective-permute-done((f32[1,6,16,128]{3,2,1,0:T(8,128)S(1)}, f32[1,6,16,128]{3,2,1,0:T(8,128)S(1)}, u32[]{:S(2)}, u32[]{:S(2)}) %collective-permute-start.4) | collective-permute-done | bytes 49184 | tf_op jit(solution)/shard_map/ppermute | solution.py:386
  40.9 12.7 %shard_map.57 = (f32[28,160,128]{2,1,0:T(8,128)S(1)}, f32[22,160,128]{2,1,0:T(8,128)S(1)}, f32[22,160,128]{2,1,0:T(8,128)S(1)}, f32[340,128]{1,0:T(8,128)S(1)}, f32[340,128]{1,0:T(8,128)S(1)}) custom-call(f32[3,16,128]{2,1,0:T(8,128)S(1)} %copy-done.8, f32[640,128]{1,0:T(8,128)} %collective-permute-done.recv1_ref, ...), custom_call_target="tpu_custom_call", output_to_operand_aliasing={{0}: (5, {}), {1}: (6, {})} | custom-call | tf_op jit(solution)/shard_map/pallas_call | solution.py:353
  53.7 5.9 %collective-permute-start.6 = (f32[340,128]{1,0:T(8,128)S(1)}, f32[340,128]{1,0:T(8,128)S(1)}, u32[]{:S(2)}, u32[]{:S(2)}) collective-permute-start(f32[340,128]{1,0:T(8,128)S(1)} %get-tuple-element.26), channel_id=1, source_target_pairs={{2,4},{4,2},{6,8},{8,6},{10,12},{12,10},{14,16},{16,14},{18,20},{2... | collective-permute-start | bytes 522248 | tf_op jit(solution)/shard_map/ppermute | solution.py:409
  59.6 12.5 %shard_map.58 = (f32[22,160,128]{2,1,0:T(8,128)S(1)}, f32[16,160,128]{2,1,0:T(8,128)S(1)}) custom-call(f32[3,16,128]{2,1,0:T(8,128)S(1)} %copy-done.8, f32[28,160,128]{2,1,0:T(8,128)S(1)} %get-tuple-element.27.field, f32[22,160,128]{2,1,0:T(8,128)S(1)} %get-tuple-element.28.one, ...), custom_call_target="tpu_custom_call", output_to_operand_aliasing={{0}: (3, {})} | custom-call | tf_op jit(solution)/shard_map/pallas_call | solution.py:353
  72.1 1.2 %copy-done = f32[22,160,128]{2,1,0:T(8,128)} copy-done((f32[22,160,128]{2,1,0:T(8,128)}, f32[22,160,128]{2,1,0:T(8,128)S(1)}, u32[]{:S(2)}) %copy-start) | copy-done | bytes 1802264
  73.4 1.1 %copy-done.2 = f32[16,160,128]{2,1,0:T(8,128)} copy-done((f32[16,160,128]{2,1,0:T(8,128)}, f32[16,160,128]{2,1,0:T(8,128)S(1)}, u32[]{:S(2)}) %copy-start.2) | copy-done | bytes 1310744
  74.4 0.7 copy-done.9
  75.1 0.7 copy-done.11
  75.8 1.5 %copy-done.1 = f32[22,160,128]{2,1,0:T(8,128)S(1)} copy-done((f32[22,160,128]{2,1,0:T(8,128)S(1)}, f32[22,160,128]{2,1,0:T(8,128)}, u32[]{:S(2)}) %copy-start.1) | copy-done | bytes 1802264
  77.3 1.3 %copy-done.3 = f32[16,160,128]{2,1,0:T(8,128)S(1)} copy-done((f32[16,160,128]{2,1,0:T(8,128)S(1)}, f32[16,160,128]{2,1,0:T(8,128)}, u32[]{:S(2)}) %copy-start.3) | copy-done | bytes 1310744
  78.6 0.9 %copy-done.10 = f32[340,128]{1,0:T(8,128)S(1)} copy-done((f32[340,128]{1,0:T(8,128)S(1)}, f32[340,128]{1,0:T(8,128)}, u32[]{:S(2)}) %copy-start.10) | copy-done | bytes 174104
  79.5 0.9 %copy-done.12 = f32[340,128]{1,0:T(8,128)S(1)} copy-done((f32[340,128]{1,0:T(8,128)S(1)}, f32[340,128]{1,0:T(8,128)}, u32[]{:S(2)}) %copy-start.12) | copy-done | bytes 174104
  80.4 6.0 %shard_map.60 = (f32[2048,128]{1,0:T(8,128)}, f32[22,160,128]{2,1,0:T(8,128)S(1)}, f32[16,160,128]{2,1,0:T(8,128)S(1)}) custom-call(f32[3,16,128]{2,1,0:T(8,128)S(1)} %copy-done.8, f32[340,128]{1,0:T(8,128)S(1)} %copy-done.10, f32[340,128]{1,0:T(8,128)S(1)} %copy-done.12, ...), custom_call_target="tpu_custom_call", output_to_operand_aliasing={{1}: (4, {}), {2}: (5, {})} | custom-call | tf_op jit(solution)/shard_map/pallas_call | solution.py:353
  (29 shorter events, 0.7 us)
Async XLA Ops:
  0.0 1.2 %copy-start.4 = (f32[8,256,128]{2,1,0:T(8,128)S(1)}, f32[8,256,128]{2,1,0:T(8,128)}, u32[]{:S(2)}) copy-start(f32[8,256,128]{2,1,0:T(8,128)} %p_ref.1) | copy-start | bytes 3145732
  1.2 8.4 %copy-start.5 = (f32[128,16,128]{2,1,0:T(8,128)S(1)}, f32[128,16,128]{2,1,0:T(8,128)}, u32[]{:S(2)}) copy-start(f32[128,16,128]{2,1,0:T(8,128)} %param.5) | copy-start | bytes 3145732
  2.3 19.4 %copy-start.8 = (f32[3,16,128]{2,1,0:T(8,128)S(1)}, f32[3,16,128]{2,1,0:T(8,128)}, u32[]{:S(2)}) copy-start(f32[3,16,128]{2,1,0:T(8,128)} %constant.14.clone.const_ref) | copy-start | bytes 73732
  2.3 73.5 %all-to-all-start = ((f32[16,8,16,128]{3,2,1,0:T(8,128)}), f32[16,8,16,128]{3,2,1,0:T(8,128)S(1)}, u32[]{:S(2)}, u32[]{:S(2)}) async-start(f32[16,8,16,128]{3,2,1,0:T(8,128)} %shard_map.59), calls=%async_computation | async-start | bytes 2097152 | tf_op jit(solution)/shard_map/all_to_all | solution.py:399
  10.9 1.0 %copy-start.6 = (f32[16,128,128]{2,1,0:T(8,128)}, f32[16,128,128]{2,1,0:T(8,128)S(1)}, u32[]{:S(2)}) copy-start(f32[16,128,128]{2,1,0:T(8,128)S(1)} %get-tuple-element.22.mid_ref) | copy-start | bytes 3145732
  11.9 4.8 %collective-permute-start.2 = (f32[16,16,128]{2,1,0:T(8,128)S(1)}, f32[16,16,128]{2,1,0:T(8,128)S(1)}, u32[]{:S(2)}, u32[]{:S(2)}) collective-permute-start(f32[16,16,128]{2,1,0:T(8,128)S(1)} %get-tuple-element.21), channel_id=1, source_target_pairs={{0,1},{1,0},{2,3},{3,2},{4,5},{5,4},{6,7},{7,6},{8,9},{9,8},{10,11... | collective-permute-start | bytes 393224 | tf_op jit(solution)/shard_map/ppermute | solution.py:373
  11.9 28.9 %collective-permute-start = (f32[640,128]{1,0:T(8,128)}, f32[640,128]{1,0:T(8,128)}, u32[]{:S(2)}, u32[]{:S(2)}) collective-permute-start(f32[640,128]{1,0:T(8,128)} %get-tuple-element.19), channel_id=1, source_target_pairs={{0,2},{2,0},{4,6},{6,4},{8,10},{10,8},{12,14},{14,12},{16,18},{18,... | collective-permute-start | bytes 983048 | tf_op jit(solution)/shard_map/ppermute | solution.py:379
  12.4 28.4 %collective-permute-start.1 = (f32[640,128]{1,0:T(8,128)}, f32[640,128]{1,0:T(8,128)}, u32[]{:S(2)}, u32[]{:S(2)}) collective-permute-start(f32[640,128]{1,0:T(8,128)} %get-tuple-element.20), channel_id=1, source_target_pairs={{2,4},{4,2},{6,8},{8,6},{10,12},{12,10},{14,16},{16,14},{18,20},{2... | collective-permute-start | bytes 983048 | tf_op jit(solution)/shard_map/ppermute | solution.py:380
  16.8 21.1 %collective-permute-start.3 = (f32[1,6,16,128]{3,2,1,0:T(8,128)S(1)}, f32[1,6,16,128]{3,2,1,0:T(8,128)S(1)}, u32[]{:S(2)}, u32[]{:S(2)}) collective-permute-start(f32[1,6,16,128]{3,2,1,0:T(8,128)S(1)} %get-tuple-element.34), channel_id=1, source_target_pairs={{0,2},{2,0},{4,6},{6,4},{8,10},{10,8},{12,14},{14,12},{16,18},{18,... | collective-permute-start | bytes 147464 | tf_op jit(solution)/shard_map/ppermute | solution.py:385
  17.4 23.5 %collective-permute-start.4 = (f32[1,6,16,128]{3,2,1,0:T(8,128)S(1)}, f32[1,6,16,128]{3,2,1,0:T(8,128)S(1)}, u32[]{:S(2)}, u32[]{:S(2)}) collective-permute-start(f32[1,6,16,128]{3,2,1,0:T(8,128)S(1)} %get-tuple-element.33), channel_id=1, source_target_pairs={{2,4},{4,2},{6,8},{8,6},{10,12},{12,10},{14,16},{16,14},{18,20},{2... | collective-permute-start | bytes 147464 | tf_op jit(solution)/shard_map/ppermute | solution.py:386
  21.7 1.2 %copy-start.7 = (f32[16,128,128]{2,1,0:T(8,128)S(1)}, f32[16,128,128]{2,1,0:T(8,128)}, u32[]{:S(2)}) copy-start(f32[16,128,128]{2,1,0:T(8,128)} %copy-done.6) | copy-start | bytes 3145732
  53.6 20.8 %collective-permute-start.5 = (f32[340,128]{1,0:T(8,128)S(1)}, f32[340,128]{1,0:T(8,128)S(1)}, u32[]{:S(2)}, u32[]{:S(2)}) collective-permute-start(f32[340,128]{1,0:T(8,128)S(1)} %get-tuple-element.25), channel_id=1, source_target_pairs={{0,2},{2,0},{4,6},{6,4},{8,10},{10,8},{12,14},{14,12},{16,18},{18,... | collective-permute-start | bytes 522248 | tf_op jit(solution)/shard_map/ppermute | solution.py:408
  53.7 21.4 %collective-permute-start.6 = (f32[340,128]{1,0:T(8,128)S(1)}, f32[340,128]{1,0:T(8,128)S(1)}, u32[]{:S(2)}, u32[]{:S(2)}) collective-permute-start(f32[340,128]{1,0:T(8,128)S(1)} %get-tuple-element.26), channel_id=1, source_target_pairs={{2,4},{4,2},{6,8},{8,6},{10,12},{12,10},{14,16},{16,14},{18,20},{2... | collective-permute-start | bytes 522248 | tf_op jit(solution)/shard_map/ppermute | solution.py:409
  59.6 16.2 %copy-start.13 = (f32[16,128]{1,0:T(8,128)S(1)}, f32[16,128]{1,0:T(8,128)}, u32[]{:S(2)}) copy-start(f32[16,128]{1,0:T(8,128)} %reach_ref.1) | copy-start | bytes 24580
  59.6 16.2 %copy-start.14 = (f32[16,128]{1,0:T(8,128)S(1)}, f32[16,128]{1,0:T(8,128)}, u32[]{:S(2)}) copy-start(f32[16,128]{1,0:T(8,128)} %avoid_ref.1) | copy-start | bytes 24580
  72.1 1.2 %copy-start = (f32[22,160,128]{2,1,0:T(8,128)}, f32[22,160,128]{2,1,0:T(8,128)S(1)}, u32[]{:S(2)}) copy-start(f32[22,160,128]{2,1,0:T(8,128)S(1)} %get-tuple-element.30.two_in) | copy-start | bytes 5406724
  73.4 1.1 %copy-start.2 = (f32[16,160,128]{2,1,0:T(8,128)}, f32[16,160,128]{2,1,0:T(8,128)S(1)}, u32[]{:S(2)}) copy-start(f32[16,160,128]{2,1,0:T(8,128)S(1)} %get-tuple-element.31.three_in) | copy-start | bytes 3932164
  74.4 0.7 copy-start.9
  75.1 0.7 copy-start.11
  75.8 1.5 %copy-start.1 = (f32[22,160,128]{2,1,0:T(8,128)S(1)}, f32[22,160,128]{2,1,0:T(8,128)}, u32[]{:S(2)}) copy-start(f32[22,160,128]{2,1,0:T(8,128)} %copy-done) | copy-start | bytes 5406724
  77.3 1.3 %copy-start.3 = (f32[16,160,128]{2,1,0:T(8,128)S(1)}, f32[16,160,128]{2,1,0:T(8,128)}, u32[]{:S(2)}) copy-start(f32[16,160,128]{2,1,0:T(8,128)} %copy-done.2) | copy-start | bytes 3932164
  78.6 0.9 %copy-start.10 = (f32[340,128]{1,0:T(8,128)S(1)}, f32[340,128]{1,0:T(8,128)}, u32[]{:S(2)}) copy-start(f32[340,128]{1,0:T(8,128)} %copy-done.9) | copy-start | bytes 522244
  79.5 0.9 %copy-start.12 = (f32[340,128]{1,0:T(8,128)S(1)}, f32[340,128]{1,0:T(8,128)}, u32[]{:S(2)}) copy-start(f32[340,128]{1,0:T(8,128)} %copy-done.11) | copy-start | bytes 522244

commit v4 on v3

--- a/solution.py
+++ b/solution.py
@@ -8,6 +8,7 @@
 from jax.experimental import pallas as pl
 from jax.experimental.pallas import tpu as pltpu
 from jax.sharding import PartitionSpec as P
+
 
 EPS = 1e-06
 SPACING = 1.0 / 64.0
@@ -192,7 +193,8 @@
         left(slabs[1])
 
 
-def spread_kernel(p_ref, o_ref):
+def spread_kernel(p_ref, after_ref, o_ref):
+    del after_ref
     rows = o_ref.shape[2]
     for i in range(o_ref.shape[0]):
         o_ref[i] = p_ref[:, pl.ds(i * rows, rows), :]
@@ -324,7 +326,7 @@
     stage(2, (two, 3), (three, 0), (field, DEPTH), part, const_ref, parts, (cols, 0, gap), turns[2])
 
 
-def last_kernel(const_ref, recv1_ref, recv2_ref, field, two_in, three_in, prior_ref, reach_ref, avoid_ref, o_ref, two, three, part, *, turns, gap, rows, cols):
+def last_kernel(const_ref, recv1_ref, recv2_ref, field, two_in, three_in, o_ref, two, three, part, *, turns, gap, rows, cols):
     del two_in, three_in
     seg, start = columns_of(cols, 3)
 
@@ -335,10 +337,7 @@
     parts = [(0, 3), (rows - 3, rows)]
     stage(2, (two, 3), (three, 0), (field, DEPTH), part, const_ref, parts, (cols, 0, gap), turns[2])
     for r in range(rows):
-        lines = pl.ds(r, LANES, stride=rows)
-        value = three[r, pl.ds(OFF, cols), :].T
-        kept = jnp.maximum(avoid_ref[pl.ds(r, LANES, stride=0), :], jnp.minimum(reach_ref[pl.ds(r, LANES, stride=0), :], value))
-        o_ref[lines, :] = jnp.minimum(prior_ref[lines, :], kept)
+        o_ref[pl.ds(r, LANES, stride=rows), :] = three[r, pl.ds(OFF, cols), :].T
 
 
 def on_device(start_value, prior, reach, avoid):
@@ -349,11 +348,11 @@
     f32 = jnp.float32
     vmem = pl.BlockSpec(memory_space=pltpu.VMEM)
 
-    def call(kernel, outs, *args, limit=LIMIT, aliases={}, scratch=(), **kw):
+    def call(kernel, outs, *args, limit=LIMIT, aliases={}, scratch=(), untouched=(), **kw):
         return pl.pallas_call(
             functools.partial(kernel, **kw) if kw else kernel,
             out_shape=[jax.ShapeDtypeStruct(o, f32) for o in outs],
-            in_specs=[vmem] * len(args),
+            in_specs=[pl.BlockSpec(memory_space=pl.ANY) if i in untouched else vmem for i in range(len(args))],
             out_specs=[vmem] * len(outs),
             input_output_aliases=aliases,
             scratch_shapes=[pltpu.VMEM(shape, f32) for shape in scratch],
@@ -395,7 +394,7 @@
     scratch = [(max(rows - 6, 12), seg, SUB, LANES)]
     field, one = call(inner_kernel, [tall, short], table, mid, yslabs[0], yslabs[-1], scratch=scratch, **common)
 
-    blocks = call(spread_kernel, [(nx, headings // nx, rows, cols)], prior)[0]
+    blocks = call(spread_kernel, [(nx, headings // nx, rows, cols)], prior, one, untouched=(1,))[0]
     regrouped = lax.all_to_all(blocks, "px", split_axis=0, concat_axis=0, tiled=True)
 
     common = dict(common, rows=rows, cols=cols)
@@ -410,12 +409,13 @@
     two, three = call(
         middle_kernel, [short, (rows, wide, headings)], table, field, one, two, aliases={3: 0}, scratch=scratch, **common
     )
-    out = call(
+    third = call(
         last_kernel, [(headings * rows, cols), short, (rows, wide, headings)],
-        table, recv1, recv2, field, two, three, regrouped.reshape(headings * rows, cols), reach, avoid,
+        table, recv1, recv2, field, two, three,
         aliases={4: 1, 5: 2}, scratch=scratch, **common,
     )[0]
-    return out.reshape(headings, rows, cols)
+    third = third.reshape(headings, rows, cols)
+    return jnp.minimum(regrouped.reshape(headings, rows, cols), jnp.maximum(avoid[None], jnp.minimum(reach[None], third)))
 
 
 def solution(mesh):

time: 86.9 us -> 91.4 us (1.052)
  waiting for transfers between devices: 11.7 us -> 21.2 us
  local copies, waits for them, and re-layouts: 11.7 us -> 4.7 us
  other arithmetic: 0.01 us -> 2.41 us
  Pallas kernels: 39.9 us -> 37.5 us
  starting transfers between devices: 23 us -> 25 us
    ppermute x1, waiting for transfers between devices: 2.97 us -> 19.8 us  [on_device(): side2 = lax.ppermute(jnp.where(even, bottom, top), 'px', pairs2)]
    ppermute x1, waiting for transfers between devices: 8.73 us -> 0.01 us  [on_device(): side1 = lax.ppermute(jnp.where(even, top, bottom), 'px', pairs1)]
    unnamed x30 -> x16, local copies, waits for them, and re-layouts: 11.7 us -> 4.7 us
    min x0 -> x1, other arithmetic: none -> 2.4 us  [on_device(): jnp.minimum(regrouped.reshape(headings, rows, cols), jnp.maximum(avoid[No...]
    pallas_call x6, Pallas kernels: 39.9 us -> 37.5 us  [call(): pl.pallas_call(functools.partial(kernel, **kw) if kw else kernel, out_sha...]
    ppermute x1, starting transfers between devices: 0.6 us -> 2.43 us  [on_device(): side1 = lax.ppermute(jnp.where(even, top, bottom), 'px', pairs1)]
    ppermute x1, starting transfers between devices: 4.29 us -> 2.47 us  [on_device(): side2 = lax.ppermute(jnp.where(even, bottom, top), 'px', pairs2)]
    ppermute x2, starting transfers between devices: 0.6 us -> 2.37 us  [on_device(): recv1 = lax.ppermute(send1, 'px', pairs1)]
  transfers between devices with their start and end apart: 8 -> 8, of which waited for: 2 -> 2; matrix products, arithmetic and copies ran while one was open for 0% -> 0% of each run, Pallas kernels for 38% -> 32%
where the time goes in v4:
time: 91.4 us; the launch traced here: 91 us
  Pallas kernels  37.5 us (41%)
  starting transfers between devices  25 us (27%)
  waiting for transfers between devices  21.2 us (23%)
  local copies, waits for them, and re-layouts  4.7 us (5%)
  other arithmetic  2.41 us (3%)
    pallas_call x6, Pallas kernels, call(): pl.pallas_call(functools.partial(kernel, **kw) if kw else kernel, out_sha...  37.5 us
    ppermute x1, waiting for transfers between devices, on_device(): side2 = lax.ppermute(jnp.where(even, bottom, top), 'px', pairs2)  19.8 us
    ppermute x2, starting transfers between devices, on_device(): recv2 = lax.ppermute(send2, 'px', pairs2)  10.4 us
    all_to_all x1, starting transfers between devices, on_device(): lax.all_to_all(blocks, 'px', split_axis=0, concat_axis=0, tiled=True)  7.33 us
    unnamed x16, local copies, waits for them, and re-layouts  4.7 us
    ppermute x1, starting transfers between devices, on_device(): side2 = lax.ppermute(jnp.where(even, bottom, top), 'px', pairs2)  2.47 us
    ppermute x1, starting transfers between devices, on_device(): side1 = lax.ppermute(jnp.where(even, top, bottom), 'px', pairs1)  2.43 us
    min x1, other arithmetic, on_device(): jnp.minimum(regrouped.reshape(headings, rows, cols), jnp.maximum(avoid[No...  2.4 us
  transfers between devices with their start and end apart: 8, of which 2 were waited for; matrix products, arithmetic and copies ran while one was open for 0% of the time, Pallas kernels for 32%

profile of v4, /device:TPU:10, one launch (start us, length us, event | category | flops | bytes accessed | tf_op | source)
XLA Modules:
  0.0 91.0 jit_solution(9159248912040656385)
XLA Ops:
  0.0 1.2 %copy-done.2 = f32[128,16,128]{2,1,0:T(8,128)S(1)} copy-done((f32[128,16,128]{2,1,0:T(8,128)S(1)}, f32[128,16,128]{2,1,0:T(8,128)}, u32[]{:S(2)}) %copy-start.2) | copy-done | bytes 1048600
  1.2 1.2 %shard_map.55 = (f32[16,128,128]{2,1,0:T(8,128)S(1)}, f32[640,128]{1,0:T(8,128)}, f32[640,128]{1,0:T(8,128)S(1)}, f32[16,16,128]{2,1,0:T(8,128)S(1)}) custom-call(f32[2048,128]{1,0:T(8,128)S(1)} %bitcast.6), custom_call_target="tpu_custom_call" | custom-call | tf_op jit(solution)/shard_map/pallas_call | solution.py:352
  2.5 0.0 collective-permute-start
  2.5 1.3 %collective-permute-done.ylow_ref.yhigh_ref = f32[16,16,128]{2,1,0:T(8,128)S(1)} collective-permute-done((f32[16,16,128]{2,1,0:T(8,128)S(1)}, f32[16,16,128]{2,1,0:T(8,128)S(1)}, u32[]{:S(2)}, u32[]{:S(2)}) %collective-permute-start) | collective-permute-done | bytes 131104 | tf_op jit(solution)/shard_map/ppermute | solution.py:372
  3.8 0.7 copy-done.4
  4.6 6.2 %shard_map.56 = (f32[28,160,128]{2,1,0:T(8,128)S(1)}, f32[22,160,128]{2,1,0:T(8,128)S(1)}) custom-call(f32[3,16,128]{2,1,0:T(8,128)S(1)} %copy-done.4, f32[16,128,128]{2,1,0:T(8,128)S(1)} %get-tuple-element.19.mid_ref, f32[16,16,128]{2,1,0:T(8,128)S(1)} %collective-permute-done.ylow_ref.yhigh_ref, f32[16,16,128]{2,1,0:T(8,128)S(1)} %collective-permute-done.ylow_ref.yhigh_ref), custom_call_target="tpu_custom_call" | custom-call | tf_op jit(solution)/shard_map/pallas_call | solution.py:352
  10.8 1.0 %shard_map.57 = f32[16,8,16,128]{3,2,1,0:T(8,128)} custom-call(f32[8,256,128]{2,1,0:T(8,128)S(1)} %copy-done.3, f32[22,160,128]{2,1,0:T(8,128)S(1)} %get-tuple-element.21.after_ref.one_in), custom_call_target="tpu_custom_call" | custom-call | tf_op jit(solution)/shard_map/pallas_call | solution.py:352
  11.8 1.2 %copy-done = f32[22,160,128]{2,1,0:T(8,128)} copy-done((f32[22,160,128]{2,1,0:T(8,128)}, f32[22,160,128]{2,1,0:T(8,128)S(1)}, u32[]{:S(2)}) %copy-start) | copy-done | bytes 1802264
  13.1 7.3 %all-to-all-start = ((f32[16,8,16,128]{3,2,1,0:T(8,128)}), f32[16,8,16,128]{3,2,1,0:T(8,128)}, u32[]{:S(2)}, u32[]{:S(2)}) async-start(f32[16,8,16,128]{3,2,1,0:T(8,128)} %shard_map.57), calls=%async_computation | async-start | bytes 2097152 | tf_op jit(solution)/shard_map/all_to_all | solution.py:398
  20.4 0.6 collective-permute-start.1
  21.0 4.3 %collective-permute-start.2 = (f32[640,128]{1,0:T(8,128)S(1)}, f32[640,128]{1,0:T(8,128)S(1)}, u32[]{:S(2)}, u32[]{:S(2)}) collective-permute-start(f32[640,128]{1,0:T(8,128)S(1)} %get-tuple-element.23), channel_id=1, source_target_pairs={{2,4},{4,2},{6,8},{8,6},{10,12},{12,10},{14,16},{16,14},{18,20},{2... | collective-permute-start | bytes 983048 | tf_op jit(solution)/shard_map/ppermute | solution.py:379
  25.3 2.5 %collective-permute-start.4 = (f32[1,6,16,128]{3,2,1,0:T(8,128)S(1)}, f32[1,6,16,128]{3,2,1,0:T(8,128)S(1)}, u32[]{:S(2)}, u32[]{:S(2)}) collective-permute-start(f32[1,6,16,128]{3,2,1,0:T(8,128)S(1)} %get-tuple-element.33), channel_id=1, source_target_pairs={{2,4},{4,2},{6,8},{8,6},{10,12},{12,10},{14,16},{16,14},{18,20},{2... | collective-permute-start | bytes 147464 | tf_op jit(solution)/shard_map/ppermute | solution.py:385
  27.7 2.4 %collective-permute-start.3 = (f32[1,6,16,128]{3,2,1,0:T(8,128)S(1)}, f32[1,6,16,128]{3,2,1,0:T(8,128)S(1)}, u32[]{:S(2)}, u32[]{:S(2)}) collective-permute-start(f32[1,6,16,128]{3,2,1,0:T(8,128)S(1)} %get-tuple-element.34), channel_id=1, source_target_pairs={{0,2},{2,0},{4,6},{6,4},{8,10},{10,8},{12,14},{14,12},{16,18},{18,... | collective-permute-start | bytes 147464 | tf_op jit(solution)/shard_map/ppermute | solution.py:384
  30.2 19.8 %collective-permute-done.4.side2_ref = f32[1,6,16,128]{3,2,1,0:T(8,128)S(1)} collective-permute-done((f32[1,6,16,128]{3,2,1,0:T(8,128)S(1)}, f32[1,6,16,128]{3,2,1,0:T(8,128)S(1)}, u32[]{:S(2)}, u32[]{:S(2)}) %collective-permute-start.4) | collective-permute-done | bytes 49184 | tf_op jit(solution)/shard_map/ppermute | solution.py:385
  50.0 0.0 collective-permute-done.3.side1_ref
  50.0 1.5 %copy-done.1 = f32[22,160,128]{2,1,0:T(8,128)S(1)} copy-done((f32[22,160,128]{2,1,0:T(8,128)S(1)}, f32[22,160,128]{2,1,0:T(8,128)}, u32[]{:S(2)}) %copy-start.1) | copy-done | bytes 1802264
  51.5 11.6 %shard_map.58 = (f32[28,160,128]{2,1,0:T(8,128)S(1)}, f32[22,160,128]{2,1,0:T(8,128)S(1)}, f32[22,160,128]{2,1,0:T(8,128)S(1)}, f32[340,128]{1,0:T(8,128)S(1)}, f32[340,128]{1,0:T(8,128)S(1)}) custom-call(f32[3,16,128]{2,1,0:T(8,128)S(1)} %copy-done.5, ...), custom_call_target="tpu_custom_call", output_to_operand_aliasing={{0}: (5, {}), {1}: (6, {})} | custom-call | tf_op jit(solution)/shard_map/pallas_call | solution.py:352
  63.2 1.8 %collective-permute-start.5 = (f32[340,128]{1,0:T(8,128)S(1)}, f32[340,128]{1,0:T(8,128)S(1)}, u32[]{:S(2)}, u32[]{:S(2)}) collective-permute-start(f32[340,128]{1,0:T(8,128)S(1)} %get-tuple-element.25), channel_id=1, source_target_pairs={{0,2},{2,0},{4,6},{6,4},{8,10},{10,8},{12,14},{14,12},{16,18},{18,... | collective-permute-start | bytes 522248 | tf_op jit(solution)/shard_map/ppermute | solution.py:407
  65.0 6.2 %collective-permute-start.6 = (f32[340,128]{1,0:T(8,128)S(1)}, f32[340,128]{1,0:T(8,128)S(1)}, u32[]{:S(2)}, u32[]{:S(2)}) collective-permute-start(f32[340,128]{1,0:T(8,128)S(1)} %get-tuple-element.26), channel_id=1, source_target_pairs={{2,4},{4,2},{6,8},{8,6},{10,12},{12,10},{14,16},{16,14},{18,20},{2... | collective-permute-start | bytes 522248 | tf_op jit(solution)/shard_map/ppermute | solution.py:408
  71.2 12.5 %shard_map.59 = (f32[22,160,128]{2,1,0:T(8,128)S(1)}, f32[16,160,128]{2,1,0:T(8,128)S(1)}) custom-call(f32[3,16,128]{2,1,0:T(8,128)S(1)} %copy-done.5, f32[28,160,128]{2,1,0:T(8,128)S(1)} %get-tuple-element.27.field, f32[22,160,128]{2,1,0:T(8,128)S(1)} %get-tuple-element.28.one, ...), custom_call_target="tpu_custom_call", output_to_operand_aliasing={{0}: (3, {})} | custom-call | tf_op jit(solution)/shard_map/pallas_call | solution.py:352
  83.7 0.0 copy-start.6
  83.7 0.0 copy-start.7
  83.7 4.9 %shard_map.60 = (f32[2048,128]{1,0:T(8,128)S(1)}, f32[22,160,128]{2,1,0:T(8,128)S(1)}, f32[16,160,128]{2,1,0:T(8,128)S(1)}) custom-call(f32[3,16,128]{2,1,0:T(8,128)S(1)} %copy-done.5, f32[340,128]{1,0:T(8,128)S(1)} %collective-permute-done.5.recv1_ref, ...), custom_call_target="tpu_custom_call", output_to_operand_aliasing={{1}: (4, {}), {2}: (5, {})} | custom-call | tf_op jit(solution)/shard_map/pallas_call | solution.py:352
  88.6 2.4 %bitcast_minimum_fusion = f32[128,16,128]{2,1,0:T(8,128)} fusion(f32[16,8,16,128]{3,2,1,0:T(8,128)} %all-to-all-done, f32[128,16,128]{2,1,0:T(8,128)S(1)} %bitcast.5, f32[16,128]{1,0:T(8,128)S(1)} %copy-done.6, f32[16,128]{1,0:T(8,128)S(1)} %copy-done.7), kind=kLoop, calls=%fused_computation | loop fusion | flops 786432 | bytes 3162112 | tf_op jit(solution)/shard_map/min | solution.py:418
  (16 shorter events, 0.0 us)
Async XLA Ops:
  0.0 1.2 %copy-start.2 = (f32[128,16,128]{2,1,0:T(8,128)S(1)}, f32[128,16,128]{2,1,0:T(8,128)}, u32[]{:S(2)}) copy-start(f32[128,16,128]{2,1,0:T(8,128)} %param.5) | copy-start | bytes 3145732
  1.2 9.6 %copy-start.3 = (f32[8,256,128]{2,1,0:T(8,128)S(1)}, f32[8,256,128]{2,1,0:T(8,128)}, u32[]{:S(2)}) copy-start(f32[8,256,128]{2,1,0:T(8,128)} %p_ref.1) | copy-start | bytes 3145732
  2.5 1.3 %collective-permute-start = (f32[16,16,128]{2,1,0:T(8,128)S(1)}, f32[16,16,128]{2,1,0:T(8,128)S(1)}, u32[]{:S(2)}, u32[]{:S(2)}) collective-permute-start(f32[16,16,128]{2,1,0:T(8,128)S(1)} %get-tuple-element.20), channel_id=1, source_target_pairs={{0,1},{1,0},{2,3},{3,2},{4,5},{5,4},{6,7},{7,6},{8,9},{9,8},{10,11... | collective-permute-start | bytes 393224 | tf_op jit(solution)/shard_map/ppermute | solution.py:372
  3.8 0.7 copy-start.4
  11.8 1.2 %copy-start = (f32[22,160,128]{2,1,0:T(8,128)}, f32[22,160,128]{2,1,0:T(8,128)S(1)}, u32[]{:S(2)}) copy-start(f32[22,160,128]{2,1,0:T(8,128)S(1)} %get-tuple-element.21.after_ref.one_in) | copy-start | bytes 5406724
  13.1 37.0 %copy-start.5 = (f32[3,16,128]{2,1,0:T(8,128)S(1)}, f32[3,16,128]{2,1,0:T(8,128)}, u32[]{:S(2)}) copy-start(f32[3,16,128]{2,1,0:T(8,128)} %constant.14.clone.const_ref) | copy-start | bytes 73732
  13.1 75.5 %all-to-all-start = ((f32[16,8,16,128]{3,2,1,0:T(8,128)}), f32[16,8,16,128]{3,2,1,0:T(8,128)}, u32[]{:S(2)}, u32[]{:S(2)}) async-start(f32[16,8,16,128]{3,2,1,0:T(8,128)} %shard_map.57), calls=%async_computation | async-start | bytes 2097152 | tf_op jit(solution)/shard_map/all_to_all | solution.py:398
  20.4 29.6 %collective-permute-start.1 = (f32[640,128]{1,0:T(8,128)}, f32[640,128]{1,0:T(8,128)S(1)}, u32[]{:S(2)}, u32[]{:S(2)}) collective-permute-start(f32[640,128]{1,0:T(8,128)} %get-tuple-element.22), channel_id=1, source_target_pairs={{0,2},{2,0},{4,6},{6,4},{8,10},{10,8},{12,14},{14,12},{16,18},{18,... | collective-permute-start | bytes 983048 | tf_op jit(solution)/shard_map/ppermute | solution.py:378
  21.0 29.1 %collective-permute-start.2 = (f32[640,128]{1,0:T(8,128)S(1)}, f32[640,128]{1,0:T(8,128)S(1)}, u32[]{:S(2)}, u32[]{:S(2)}) collective-permute-start(f32[640,128]{1,0:T(8,128)S(1)} %get-tuple-element.23), channel_id=1, source_target_pairs={{2,4},{4,2},{6,8},{8,6},{10,12},{12,10},{14,16},{16,14},{18,20},{2... | collective-permute-start | bytes 983048 | tf_op jit(solution)/shard_map/ppermute | solution.py:379
  25.3 24.8 %collective-permute-start.4 = (f32[1,6,16,128]{3,2,1,0:T(8,128)S(1)}, f32[1,6,16,128]{3,2,1,0:T(8,128)S(1)}, u32[]{:S(2)}, u32[]{:S(2)}) collective-permute-start(f32[1,6,16,128]{3,2,1,0:T(8,128)S(1)} %get-tuple-element.33), channel_id=1, source_target_pairs={{2,4},{4,2},{6,8},{8,6},{10,12},{12,10},{14,16},{16,14},{18,20},{2... | collective-permute-start | bytes 147464 | tf_op jit(solution)/shard_map/ppermute | solution.py:385
  27.7 22.3 %collective-permute-start.3 = (f32[1,6,16,128]{3,2,1,0:T(8,128)S(1)}, f32[1,6,16,128]{3,2,1,0:T(8,128)S(1)}, u32[]{:S(2)}, u32[]{:S(2)}) collective-permute-start(f32[1,6,16,128]{3,2,1,0:T(8,128)S(1)} %get-tuple-element.34), channel_id=1, source_target_pairs={{0,2},{2,0},{4,6},{6,4},{8,10},{10,8},{12,14},{14,12},{16,18},{18,... | collective-permute-start | bytes 147464 | tf_op jit(solution)/shard_map/ppermute | solution.py:384
  50.0 1.5 %copy-start.1 = (f32[22,160,128]{2,1,0:T(8,128)S(1)}, f32[22,160,128]{2,1,0:T(8,128)}, u32[]{:S(2)}) copy-start(f32[22,160,128]{2,1,0:T(8,128)} %copy-done) | copy-start | bytes 5406724
  63.2 20.5 %collective-permute-start.5 = (f32[340,128]{1,0:T(8,128)S(1)}, f32[340,128]{1,0:T(8,128)S(1)}, u32[]{:S(2)}, u32[]{:S(2)}) collective-permute-start(f32[340,128]{1,0:T(8,128)S(1)} %get-tuple-element.25), channel_id=1, source_target_pairs={{0,2},{2,0},{4,6},{6,4},{8,10},{10,8},{12,14},{14,12},{16,18},{18,... | collective-permute-start | bytes 522248 | tf_op jit(solution)/shard_map/ppermute | solution.py:407
  65.0 18.7 %collective-permute-start.6 = (f32[340,128]{1,0:T(8,128)S(1)}, f32[340,128]{1,0:T(8,128)S(1)}, u32[]{:S(2)}, u32[]{:S(2)}) collective-permute-start(f32[340,128]{1,0:T(8,128)S(1)} %get-tuple-element.26), channel_id=1, source_target_pairs={{2,4},{4,2},{6,8},{8,6},{10,12},{12,10},{14,16},{16,14},{18,20},{2... | collective-permute-start | bytes 522248 | tf_op jit(solution)/shard_map/ppermute | solution.py:408
  83.7 4.9 %copy-start.6 = (f32[16,128]{1,0:T(8,128)S(1)}, f32[16,128]{1,0:T(8,128)}, u32[]{:S(2)}) copy-start(f32[16,128]{1,0:T(8,128)} %param.7) | copy-start | bytes 24580
  83.7 4.9 %copy-start.7 = (f32[16,128]{1,0:T(8,128)S(1)}, f32[16,128]{1,0:T(8,128)}, u32[]{:S(2)}) copy-start(f32[16,128]{1,0:T(8,128)} %param.8) | copy-start | bytes 24580

commit v5 on v4

--- a/solution.py
+++ b/solution.py
@@ -178,26 +178,69 @@
         unpack(two_ref, False)
 
 
-def prep_kernel(x_ref, mid_ref, one_ref, two_ref, *slabs):
-    rows, cols = mid_ref.shape[:2]
+def prep_kernel(x_ref, const_ref, own_ref, *slabs):
+    del const_ref
+    rows = own_ref.shape[0]
+    cols = x_ref.shape[1]
     for r in range(rows):
-        mid_ref[r] = x_ref[pl.ds(r, LANES, stride=rows), :].T
-    pack_pair(one_ref, two_ref, lambda r: mid_ref[r], rows, cols, FULL1, HALF1)
-    right = lambda ref: ref.__setitem__(Ellipsis, mid_ref[:, pl.ds(cols - OFF, OFF), :])
-    left = lambda ref: ref.__setitem__(Ellipsis, mid_ref[:, pl.ds(0, OFF), :])
+        own_ref[r, pl.ds(OFF, cols), :] = x_ref[pl.ds(r, LANES, stride=rows), :].T
+
+    def cut(ref, begin):
+        ref[...] = own_ref[:, pl.ds(begin, OFF), :]
+
     if len(slabs) == 1:
-        pl.when(lax.axis_index("py") == 0)(lambda: right(slabs[0]))
-        pl.when(lax.axis_index("py") != 0)(lambda: left(slabs[0]))
+        pl.when(lax.axis_index("py") == 0)(lambda: cut(slabs[0], cols))
+        pl.when(lax.axis_index("py") != 0)(lambda: cut(slabs[0], OFF))
     else:
-        right(slabs[0])
-        left(slabs[1])
-
-
-def spread_kernel(p_ref, after_ref, o_ref):
+        cut(slabs[0], cols)
+        cut(slabs[1], OFF)
+
+
+def send_kernel(own_in, ylow_ref, yhigh_ref, own, one_ref, two_ref):
+    del own_in
+    rows, wide = own.shape[:2]
+    cols = wide - 2 * OFF
+    own[:, pl.ds(0, OFF), :] = ylow_ref[...]
+    own[:, pl.ds(OFF + cols, OFF), :] = yhigh_ref[...]
+    clear_columns((own, 0), [(0, rows)], cols)
+    for begin, count, at in message_parts(cols):
+        read = lambda r: own[r, pl.ds(beside(begin), count), :]
+        where = pl.ds(at, message_lines(count))
+        pack_pair(one_ref.at[where], two_ref.at[where], read, rows, count, FULL1, HALF1)
+
+
+def message_parts(cols):
+    begins = [0, -OFF, cols]
+    if lax.axis_size("py") == 2:
+        begins = [0, pl.multiple_of(jnp.where(lax.axis_index("py") == 0, cols, -OFF), OFF)]
+    parts, at = [], 0
+    for begin in begins:
+        count = OFF if parts else cols
+        parts.append((begin, count, at))
+        at += message_lines(count)
+    return parts
+
+
+def beside(begin):
+    return OFF + begin if isinstance(begin, int) else pl.multiple_of(OFF + begin, OFF)
+
+
+def message_lines(count):
+    return FULL1 * count + HALF1 * (count // 2)
+
+
+def spread_kernel(p_ref, after_ref, o_ref, held, came, gone):
     del after_ref
-    rows = o_ref.shape[2]
-    for i in range(o_ref.shape[0]):
-        o_ref[i] = p_ref[:, pl.ds(i * rows, rows), :]
+    count, rows = o_ref.shape[0], o_ref.shape[2]
+    load = lambda i: pltpu.make_async_copy(p_ref.at[:, pl.ds(i * rows, rows), :], held.at[i], came.at[i])
+    save = lambda i: pltpu.make_async_copy(held.at[i], o_ref.at[i], gone.at[i])
+    for i in range(count):
+        load(i).start()
+    for i in range(count):
+        load(i).wait()
+        save(i).start()
+    for i in range(count):
+        save(i).wait()
 
 
 def columns_of(cols, margin):
@@ -264,42 +307,28 @@
                 dst[0][pl.ds(lo + dst[1], hi - lo), pl.ds(begin, OFF), :] = jnp.zeros((hi - lo, OFF, LANES), jnp.float32)
 
 
-def inner_kernel(const_ref, mid_ref, ylow_ref, yhigh_ref, field, one, part, *, turns, gap):
-    rows, cols = mid_ref.shape[:2]
-    own = pl.ds(DEPTH, rows)
-    field[own, pl.ds(OFF, cols), :] = mid_ref[...]
-    field[own, pl.ds(0, OFF), :] = ylow_ref[...]
-    field[own, pl.ds(OFF + cols, OFF), :] = yhigh_ref[...]
-    clear_columns((field, DEPTH), [(0, rows)], cols)
+def inner_kernel(const_ref, own, one, part, *, turns, gap):
+    rows, wide = own.shape[:2]
+    cols = wide - 2 * OFF
     parts = [(3, rows - 3)]
-    stage(0, (field, DEPTH), (one, 3), None, part, const_ref, parts, (cols, 6, gap), turns[0])
-    clear_columns((one, 3), parts, cols)
-
-
-def outer_kernel(const_ref, recv1_ref, recv2_ref, side1_ref, side2_ref, field_in, one_in, field, one, two, send1, send2, part, *, turns, gap, rows, cols):
-    del field_in, one_in
+    stage(0, (own, 0), (one, -3), None, part, const_ref, parts, (cols, 6, gap), turns[0])
+    clear_columns((one, -3), parts, cols)
+
+
+def outer_kernel(const_ref, recv1_ref, recv2_ref, own, inner, one, two, send1, send2, field, part, *, turns, gap):
+    rows, wide = own.shape[:2]
+    cols = wide - 2 * OFF
 
     def write(row, col, values):
-        field[row + DEPTH, pl.ds(OFF + col, values.shape[0]), :] = values
-
-    unpack_pair(recv1_ref, recv2_ref, write, rows, cols, FULL1, HALF1)
-    low, high = pl.ds(0, DEPTH), pl.ds(DEPTH + rows, DEPTH)
-
-    def sides(ref, where):
-        field[where, pl.ds(0, OFF), :] = ref[0]
-        field[where, pl.ds(OFF + cols, OFF), :] = ref[ref.shape[0] - 1]
-
-    @pl.when(even_tile())
-    def _():
-        sides(side1_ref, high)
-        sides(side2_ref, low)
-
-    @pl.when(jnp.logical_not(even_tile()))
-    def _():
-        sides(side1_ref, low)
-        sides(side2_ref, high)
-
+        field[row + DEPTH, pl.ds(beside(begin) + col, values.shape[0]), :] = values
+
+    for begin, count, at in message_parts(cols):
+        where = pl.ds(at, message_lines(count))
+        unpack_pair(recv1_ref.at[where], recv2_ref.at[where], write, rows, count, FULL1, HALF1)
     clear_columns((field, DEPTH), [(-DEPTH, 0), (rows, rows + DEPTH)], cols)
+    field[pl.ds(DEPTH, DEPTH)] = own[pl.ds(0, DEPTH)]
+    field[pl.ds(rows, DEPTH)] = own[pl.ds(rows - DEPTH, DEPTH)]
+    one[pl.ds(6, rows - 6)] = inner[...]
     parts = [(-3, 3), (rows - 3, rows + 3)]
     stage(0, (field, DEPTH), (one, 3), None, part, const_ref, parts, (cols, 6, gap), turns[0])
     clear_columns((one, 3), parts, cols)
@@ -311,23 +340,27 @@
             one[pl.ds(begin, 3)] = jnp.zeros((3,) + one.shape[1:], jnp.float32)
 
     parts = [(0, 3), (rows - 3, rows)]
-    stage(1, (one, 3), (two, 3), (field, DEPTH), part, const_ref, parts, (cols, 3, gap), turns[1])
+    stage(1, (one, 3), (two, 3), (own, 0), part, const_ref, parts, (cols, 3, gap), turns[1])
     clear_columns((two, 3), parts, cols)
     seg, start = columns_of(cols, 3)
     count = seg * SUB
     pack_pair(send1, send2, lambda r: two[r + 3, pl.ds(OFF + start, count), :], rows, count, FULL2, HALF2)
 
 
-def middle_kernel(const_ref, field, one, two_in, two, three, part, *, turns, gap, rows, cols):
+def middle_kernel(const_ref, own, one, two_in, two, three, part, *, turns, gap):
     del two_in
+    rows, wide = own.shape[:2]
+    cols = wide - 2 * OFF
     parts = [(3, rows - 3)]
-    stage(1, (one, 3), (two, 3), (field, DEPTH), part, const_ref, parts, (cols, 3, gap), turns[1])
+    stage(1, (one, 3), (two, 3), (own, 0), part, const_ref, parts, (cols, 3, gap), turns[1])
     clear_columns((two, 3), parts, cols)
-    stage(2, (two, 3), (three, 0), (field, DEPTH), part, const_ref, parts, (cols, 0, gap), turns[2])
-
-
-def last_kernel(const_ref, recv1_ref, recv2_ref, field, two_in, three_in, o_ref, two, three, part, *, turns, gap, rows, cols):
+    stage(2, (two, 3), (three, 0), (own, 0), part, const_ref, parts, (cols, 0, gap), turns[2])
+
+
+def last_kernel(const_ref, recv1_ref, recv2_ref, own, two_in, three_in, o_ref, two, three, part, *, turns, gap):
     del two_in, three_in
+    rows, wide = own.shape[:2]
+    cols = wide - 2 * OFF
     seg, start = columns_of(cols, 3)
 
     def write(row, col, values):
@@ -335,9 +368,14 @@
 
     unpack_pair(recv1_ref, recv2_ref, write, rows, seg * SUB, FULL2, HALF2)
     parts = [(0, 3), (rows - 3, rows)]
-    stage(2, (two, 3), (three, 0), (field, DEPTH), part, const_ref, parts, (cols, 0, gap), turns[2])
+    stage(2, (two, 3), (three, 0), (own, 0), part, const_ref, parts, (cols, 0, gap), turns[2])
     for r in range(rows):
         o_ref[pl.ds(r, LANES, stride=rows), :] = three[r, pl.ds(OFF, cols), :].T
+
+
+def final_kernel(third_ref, prior_ref, reach_ref, avoid_ref, o_ref):
+    kept = jnp.maximum(avoid_ref[...][None], jnp.minimum(reach_ref[...][None], third_ref[...]))
+    o_ref[...] = jnp.minimum(prior_ref[...], kept)
 
 
 def on_device(start_value, prior, reach, avoid):
@@ -348,23 +386,31 @@
     f32 = jnp.float32
     vmem = pl.BlockSpec(memory_space=pltpu.VMEM)
 
-    def call(kernel, outs, *args, limit=LIMIT, aliases={}, scratch=(), untouched=(), **kw):
+    def call(kernel, outs, *args, limit=LIMIT, aliases={}, scratch=(), **kw):
         return pl.pallas_call(
             functools.partial(kernel, **kw) if kw else kernel,
             out_shape=[jax.ShapeDtypeStruct(o, f32) for o in outs],
-            in_specs=[pl.BlockSpec(memory_space=pl.ANY) if i in untouched else vmem for i in range(len(args))],
+            in_specs=[vmem] * len(args),
             out_specs=[vmem] * len(outs),
             input_output_aliases=aliases,
             scratch_shapes=[pltpu.VMEM(shape, f32) for shape in scratch],
             compiler_params=pltpu.CompilerParams(vmem_limit_bytes=limit * 2**20),
         )(*args)
 
+    tables = [stage_constants(headings, part) for part in (1.0, 0.25, 2.0 / 3.0)]
+    table = jnp.asarray(np.stack([t[0] for t in tables]))
+    common = dict(turns=[t[1] for t in tables], gap=gap)
+    seg = columns_of(cols, 6)[0]
+    wide = cols + 2 * OFF
+    tall = (rows + 2 * DEPTH, wide, headings)
+    short = (rows + 6, wide, headings)
+    work = (max(rows - 6, 12), seg, SUB, LANES)
+
     sides = 1 if ny == 2 else 2
-    message = (FULL1 * cols + HALF1 * cols // 2, headings)
-    mid, send1, send2, *slabs = call(
+    own, *slabs = call(
         prep_kernel,
-        [(rows, cols, headings), message, message] + [(rows, OFF, headings)] * sides,
-        start_value.reshape(headings * rows, cols),
+        [(rows, wide, headings)] + [(rows, OFF, headings)] * sides,
+        start_value.reshape(headings * rows, cols), table,
     )
     pairs1 = [(i, i ^ 1) for i in range(nx)]
     pairs2 = [(i, j) for i in range(nx) for j in [((i + 1) ^ 1) - 1] if 0 <= j < nx]
@@ -375,47 +421,51 @@
             lax.ppermute(slabs[0], "py", [(i, i + 1) for i in range(ny - 1)]),
             lax.ppermute(slabs[1], "py", [(i + 1, i) for i in range(ny - 1)]),
         ]
+    lines = message_lines(cols) + sides * message_lines(OFF)
+    own, send1, send2 = call(
+        send_kernel, [(rows, wide, headings)] + [(lines, headings)] * 2, own, yslabs[0], yslabs[-1], aliases={0: 0}
+    )
     recv1 = lax.ppermute(send1, "px", pairs1)
     recv2 = lax.ppermute(send2, "px", pairs2)
-    corners = jnp.stack(yslabs)
-    even = lax.rem(lax.axis_index("px"), 2) == 0
-    top = lax.slice_in_dim(corners, rows - DEPTH, rows, axis=1)
-    bottom = lax.slice_in_dim(corners, 0, DEPTH, axis=1)
-    side1 = lax.ppermute(jnp.where(even, top, bottom), "px", pairs1)
-    side2 = lax.ppermute(jnp.where(even, bottom, top), "px", pairs2)
-
-    tables = [stage_constants(headings, part) for part in (1.0, 0.25, 2.0 / 3.0)]
-    table = jnp.asarray(np.stack([t[0] for t in tables]))
-    common = dict(turns=[t[1] for t in tables], gap=gap)
-    seg = columns_of(cols, 6)[0]
-    wide = cols + 2 * OFF
-    tall = (rows + 2 * DEPTH, wide, headings)
-    short = (rows + 6, wide, headings)
-    scratch = [(max(rows - 6, 12), seg, SUB, LANES)]
-    field, one = call(inner_kernel, [tall, short], table, mid, yslabs[0], yslabs[-1], scratch=scratch, **common)
-
-    blocks = call(spread_kernel, [(nx, headings // nx, rows, cols)], prior, one, untouched=(1,))[0]
+    inner = call(inner_kernel, [(rows - 6, wide, headings)], table, own, scratch=[work], **common)[0]
+
+    blocks = (nx, headings // nx, rows, cols)
+    hbm = pl.BlockSpec(memory_space=pltpu.HBM)
+    blocks = pl.pallas_call(
+        spread_kernel,
+        out_shape=jax.ShapeDtypeStruct(blocks, f32),
+        in_specs=[hbm, pl.BlockSpec(memory_space=pl.ANY)],
+        out_specs=hbm,
+        scratch_shapes=[pltpu.VMEM(blocks, f32), pltpu.SemaphoreType.DMA((nx,)), pltpu.SemaphoreType.DMA((nx,))],
+        compiler_params=pltpu.CompilerParams(vmem_limit_bytes=61 * 2**20),
+    )(prior, inner)
     regrouped = lax.all_to_all(blocks, "px", split_axis=0, concat_axis=0, tiled=True)
 
-    common = dict(common, rows=rows, cols=cols)
     count = columns_of(cols, 3)[0] * SUB
     message = (FULL2 * count + HALF2 * count // 2, headings)
-    field, one, two, send1, send2 = call(
-        outer_kernel, [tall, short, short, message, message],
-        table, recv1, recv2, side1, side2, field, one, aliases={5: 0, 6: 1}, scratch=scratch, **common,
+    one, two, send1, send2 = call(
+        outer_kernel, [short, short, message, message], table, recv1, recv2, own, inner, scratch=[tall, work], **common
     )
     recv1 = lax.ppermute(send1, "px", pairs1)
     recv2 = lax.ppermute(send2, "px", pairs2)
     two, three = call(
-        middle_kernel, [short, (rows, wide, headings)], table, field, one, two, aliases={3: 0}, scratch=scratch, **common
+        middle_kernel, [short, (rows, wide, headings)], table, own, one, two, aliases={3: 0}, scratch=[work], **common
     )
     third = call(
         last_kernel, [(headings * rows, cols), short, (rows, wide, headings)],
-        table, recv1, recv2, field, two, three,
-        aliases={4: 1, 5: 2}, scratch=scratch, **common,
+        table, recv1, recv2, own, two, three, aliases={4: 1, 5: 2}, scratch=[work], **common,
     )[0]
-    third = third.reshape(headings, rows, cols)
-    return jnp.minimum(regrouped.reshape(headings, rows, cols), jnp.maximum(avoid[None], jnp.minimum(reach[None], third)))
+    cut = 16
+    block = pl.BlockSpec((cut, rows, cols), lambda i: (i, 0, 0))
+    plane = pl.BlockSpec((rows, cols), lambda i: (0, 0))
+    return pl.pallas_call(
+        final_kernel,
+        grid=(headings // cut,),
+        out_shape=jax.ShapeDtypeStruct((headings, rows, cols), f32),
+        in_specs=[block, block, plane, plane],
+        out_specs=block,
+        compiler_params=pltpu.CompilerParams(vmem_limit_bytes=LIMIT * 2**20),
+    )(third.reshape(headings, rows, cols), regrouped.reshape(headings, rows, cols), reach, avoid)
 
 
 def solution(mesh):

time: 91.4 us -> 93.8 us (1.026)
  Pallas kernels: 37.5 us -> 43.3 us
  starting transfers between devices: 25 us -> 20.3 us
  waiting for transfers between devices: 21.2 us -> 25.8 us
  other arithmetic: 2.41 us -> 0 us
  local copies, waits for them, and re-layouts: 4.7 us -> 3.65 us
    ppermute x2 -> x0, waiting for transfers between devices: 19.9 us -> none  [the longest x1 19.8 us: on_device(): side2 = lax.ppermute(jnp.where(even, bottom, top), 'px', pairs2)]
    ppermute x2, waiting for transfers between devices: 0.01 us -> 12.6 us  [on_device(): recv1 = lax.ppermute(send1, 'px', pairs1)]
    ppermute x2, waiting for transfers between devices: 0.01 us -> 11.9 us  [on_device(): recv2 = lax.ppermute(send2, 'px', pairs2)]
    pallas_call x0 -> x2, Pallas kernels: none -> 7.4 us  [the longest x1 5.24 us: on_device(): pl.pallas_call(final_kernel, grid=(headings // cut,), out_shape=jax.Shape...]
    ppermute x2 -> x0, starting transfers between devices: 4.9 us -> none  [the longest x1 2.47 us: on_device(): side2 = lax.ppermute(jnp.where(even, bottom, top), 'px', pairs2)]
    min x1 -> x0, other arithmetic: 2.4 us -> none  [on_device(): jnp.minimum(regrouped.reshape(headings, rows, cols), jnp.maximum(avoid[No...]
    pallas_call x6, Pallas kernels: 37.5 us -> 35.9 us  [call(): pl.pallas_call(functools.partial(kernel, **kw) if kw else kernel, out_sha...]
    unnamed x16 -> x18, local copies, waits for them, and re-layouts: 4.7 us -> 3.65 us
  transfers between devices with their start and end apart: 8 -> 6, of which waited for: 2 -> 3; matrix products, arithmetic and copies ran while one was open for 0% -> 0% of each run, Pallas kernels for 32% -> 31%
where the time goes in v5:
time: 93.8 us; the launch traced here: 93.3 us
  Pallas kernels  43.3 us (46%)
  waiting for transfers between devices  25.8 us (28%)
  starting transfers between devices  20.3 us (22%)
  local copies, waits for them, and re-layouts  3.65 us (4%)
    pallas_call x6, Pallas kernels, call(): pl.pallas_call(functools.partial(kernel, **kw) if kw else kernel, out_sha...  35.9 us
    ppermute x2, waiting for transfers between devices, on_device(): recv1 = lax.ppermute(send1, 'px', pairs1)  12.6 us
    ppermute x2, waiting for transfers between devices, on_device(): recv2 = lax.ppermute(send2, 'px', pairs2)  11.9 us
    ppermute x2, starting transfers between devices, on_device(): recv2 = lax.ppermute(send2, 'px', pairs2)  10.4 us
    all_to_all x1, starting transfers between devices, on_device(): lax.all_to_all(blocks, 'px', split_axis=0, concat_axis=0, tiled=True)  7.34 us
    pallas_call x1, Pallas kernels, on_device(): pl.pallas_call(final_kernel, grid=(headings // cut,), out_shape=jax.Shape...  5.24 us
    unnamed x18, local copies, waits for them, and re-layouts  3.65 us
    ppermute x2, starting transfers between devices, on_device(): recv1 = lax.ppermute(send1, 'px', pairs1)  2.5 us
  transfers between devices with their start and end apart: 6, of which 3 were waited for; matrix products, arithmetic and copies ran while one was open for 0% of the time, Pallas kernels for 31%

profile of v5, /device:TPU:10, one launch (start us, length us, event | category | flops | bytes accessed | tf_op | source)
XLA Modules:
  0.0 93.3 jit_solution(16088749382478333510)
XLA Ops:
  0.0 1.2 %copy-done.2 = f32[128,16,128]{2,1,0:T(8,128)S(1)} copy-done((f32[128,16,128]{2,1,0:T(8,128)S(1)}, f32[128,16,128]{2,1,0:T(8,128)}, u32[]{:S(2)}) %copy-start.2) | copy-done | bytes 1048600
  1.2 0.7 copy-done.3
  2.0 0.4 shard_map.55
  2.3 0.1 collective-permute-start
  2.4 1.3 %collective-permute-done.ylow_ref.yhigh_ref = f32[16,16,128]{2,1,0:T(8,128)S(1)} collective-permute-done((f32[16,16,128]{2,1,0:T(8,128)S(1)}, f32[16,16,128]{2,1,0:T(8,128)S(1)}, u32[]{:S(2)}, u32[]{:S(2)}) %collective-permute-start) | collective-permute-done | bytes 131104 | tf_op jit(solution)/shard_map/ppermute | solution.py:418
  3.8 0.2 shard_map.56
  4.0 0.0 copy-start.7
  4.0 0.7 copy-done.7
  4.7 6.1 %shard_map.57.inner.after_ref = f32[10,160,128]{2,1,0:T(8,128)S(1)} custom-call(f32[3,16,128]{2,1,0:T(8,128)S(1)} %copy-done.3, f32[16,160,128]{2,1,0:T(8,128)S(1)} %get-tuple-element.21.own), custom_call_target="tpu_custom_call" | custom-call | tf_op jit(solution)/shard_map/pallas_call | solution.py:390
  10.9 0.9 copy-done
  11.8 2.2 %shard_map.61 = f32[16,8,16,128]{3,2,1,0:T(8,128)} custom-call(f32[8,256,128]{2,1,0:T(8,128)} %p_ref.1, f32[10,160,128]{2,1,0:T(8,128)} %copy-done), custom_call_target="tpu_custom_call" | custom-call | tf_op jit(solution)/shard_map/pallas_call | solution.py:434
  14.0 7.3 %all-to-all-start = ((f32[16,8,16,128]{3,2,1,0:T(8,128)}), f32[16,8,16,128]{3,2,1,0:T(8,128)}, u32[]{:S(2)}, u32[]{:S(2)}) async-start(f32[16,8,16,128]{3,2,1,0:T(8,128)} %shard_map.61), calls=%async_computation | async-start | bytes 2097152 | tf_op jit(solution)/shard_map/all_to_all | solution.py:442
  21.3 0.6 collective-permute-start.1
  22.0 4.3 %collective-permute-start.2 = (f32[720,128]{1,0:T(8,128)S(1)}, f32[720,128]{1,0:T(8,128)S(1)}, u32[]{:S(2)}, u32[]{:S(2)}) collective-permute-start(f32[720,128]{1,0:T(8,128)S(1)} %get-tuple-element.20), channel_id=1, source_target_pairs={{2,4},{4,2},{6,8},{8,6},{10,12},{12,10},{14,16},{16,14},{18,20},{2... | collective-permute-start | bytes 1105928 | tf_op jit(solution)/shard_map/ppermute | solution.py:429
  26.2 12.6 %collective-permute-done.1.recv1_ref = f32[720,128]{1,0:T(8,128)S(1)} collective-permute-done((f32[720,128]{1,0:T(8,128)S(1)}, f32[720,128]{1,0:T(8,128)S(1)}, u32[]{:S(2)}, u32[]{:S(2)}) %collective-permute-start.1) | collective-permute-done | bytes 368672 | tf_op jit(solution)/shard_map/ppermute | solution.py:428
  38.8 11.9 %collective-permute-done.2.recv2_ref = f32[720,128]{1,0:T(8,128)S(1)} collective-permute-done((f32[720,128]{1,0:T(8,128)S(1)}, f32[720,128]{1,0:T(8,128)S(1)}, u32[]{:S(2)}, u32[]{:S(2)}) %collective-permute-start.2) | collective-permute-done | bytes 368672 | tf_op jit(solution)/shard_map/ppermute | solution.py:429
  50.7 11.8 %shard_map.58 = (f32[22,160,128]{2,1,0:T(8,128)S(1)}, f32[22,160,128]{2,1,0:T(8,128)S(1)}, f32[340,128]{1,0:T(8,128)S(1)}, f32[340,128]{1,0:T(8,128)S(1)}) custom-call(f32[3,16,128]{2,1,0:T(8,128)S(1)} %copy-done.4, f32[720,128]{1,0:T(8,128)S(1)} %collective-permute-done.1.recv1_ref, f32[720,128]{1,0:T(8,128)S(1)} %collective-permute-done.2.recv2_ref, ...), custom_call_target="tpu_custom_call" | custom-call | tf_op jit(solution)/shard_map/pallas_call | solution.py:390
  62.5 1.9 %collective-permute-start.3 = (f32[340,128]{1,0:T(8,128)S(1)}, f32[340,128]{1,0:T(8,128)S(1)}, u32[]{:S(2)}, u32[]{:S(2)}) collective-permute-start(f32[340,128]{1,0:T(8,128)S(1)} %get-tuple-element.22), channel_id=1, source_target_pairs={{0,2},{2,0},{4,6},{6,4},{8,10},{10,8},{12,14},{14,12},{16,18},{18,... | collective-permute-start | bytes 522248 | tf_op jit(solution)/shard_map/ppermute | solution.py:449
  64.4 6.2 %collective-permute-start.4 = (f32[340,128]{1,0:T(8,128)S(1)}, f32[340,128]{1,0:T(8,128)S(1)}, u32[]{:S(2)}, u32[]{:S(2)}) collective-permute-start(f32[340,128]{1,0:T(8,128)S(1)} %get-tuple-element.23), channel_id=1, source_target_pairs={{2,4},{4,2},{6,8},{8,6},{10,12},{12,10},{14,16},{16,14},{18,20},{2... | collective-permute-start | bytes 522248 | tf_op jit(solution)/shard_map/ppermute | solution.py:450
  70.6 12.5 %shard_map.59 = (f32[22,160,128]{2,1,0:T(8,128)S(1)}, f32[16,160,128]{2,1,0:T(8,128)S(1)}) custom-call(f32[3,16,128]{2,1,0:T(8,128)S(1)} %copy-done.4, f32[16,160,128]{2,1,0:T(8,128)S(1)} %get-tuple-element.21.own, f32[22,160,128]{2,1,0:T(8,128)S(1)} %get-tuple-element.24.one, ...), custom_call_target="tpu_custom_call", output_to_operand_aliasing={{0}: (3, {})} | custom-call | tf_op jit(solution)/shard_map/pallas_call | solution.py:390
  83.1 0.0 copy-start.5
  83.1 0.0 copy-start.6
  83.1 4.9 %shard_map.60 = (f32[2048,128]{1,0:T(8,128)S(1)}, f32[22,160,128]{2,1,0:T(8,128)S(1)}, f32[16,160,128]{2,1,0:T(8,128)S(1)}) custom-call(f32[3,16,128]{2,1,0:T(8,128)S(1)} %copy-done.4, f32[340,128]{1,0:T(8,128)S(1)} %collective-permute-done.3.recv1_ref, ...), custom_call_target="tpu_custom_call", output_to_operand_aliasing={{1}: (4, {}), {2}: (5, {})} | custom-call | tf_op jit(solution)/shard_map/pallas_call | solution.py:390
  88.0 5.2 %shard_map.62 = f32[128,16,128]{2,1,0:T(8,128)} custom-call(f32[128,16,128]{2,1,0:T(8,128)S(1)} %bitcast.3, f32[128,16,128]{2,1,0:T(8,128)} %bitcast.2.prior_ref, f32[16,128]{1,0:T(8,128)S(1)} %copy-done.5, f32[16,128]{1,0:T(8,128)S(1)} %copy-done.6), custom_call_target="tpu_custom_call" | custom-call | tf_op jit(solution)/shard_map/pallas_call | solution.py:461
  (14 shorter events, 0.0 us)
Async XLA Ops:
  0.0 1.2 %copy-start.2 = (f32[128,16,128]{2,1,0:T(8,128)S(1)}, f32[128,16,128]{2,1,0:T(8,128)}, u32[]{:S(2)}) copy-start(f32[128,16,128]{2,1,0:T(8,128)} %param.5) | copy-start | bytes 3145732
  1.2 0.7 copy-start.3
  2.3 1.4 %collective-permute-start = (f32[16,16,128]{2,1,0:T(8,128)S(1)}, f32[16,16,128]{2,1,0:T(8,128)S(1)}, u32[]{:S(2)}, u32[]{:S(2)}) collective-permute-start(f32[16,16,128]{2,1,0:T(8,128)S(1)} %get-tuple-element.18), channel_id=1, source_target_pairs={{0,1},{1,0},{2,3},{3,2},{4,5},{5,4},{6,7},{7,6},{8,9},{9,8},{10,11... | collective-permute-start | bytes 393224 | tf_op jit(solution)/shard_map/ppermute | solution.py:418
  4.0 0.7 copy-start.7
  10.9 0.9 copy-start
  11.8 38.9 %copy-start.4 = (f32[3,16,128]{2,1,0:T(8,128)S(1)}, f32[3,16,128]{2,1,0:T(8,128)}, u32[]{:S(2)}) copy-start(f32[3,16,128]{2,1,0:T(8,128)} %constant.2.clone.const_ref) | copy-start | bytes 73732
  14.0 7.4 %copy-start.8 = (f32[720,128]{1,0:T(8,128)S(1)}, f32[720,128]{1,0:T(8,128)}, u32[]{:S(2)}) copy-start(f32[720,128]{1,0:T(8,128)} %copy-done.7) | copy-start | bytes 1105924
  14.0 36.7 %copy-start.1 = (f32[10,160,128]{2,1,0:T(8,128)S(1)}, f32[10,160,128]{2,1,0:T(8,128)}, u32[]{:S(2)}) copy-start(f32[10,160,128]{2,1,0:T(8,128)} %copy-done) | copy-start | bytes 2457604
  14.0 74.0 %all-to-all-start = ((f32[16,8,16,128]{3,2,1,0:T(8,128)}), f32[16,8,16,128]{3,2,1,0:T(8,128)}, u32[]{:S(2)}, u32[]{:S(2)}) async-start(f32[16,8,16,128]{3,2,1,0:T(8,128)} %shard_map.61), calls=%async_computation | async-start | bytes 2097152 | tf_op jit(solution)/shard_map/all_to_all | solution.py:442
  21.3 17.5 %collective-permute-start.1 = (f32[720,128]{1,0:T(8,128)S(1)}, f32[720,128]{1,0:T(8,128)S(1)}, u32[]{:S(2)}, u32[]{:S(2)}) collective-permute-start(f32[720,128]{1,0:T(8,128)S(1)} %copy-done.8), channel_id=1, source_target_pairs={{0,2},{2,0},{4,6},{6,4},{8,10},{10,8},{12,14},{14,12},{16,18},{18,... | collective-permute-start | bytes 1105928 | tf_op jit(solution)/shard_map/ppermute | solution.py:428
  22.0 28.7 %collective-permute-start.2 = (f32[720,128]{1,0:T(8,128)S(1)}, f32[720,128]{1,0:T(8,128)S(1)}, u32[]{:S(2)}, u32[]{:S(2)}) collective-permute-start(f32[720,128]{1,0:T(8,128)S(1)} %get-tuple-element.20), channel_id=1, source_target_pairs={{2,4},{4,2},{6,8},{8,6},{10,12},{12,10},{14,16},{16,14},{18,20},{2... | collective-permute-start | bytes 1105928 | tf_op jit(solution)/shard_map/ppermute | solution.py:429
  62.5 20.5 %collective-permute-start.3 = (f32[340,128]{1,0:T(8,128)S(1)}, f32[340,128]{1,0:T(8,128)S(1)}, u32[]{:S(2)}, u32[]{:S(2)}) collective-permute-start(f32[340,128]{1,0:T(8,128)S(1)} %get-tuple-element.22), channel_id=1, source_target_pairs={{0,2},{2,0},{4,6},{6,4},{8,10},{10,8},{12,14},{14,12},{16,18},{18,... | collective-permute-start | bytes 522248 | tf_op jit(solution)/shard_map/ppermute | solution.py:449
  64.4 18.7 %collective-permute-start.4 = (f32[340,128]{1,0:T(8,128)S(1)}, f32[340,128]{1,0:T(8,128)S(1)}, u32[]{:S(2)}, u32[]{:S(2)}) collective-permute-start(f32[340,128]{1,0:T(8,128)S(1)} %get-tuple-element.23), channel_id=1, source_target_pairs={{2,4},{4,2},{6,8},{8,6},{10,12},{12,10},{14,16},{16,14},{18,20},{2... | collective-permute-start | bytes 522248 | tf_op jit(solution)/shard_map/ppermute | solution.py:450
  83.1 4.9 %copy-start.5 = (f32[16,128]{1,0:T(8,128)S(1)}, f32[16,128]{1,0:T(8,128)}, u32[]{:S(2)}) copy-start(f32[16,128]{1,0:T(8,128)} %reach_ref.1) | copy-start | bytes 24580
  83.1 4.9 %copy-start.6 = (f32[16,128]{1,0:T(8,128)S(1)}, f32[16,128]{1,0:T(8,128)}, u32[]{:S(2)}) copy-start(f32[16,128]{1,0:T(8,128)} %avoid_ref.1) | copy-start | bytes 24580

commit v6 on v5

--- a/solution.py
+++ b/solution.py
@@ -15,6 +15,7 @@
 SPEED = 1.0
 TURN = 2.0
 COURANT = 0.5
+SHARES = (1.0, 0.25, 2.0 / 3.0)
 LANES = 128
 SUB = 8
 DEPTH = 6
@@ -28,26 +29,8 @@
     return -(-a // b)
 
 
-def stage_constants(headings, share):
-    gap = 2.0 * math.pi / headings
-    dt = COURANT / (2.0 * SPEED / SPACING + TURN / gap)
-    angles = (np.float32(gap) * np.arange(headings, dtype=np.float32)).astype(np.float64)
-    rows = []
-    for wave in (np.cos(angles), np.sin(angles)):
-        g = share * dt * SPEED * wave / SPACING
-        ahead = wave >= 0
-        rows += [
-            g,
-            np.where(ahead, -g / 3, g / 6),
-            np.where(ahead, -g / 6, g / 3),
-            np.where(ahead, 0.5, 1.0 / 6.0),
-            np.where(ahead, 1.0 / 6.0, 0.5),
-            np.where(ahead, g / 6, -g / 3),
-            np.where(ahead, g / 3, -g / 6),
-            np.where(ahead, 1.0, 0.0),
-        ]
-    turn = share * dt * TURN / (6.0 * gap)
-    return np.stack(rows).astype(np.float32), float(turn)
+def time_step(gap):
+    return COURANT / (2.0 * SPEED / SPACING + TURN / gap)
 
 
 def weights_of(a, b, d, eps, want):
@@ -178,10 +161,34 @@
         unpack(two_ref, False)
 
 
-def prep_kernel(x_ref, const_ref, own_ref, *slabs):
-    del const_ref
+def fill_table(table_ref):
+    headings = table_ref.shape[2]
+    gap = 2.0 * math.pi / headings
+    lane = lax.broadcasted_iota(jnp.int32, (SUB, headings), 1)
+    angle = lane.astype(jnp.float32) * np.float32(gap)
+    behind_x = (lane >= headings // 4) & (lane < 3 * headings // 4)
+    for stage_index, share in enumerate(SHARES):
+        step = share * time_step(gap) * SPEED / SPACING
+        for at, wave, back in ((0, jnp.cos(angle), behind_x), (8, jnp.sin(angle), lane > headings // 2)):
+            g = wave * np.float32(step)
+            rows = [
+                g,
+                g * jnp.where(back, 1.0 / 6.0, -1.0 / 3.0),
+                g * jnp.where(back, 1.0 / 3.0, -1.0 / 6.0),
+                jnp.where(back, 1.0 / 6.0, 0.5),
+                jnp.where(back, 0.5, 1.0 / 6.0),
+                g * jnp.where(back, -1.0 / 3.0, 1.0 / 6.0),
+                g * jnp.where(back, -1.0 / 6.0, 1.0 / 3.0),
+                jnp.where(back, 0.0, 1.0),
+            ]
+            for i, values in enumerate(rows):
+                table_ref[stage_index, pl.ds(at + i, 1), :] = values[:1]
+
+
+def prep_kernel(x_ref, own_ref, table_ref, *slabs):
     rows = own_ref.shape[0]
     cols = x_ref.shape[1]
+    fill_table(table_ref)
     for r in range(rows):
         own_ref[r, pl.ds(OFF, cols), :] = x_ref[pl.ds(r, LANES, stride=rows), :].T
 
@@ -194,6 +201,12 @@
     else:
         cut(slabs[0], cols)
         cut(slabs[1], OFF)
+
+
+def spread_kernel(p_ref, o_ref):
+    rows = o_ref.shape[2]
+    for i in range(o_ref.shape[0]):
+        o_ref[i] = p_ref[:, pl.ds(i * rows, rows), :]
 
 
 def send_kernel(own_in, ylow_ref, yhigh_ref, own, one_ref, two_ref):
@@ -227,20 +240,6 @@
 
 def message_lines(count):
     return FULL1 * count + HALF1 * (count // 2)
-
-
-def spread_kernel(p_ref, after_ref, o_ref, held, came, gone):
-    del after_ref
-    count, rows = o_ref.shape[0], o_ref.shape[2]
-    load = lambda i: pltpu.make_async_copy(p_ref.at[:, pl.ds(i * rows, rows), :], held.at[i], came.at[i])
-    save = lambda i: pltpu.make_async_copy(held.at[i], o_ref.at[i], gone.at[i])
-    for i in range(count):
-        load(i).start()
-    for i in range(count):
-        load(i).wait()
-        save(i).start()
-    for i in range(count):
-        save(i).wait()
 
 
 def columns_of(cols, margin):
@@ -373,9 +372,21 @@
         o_ref[pl.ds(r, LANES, stride=rows), :] = three[r, pl.ds(OFF, cols), :].T
 
 
-def final_kernel(third_ref, prior_ref, reach_ref, avoid_ref, o_ref):
-    kept = jnp.maximum(avoid_ref[...][None], jnp.minimum(reach_ref[...][None], third_ref[...]))
-    o_ref[...] = jnp.minimum(prior_ref[...], kept)
+def final_kernel(third_ref, prior_hbm, reach_ref, avoid_ref, o_hbm, held, came, gone):
+    count = held.shape[0] // came.shape[0]
+    part = lambda i: pl.ds(i * count, count)
+    load = lambda i: pltpu.make_async_copy(prior_hbm.at[part(i)], held.at[part(i)], came.at[i])
+    save = lambda i: pltpu.make_async_copy(held.at[part(i)], o_hbm.at[part(i)], gone.at[i])
+    for i in range(came.shape[0]):
+        load(i).start()
+    reach, avoid = reach_ref[...][None], avoid_ref[...][None]
+    for i in range(came.shape[0]):
+        load(i).wait()
+        kept = jnp.maximum(avoid, jnp.minimum(reach, third_ref[part(i)]))
+        held[part(i)] = jnp.minimum(held[part(i)], kept)
+        save(i).start()
+    for i in range(came.shape[0]):
+        save(i).wait()
 
 
 def on_device(start_value, prior, reach, avoid):
@@ -397,9 +408,7 @@
             compiler_params=pltpu.CompilerParams(vmem_limit_bytes=limit * 2**20),
         )(*args)
 
-    tables = [stage_constants(headings, part) for part in (1.0, 0.25, 2.0 / 3.0)]
-    table = jnp.asarray(np.stack([t[0] for t in tables]))
-    common = dict(turns=[t[1] for t in tables], gap=gap)
+    common = dict(turns=[share * time_step(gap) * TURN / (6.0 * gap) for share in SHARES], gap=gap)
     seg = columns_of(cols, 6)[0]
     wide = cols + 2 * OFF
     tall = (rows + 2 * DEPTH, wide, headings)
@@ -407,11 +416,12 @@
     work = (max(rows - 6, 12), seg, SUB, LANES)
 
     sides = 1 if ny == 2 else 2
-    own, *slabs = call(
+    own, table, *slabs = call(
         prep_kernel,
-        [(rows, wide, headings)] + [(rows, OFF, headings)] * sides,
-        start_value.reshape(headings * rows, cols), table,
+        [(rows, wide, headings), (len(SHARES), 16, headings)] + [(rows, OFF, headings)] * sides,
+        start_value.reshape(headings * rows, cols),
     )
+    blocks = call(spread_kernel, [(nx, headings // nx, rows, cols)], prior)[0]
     pairs1 = [(i, i ^ 1) for i in range(nx)]
     pairs2 = [(i, j) for i in range(nx) for j in [((i + 1) ^ 1) - 1] if 0 <= j < nx]
     if sides == 1:
@@ -429,16 +439,6 @@
     recv2 = lax.ppermute(send2, "px", pairs2)
     inner = call(inner_kernel, [(rows - 6, wide, headings)], table, own, scratch=[work], **common)[0]
 
-    blocks = (nx, headings // nx, rows, cols)
-    hbm = pl.BlockSpec(memory_space=pltpu.HBM)
-    blocks = pl.pallas_call(
-        spread_kernel,
-        out_shape=jax.ShapeDtypeStruct(blocks, f32),
-        in_specs=[hbm, pl.BlockSpec(memory_space=pl.ANY)],
-        out_specs=hbm,
-        scratch_shapes=[pltpu.VMEM(blocks, f32), pltpu.SemaphoreType.DMA((nx,)), pltpu.SemaphoreType.DMA((nx,))],
-        compiler_params=pltpu.CompilerParams(vmem_limit_bytes=61 * 2**20),
-    )(prior, inner)
     regrouped = lax.all_to_all(blocks, "px", split_axis=0, concat_axis=0, tiled=True)
 
     count = columns_of(cols, 3)[0] * SUB
@@ -455,15 +455,17 @@
         last_kernel, [(headings * rows, cols), short, (rows, wide, headings)],
         table, recv1, recv2, own, two, three, aliases={4: 1, 5: 2}, scratch=[work], **common,
     )[0]
-    cut = 16
-    block = pl.BlockSpec((cut, rows, cols), lambda i: (i, 0, 0))
-    plane = pl.BlockSpec((rows, cols), lambda i: (0, 0))
+    pieces = 4
     return pl.pallas_call(
         final_kernel,
-        grid=(headings // cut,),
         out_shape=jax.ShapeDtypeStruct((headings, rows, cols), f32),
-        in_specs=[block, block, plane, plane],
-        out_specs=block,
+        in_specs=[vmem, pl.BlockSpec(memory_space=pl.ANY), vmem, vmem],
+        out_specs=pl.BlockSpec(memory_space=pl.ANY),
+        scratch_shapes=[
+            pltpu.VMEM((headings, rows, cols), f32),
+            pltpu.SemaphoreType.DMA((pieces,)),
+            pltpu.SemaphoreType.DMA((pieces,)),
+        ],
         compiler_params=pltpu.CompilerParams(vmem_limit_bytes=LIMIT * 2**20),
     )(third.reshape(headings, rows, cols), regrouped.reshape(headings, rows, cols), reach, avoid)
 

time: 93.8 us -> 77.2 us (0.82)
  waiting for transfers between devices: 25.8 us -> 18.2 us
  Pallas kernels: 43.3 us -> 38.1 us
  local copies, waits for them, and re-layouts: 3.65 us -> 1.24 us
  starting transfers between devices: 20.3 us -> 19.3 us
    ppermute x2, waiting for transfers between devices: 12.6 us -> 5.28 us  [on_device(): recv1 = lax.ppermute(send1, 'px', pairs1)]
    pallas_call x2 -> x1, Pallas kernels: 7.4 us -> 1.14 us  [on_device(): pl.pallas_call(final_kernel, out_shape=jax.ShapeDtypeStruct((headings, ro...]
    unnamed x18 -> x8, local copies, waits for them, and re-layouts: 3.65 us -> 1.24 us
    pallas_call x6 -> x7, Pallas kernels: 35.9 us -> 37 us  [call(): pl.pallas_call(functools.partial(kernel, **kw) if kw else kernel, out_sha...]
    ppermute x2, starting transfers between devices: 2.5 us -> 1.53 us  [on_device(): recv1 = lax.ppermute(send1, 'px', pairs1)]
  transfers between devices with their start and end apart: 6 -> 6, of which waited for: 3 -> 3; matrix products, arithmetic and copies ran while one was open for 0% -> 0% of each run, Pallas kernels for 31% -> 47%
where the time goes in v6:
time: 77.2 us; the launch traced here: 77 us
  Pallas kernels  38.1 us (49%)
  starting transfers between devices  19.3 us (25%)
  waiting for transfers between devices  18.2 us (24%)
  local copies, waits for them, and re-layouts  1.24 us (2%)
    pallas_call x7, Pallas kernels, call(): pl.pallas_call(functools.partial(kernel, **kw) if kw else kernel, out_sha...  37 us
    ppermute x2, waiting for transfers between devices, on_device(): recv2 = lax.ppermute(send2, 'px', pairs2)  11.6 us
    ppermute x2, starting transfers between devices, on_device(): recv2 = lax.ppermute(send2, 'px', pairs2)  10.5 us
    all_to_all x1, starting transfers between devices, on_device(): lax.all_to_all(blocks, 'px', split_axis=0, concat_axis=0, tiled=True)  7.2 us
    ppermute x2, waiting for transfers between devices, on_device(): recv1 = lax.ppermute(send1, 'px', pairs1)  5.28 us
  transfers between devices with their start and end apart: 6, of which 3 were waited for; matrix products, arithmetic and copies ran while one was open for 0% of the time, Pallas kernels for 47%

profile of v6, /device:TPU:10, one launch (start us, length us, event | category | flops | bytes accessed | tf_op | source)
XLA Modules:
  0.0 77.0 jit_solution(2077479832732860878)
XLA Ops:
  0.0 1.2 %copy-done = f32[8,256,128]{2,1,0:T(8,128)S(1)} copy-done((f32[8,256,128]{2,1,0:T(8,128)S(1)}, f32[8,256,128]{2,1,0:T(8,128)}, u32[]{:S(2)}) %copy-start) | copy-done | bytes 1048600
  1.2 1.0 %shard_map.52 = f32[16,8,16,128]{3,2,1,0:T(8,128)} custom-call(f32[8,256,128]{2,1,0:T(8,128)S(1)} %copy-done), custom_call_target="tpu_custom_call" | custom-call | tf_op jit(solution)/shard_map/pallas_call | solution.py:401
  2.3 7.2 %all-to-all-start = ((f32[16,8,16,128]{3,2,1,0:T(8,128)}), f32[16,8,16,128]{3,2,1,0:T(8,128)S(1)}, u32[]{:S(2)}, u32[]{:S(2)}) async-start(f32[16,8,16,128]{3,2,1,0:T(8,128)} %shard_map.52), calls=%async_computation | async-start | bytes 2097152 | tf_op jit(solution)/shard_map/all_to_all | solution.py:442
  9.5 0.4 shard_map.46
  9.8 0.1 collective-permute-start
  9.9 1.3 %collective-permute-done.ylow_ref.yhigh_ref = f32[16,16,128]{2,1,0:T(8,128)S(1)} collective-permute-done((f32[16,16,128]{2,1,0:T(8,128)S(1)}, f32[16,16,128]{2,1,0:T(8,128)S(1)}, u32[]{:S(2)}, u32[]{:S(2)}) %collective-permute-start) | collective-permute-done | bytes 131104 | tf_op jit(solution)/shard_map/ppermute | solution.py:428
  11.3 0.2 shard_map.47
  11.5 0.6 collective-permute-start.1
  12.1 4.3 %collective-permute-start.2 = (f32[720,128]{1,0:T(8,128)S(1)}, f32[720,128]{1,0:T(8,128)S(1)}, u32[]{:S(2)}, u32[]{:S(2)}) collective-permute-start(f32[720,128]{1,0:T(8,128)S(1)} %get-tuple-element.22), channel_id=1, source_target_pairs={{2,4},{4,2},{6,8},{8,6},{10,12},{12,10},{14,16},{16,14},{18,20},{2... | collective-permute-start | bytes 1105928 | tf_op jit(solution)/shard_map/ppermute | solution.py:439
  16.4 6.1 %shard_map.48.inner = f32[10,160,128]{2,1,0:T(8,128)S(1)} custom-call(f32[3,16,128]{2,1,0:T(8,128)S(1)} %get-tuple-element.18.const_ref, f32[16,160,128]{2,1,0:T(8,128)S(1)} %get-tuple-element.23.own), custom_call_target="tpu_custom_call" | custom-call | tf_op jit(solution)/shard_map/pallas_call | solution.py:401
  22.5 5.3 %collective-permute-done.1.recv1_ref = f32[720,128]{1,0:T(8,128)S(1)} collective-permute-done((f32[720,128]{1,0:T(8,128)S(1)}, f32[720,128]{1,0:T(8,128)S(1)}, u32[]{:S(2)}, u32[]{:S(2)}) %collective-permute-start.1) | collective-permute-done | bytes 368672 | tf_op jit(solution)/shard_map/ppermute | solution.py:438
  27.8 11.6 %collective-permute-done.2.recv2_ref = f32[720,128]{1,0:T(8,128)S(1)} collective-permute-done((f32[720,128]{1,0:T(8,128)S(1)}, f32[720,128]{1,0:T(8,128)S(1)}, u32[]{:S(2)}, u32[]{:S(2)}) %collective-permute-start.2) | collective-permute-done | bytes 368672 | tf_op jit(solution)/shard_map/ppermute | solution.py:439
  39.4 11.8 %shard_map.49 = (f32[22,160,128]{2,1,0:T(8,128)S(1)}, f32[22,160,128]{2,1,0:T(8,128)S(1)}, f32[340,128]{1,0:T(8,128)S(1)}, f32[340,128]{1,0:T(8,128)S(1)}) custom-call(f32[3,16,128]{2,1,0:T(8,128)S(1)} %get-tuple-element.18.const_ref, f32[720,128]{1,0:T(8,128)S(1)} %collective-permute-done.1.recv1_ref, f32[720,128]{1,0:T(8,128)S(1)} %collective-permute-done.2.recv2_ref, ...), custom_call_target="tpu_custom_call" | custom-call | tf_op jit(solution)/shard_map/pallas_call | solution.py:401
  51.2 0.9 %collective-permute-start.3 = (f32[340,128]{1,0:T(8,128)S(1)}, f32[340,128]{1,0:T(8,128)S(1)}, u32[]{:S(2)}, u32[]{:S(2)}) collective-permute-start(f32[340,128]{1,0:T(8,128)S(1)} %get-tuple-element.24), channel_id=1, source_target_pairs={{0,2},{2,0},{4,6},{6,4},{8,10},{10,8},{12,14},{14,12},{16,18},{18,... | collective-permute-start | bytes 522248 | tf_op jit(solution)/shard_map/ppermute | solution.py:449
  52.2 6.2 %collective-permute-start.4 = (f32[340,128]{1,0:T(8,128)S(1)}, f32[340,128]{1,0:T(8,128)S(1)}, u32[]{:S(2)}, u32[]{:S(2)}) collective-permute-start(f32[340,128]{1,0:T(8,128)S(1)} %get-tuple-element.25), channel_id=1, source_target_pairs={{2,4},{4,2},{6,8},{8,6},{10,12},{12,10},{14,16},{16,14},{18,20},{2... | collective-permute-start | bytes 522248 | tf_op jit(solution)/shard_map/ppermute | solution.py:450
  58.4 12.5 %shard_map.50 = (f32[22,160,128]{2,1,0:T(8,128)S(1)}, f32[16,160,128]{2,1,0:T(8,128)S(1)}) custom-call(f32[3,16,128]{2,1,0:T(8,128)S(1)} %get-tuple-element.18.const_ref, f32[16,160,128]{2,1,0:T(8,128)S(1)} %get-tuple-element.23.own, f32[22,160,128]{2,1,0:T(8,128)S(1)} %get-tuple-element.26.one, ...), custom_call_target="tpu_custom_call", output_to_operand_aliasing={{0}: (3, {})} | custom-call | tf_op jit(solution)/shard_map/pallas_call | solution.py:401
  70.9 0.0 collective-permute-done.3.recv1_ref
  70.9 0.0 collective-permute-done.4.recv2_ref
  70.9 0.0 copy-start.2
  70.9 0.0 copy-start.3
  70.9 4.9 %shard_map.51 = (f32[2048,128]{1,0:T(8,128)S(1)}, f32[22,160,128]{2,1,0:T(8,128)S(1)}, f32[16,160,128]{2,1,0:T(8,128)S(1)}) custom-call(f32[3,16,128]{2,1,0:T(8,128)S(1)} %get-tuple-element.18.const_ref, f32[340,128]{1,0:T(8,128)S(1)} %collective-permute-done.3.recv1_ref, ...), custom_call_target="tpu_custom_call", output_to_operand_aliasing={{1}: (4, {}), {2}: (5, {})} | custom-call | tf_op jit(solution)/shard_map/pallas_call | solution.py:401
  75.8 0.0 all-to-all-done
  75.8 0.0 copy-done.2
  75.8 1.1 %shard_map.53 = f32[128,16,128]{2,1,0:T(8,128)} custom-call(f32[128,16,128]{2,1,0:T(8,128)S(1)} %bitcast.4, f32[128,16,128]{2,1,0:T(8,128)S(1)} %bitcast.3, f32[16,128]{1,0:T(8,128)S(1)} %copy-done.2, f32[16,128]{1,0:T(8,128)S(1)} %copy-done.3), custom_call_target="tpu_custom_call" | custom-call | tf_op jit(solution)/shard_map/pallas_call | solution.py:459
  (4 shorter events, 0.0 us)
Async XLA Ops:
  0.0 1.2 %copy-start = (f32[8,256,128]{2,1,0:T(8,128)S(1)}, f32[8,256,128]{2,1,0:T(8,128)}, u32[]{:S(2)}) copy-start(f32[8,256,128]{2,1,0:T(8,128)} %p_ref.1) | copy-start | bytes 3145732
  1.2 8.2 %copy-start.1 = (f32[128,16,128]{2,1,0:T(8,128)S(1)}, f32[128,16,128]{2,1,0:T(8,128)}, u32[]{:S(2)}) copy-start(f32[128,16,128]{2,1,0:T(8,128)} %param.4) | copy-start | bytes 3145732
  2.3 73.6 %all-to-all-start = ((f32[16,8,16,128]{3,2,1,0:T(8,128)}), f32[16,8,16,128]{3,2,1,0:T(8,128)S(1)}, u32[]{:S(2)}, u32[]{:S(2)}) async-start(f32[16,8,16,128]{3,2,1,0:T(8,128)} %shard_map.52), calls=%async_computation | async-start | bytes 2097152 | tf_op jit(solution)/shard_map/all_to_all | solution.py:442
  9.8 1.4 %collective-permute-start = (f32[16,16,128]{2,1,0:T(8,128)S(1)}, f32[16,16,128]{2,1,0:T(8,128)S(1)}, u32[]{:S(2)}, u32[]{:S(2)}) collective-permute-start(f32[16,16,128]{2,1,0:T(8,128)S(1)} %get-tuple-element.20), channel_id=1, source_target_pairs={{0,1},{1,0},{2,3},{3,2},{4,5},{5,4},{6,7},{7,6},{8,9},{9,8},{10,11... | collective-permute-start | bytes 393224 | tf_op jit(solution)/shard_map/ppermute | solution.py:428
  11.5 16.3 %collective-permute-start.1 = (f32[720,128]{1,0:T(8,128)S(1)}, f32[720,128]{1,0:T(8,128)S(1)}, u32[]{:S(2)}, u32[]{:S(2)}) collective-permute-start(f32[720,128]{1,0:T(8,128)S(1)} %get-tuple-element.21), channel_id=1, source_target_pairs={{0,2},{2,0},{4,6},{6,4},{8,10},{10,8},{12,14},{14,12},{16,18},{18,... | collective-permute-start | bytes 1105928 | tf_op jit(solution)/shard_map/ppermute | solution.py:438
  12.1 27.3 %collective-permute-start.2 = (f32[720,128]{1,0:T(8,128)S(1)}, f32[720,128]{1,0:T(8,128)S(1)}, u32[]{:S(2)}, u32[]{:S(2)}) collective-permute-start(f32[720,128]{1,0:T(8,128)S(1)} %get-tuple-element.22), channel_id=1, source_target_pairs={{2,4},{4,2},{6,8},{8,6},{10,12},{12,10},{14,16},{16,14},{18,20},{2... | collective-permute-start | bytes 1105928 | tf_op jit(solution)/shard_map/ppermute | solution.py:439
  51.2 19.7 %collective-permute-start.3 = (f32[340,128]{1,0:T(8,128)S(1)}, f32[340,128]{1,0:T(8,128)S(1)}, u32[]{:S(2)}, u32[]{:S(2)}) collective-permute-start(f32[340,128]{1,0:T(8,128)S(1)} %get-tuple-element.24), channel_id=1, source_target_pairs={{0,2},{2,0},{4,6},{6,4},{8,10},{10,8},{12,14},{14,12},{16,18},{18,... | collective-permute-start | bytes 522248 | tf_op jit(solution)/shard_map/ppermute | solution.py:449
  52.2 18.7 %collective-permute-start.4 = (f32[340,128]{1,0:T(8,128)S(1)}, f32[340,128]{1,0:T(8,128)S(1)}, u32[]{:S(2)}, u32[]{:S(2)}) collective-permute-start(f32[340,128]{1,0:T(8,128)S(1)} %get-tuple-element.25), channel_id=1, source_target_pairs={{2,4},{4,2},{6,8},{8,6},{10,12},{12,10},{14,16},{16,14},{18,20},{2... | collective-permute-start | bytes 522248 | tf_op jit(solution)/shard_map/ppermute | solution.py:450
  70.9 4.9 %copy-start.2 = (f32[16,128]{1,0:T(8,128)S(1)}, f32[16,128]{1,0:T(8,128)}, u32[]{:S(2)}) copy-start(f32[16,128]{1,0:T(8,128)} %reach_ref.1) | copy-start | bytes 24580
  70.9 4.9 %copy-start.3 = (f32[16,128]{1,0:T(8,128)S(1)}, f32[16,128]{1,0:T(8,128)}, u32[]{:S(2)}) copy-start(f32[16,128]{1,0:T(8,128)} %avoid_ref.1) | copy-start | bytes 24580

commit v7 on v6

--- a/solution.py
+++ b/solution.py
@@ -70,26 +70,62 @@
     return faces
 
 
-def turning(v, eps):
-    ahead = lambda x: pltpu.roll(x, LANES - 1, x.ndim - 1)
-    behind = lambda x: pltpu.roll(x, 1, x.ndim - 1)
-    u = ahead(v) - v
-    w = u - behind(u)
-    wn = ahead(w)
-    d = wn - w
-    low, mid, high = weights_of(w, wn, d, eps, "LCR")
-    m1 = behind(low)
-    m3 = ahead(high)
-    g1 = d - behind(d)
-    g2 = ahead(g1)
-    v0 = (m1 + m3) * 0.5 + mid * 3.0
-    a1 = m1 * g1
-    a3 = m3 * g2
-    s = w + wn
-    top = u * 6.0 + wn + s
-    back = (a1 + 1.5 * a3) * inverse(v0 + m3) - top
-    fore = (top - 3.0 * s) + (a3 + 1.5 * a1) * inverse(v0 + m1)
-    return jnp.minimum(behind(back), fore)
+def turning(vals, eps):
+    n = len(vals)
+    u = [vals[i + 1] - vals[i] for i in range(n - 1)]
+    w = [None] + [u[i] - u[i - 1] for i in range(1, n - 1)]
+    d = [None] + [w[i + 1] - w[i] for i in range(1, n - 2)]
+    tri = [None] + [weights_of(w[i], w[i + 1], d[i], eps, "LCR") for i in range(1, n - 2)]
+    third = [None, None] + [d[i] - d[i - 1] for i in range(2, n - 2)]
+    out = []
+    back = None
+    for k in range(2, n - 3):
+        m1 = tri[k - 1][0]
+        m3 = tri[k + 1][2]
+        v0 = (m1 + m3) * 0.5 + tri[k][1] * 3.0
+        a1 = m1 * third[k]
+        a3 = m3 * third[k + 1]
+        s = w[k] + w[k + 1]
+        top = u[k] * 6.0 + w[k + 1] + s
+        if k > 2:
+            out.append(jnp.minimum(back, (top - 3.0 * s) + (a3 + 1.5 * a1) * inverse(v0 + m1)))
+        back = (a1 + 1.5 * a3) * inverse(v0 + m3) - top
+    return out
+
+
+def turn_blocks(flat, turned, across, result, blocks, eps, turn):
+    span = LANES // SUB
+
+    def bring(b, slot):
+        tile = flat[pl.ds(pl.multiple_of(b * LANES, LANES), LANES), :].T
+        across[slot, pl.ds(SUB, LANES), :] = tile
+        across[slot, pl.ds(0, SUB), :] = tile[LANES - SUB :]
+        across[slot, pl.ds(SUB + LANES, SUB), :] = tile[:SUB]
+
+    def work(slot):
+        vals = [across[slot, pl.ds(SUB + j, SUB, stride=span), :] for j in range(-3, span + 3)]
+        for j, x in enumerate(turning(vals, eps)):
+            result[slot, pl.ds(j, SUB, stride=span), :] = turn * x
+
+    def back(b, slot):
+        turned[pl.ds(pl.multiple_of(b * LANES, LANES), LANES), :] = result[slot].T
+
+    bring(0, 0)
+
+    @pl.loop(0, blocks // 2)
+    def _(c):
+        b = 2 * c
+        back(jnp.maximum(b - 1, 0), 1)
+        work(0)
+        bring(b + 1, 1)
+        back(b, 0)
+        work(1)
+        bring(jnp.minimum(b + 2, blocks - 1), 0)
+
+    back(2 * (blocks // 2) - 1, 1)
+    if blocks % 2:
+        work(0)
+        back(blocks - 1, 0)
 
 
 def lanes_of(shape):
@@ -244,6 +280,8 @@
 
 def columns_of(cols, margin):
     seg = ceil_div(cols + 2 * margin, SUB)
+    if seg % SUB == 0:
+        seg += 1
     return seg, -((seg * SUB - cols) // 2)
 
 
@@ -252,6 +290,7 @@
     seg, start = columns_of(cols, margin)
     eps_xy = 0.5 * EPS * SPACING**2
     eps_t = 0.5 * EPS * gap**2
+    part, flat, turned, across, result = part
     weights = (None, (0.25, 0.75), (2.0 / 3.0, 1.0 / 3.0))[index]
 
     def column(array, row, j):
@@ -278,9 +317,11 @@
                 if weights is not None:
                     here = here * weights[0] + column(base, r, j) * weights[1]
                 part[at, j] = here + move
+                flat[pl.ds(at * seg * SUB + j, SUB, stride=seg), :] = vals[i]
                 at += 1
 
     counts = [hi - lo for lo, hi in parts]
+    turn_blocks(flat, turned, across, result, ceil_div(sum(counts) * seg * SUB, LANES), eps_t, turn)
 
     @pl.loop(0, sum(counts))
     def _(t):
@@ -292,7 +333,7 @@
         for j in range(seg):
             i = j + 3
             move = jnp.where(ymask, faces[i], faces[i - 1])
-            out = part[t, j] + move + turn * turning(vals[i], eps_t)
+            out = part[t, j] + move + turned[pl.ds(t * seg * SUB + j, SUB, stride=seg), :]
             dst[0][row + dst[1], pl.ds(OFF + start + j, SUB, stride=seg), :] = out
 
 
@@ -306,7 +347,7 @@
                 dst[0][pl.ds(lo + dst[1], hi - lo), pl.ds(begin, OFF), :] = jnp.zeros((hi - lo, OFF, LANES), jnp.float32)
 
 
-def inner_kernel(const_ref, own, one, part, *, turns, gap):
+def inner_kernel(const_ref, own, one, *part, turns, gap):
     rows, wide = own.shape[:2]
     cols = wide - 2 * OFF
     parts = [(3, rows - 3)]
@@ -314,7 +355,7 @@
     clear_columns((one, -3), parts, cols)
 
 
-def outer_kernel(const_ref, recv1_ref, recv2_ref, own, inner, one, two, send1, send2, field, part, *, turns, gap):
+def outer_kernel(const_ref, recv1_ref, recv2_ref, own, inner, one, two, send1, send2, field, *part, turns, gap):
     rows, wide = own.shape[:2]
     cols = wide - 2 * OFF
 
@@ -346,7 +387,7 @@
     pack_pair(send1, send2, lambda r: two[r + 3, pl.ds(OFF + start, count), :], rows, count, FULL2, HALF2)
 
 
-def middle_kernel(const_ref, own, one, two_in, two, three, part, *, turns, gap):
+def middle_kernel(const_ref, own, one, two_in, two, three, *part, turns, gap):
     del two_in
     rows, wide = own.shape[:2]
     cols = wide - 2 * OFF
@@ -356,7 +397,7 @@
     stage(2, (two, 3), (three, 0), (own, 0), part, const_ref, parts, (cols, 0, gap), turns[2])
 
 
-def last_kernel(const_ref, recv1_ref, recv2_ref, own, two_in, three_in, o_ref, two, three, part, *, turns, gap):
+def last_kernel(const_ref, recv1_ref, recv2_ref, own, two_in, three_in, o_ref, two, three, *part, turns, gap):
     del two_in, three_in
     rows, wide = own.shape[:2]
     cols = wide - 2 * OFF
@@ -413,7 +454,15 @@
     wide = cols + 2 * OFF
     tall = (rows + 2 * DEPTH, wide, headings)
     short = (rows + 6, wide, headings)
-    work = (max(rows - 6, 12), seg, SUB, LANES)
+    most = max(rows - 6, 12)
+    lines = ceil_div(most * seg * SUB, LANES) * LANES
+    work = [
+        (most, seg, SUB, LANES),
+        (lines, LANES),
+        (lines, LANES),
+        (2, LANES + 2 * SUB, LANES),
+        (2, LANES, LANES),
+    ]
 
     sides = 1 if ny == 2 else 2
     own, table, *slabs = call(
@@ -431,29 +480,29 @@
             lax.ppermute(slabs[0], "py", [(i, i + 1) for i in range(ny - 1)]),
             lax.ppermute(slabs[1], "py", [(i + 1, i) for i in range(ny - 1)]),
         ]
-    lines = message_lines(cols) + sides * message_lines(OFF)
+    length = message_lines(cols) + sides * message_lines(OFF)
     own, send1, send2 = call(
-        send_kernel, [(rows, wide, headings)] + [(lines, headings)] * 2, own, yslabs[0], yslabs[-1], aliases={0: 0}
+        send_kernel, [(rows, wide, headings)] + [(length, headings)] * 2, own, yslabs[0], yslabs[-1], aliases={0: 0}
     )
     recv1 = lax.ppermute(send1, "px", pairs1)
     recv2 = lax.ppermute(send2, "px", pairs2)
-    inner = call(inner_kernel, [(rows - 6, wide, headings)], table, own, scratch=[work], **common)[0]
+    inner = call(inner_kernel, [(rows - 6, wide, headings)], table, own, scratch=work, **common)[0]
 
     regrouped = lax.all_to_all(blocks, "px", split_axis=0, concat_axis=0, tiled=True)
 
     count = columns_of(cols, 3)[0] * SUB
     message = (FULL2 * count + HALF2 * count // 2, headings)
     one, two, send1, send2 = call(
-        outer_kernel, [short, short, message, message], table, recv1, recv2, own, inner, scratch=[tall, work], **common
+        outer_kernel, [short, short, message, message], table, recv1, recv2, own, inner, scratch=[tall] + work, **common
     )
     recv1 = lax.ppermute(send1, "px", pairs1)
     recv2 = lax.ppermute(send2, "px", pairs2)
     two, three = call(
-        middle_kernel, [short, (rows, wide, headings)], table, own, one, two, aliases={3: 0}, scratch=[work], **common
+        middle_kernel, [short, (rows, wide, headings)], table, own, one, two, aliases={3: 0}, scratch=work, **common
     )
     third = call(
         last_kernel, [(headings * rows, cols), short, (rows, wide, headings)],
-        table, recv1, recv2, own, two, three, aliases={4: 1, 5: 2}, scratch=[work], **common,
+        table, recv1, recv2, own, two, three, aliases={4: 1, 5: 2}, scratch=work, **common,
     )[0]
     pieces = 4
     return pl.pallas_call(

time: 77.2 us -> 68.8 us (0.89)
  Pallas kernels: 38.1 us -> 28.1 us
  waiting for transfers between devices: 18.2 us -> 19.9 us
    pallas_call x7, Pallas kernels: 37 us -> 27 us  [call(): pl.pallas_call(functools.partial(kernel, **kw) if kw else kernel, out_sha...]
    ppermute x2, waiting for transfers between devices: 5.28 us -> 6.92 us  [on_device(): recv1 = lax.ppermute(send1, 'px', pairs1)]
  transfers between devices with their start and end apart: 6 -> 6, of which waited for: 3 -> 3; matrix products, arithmetic and copies ran while one was open for 0% -> 0% of each run, Pallas kernels for 47% -> 38%
where the time goes in v7:
time: 68.8 us; the launch traced here: 68.6 us
  Pallas kernels  28.1 us (41%)
  waiting for transfers between devices  19.9 us (29%)
  starting transfers between devices  19.3 us (28%)
  local copies, waits for them, and re-layouts  1.24 us (2%)
    pallas_call x7, Pallas kernels, call(): pl.pallas_call(functools.partial(kernel, **kw) if kw else kernel, out_sha...  27 us
    ppermute x2, waiting for transfers between devices, on_device(): recv2 = lax.ppermute(send2, 'px', pairs2)  11.6 us
    ppermute x2, starting transfers between devices, on_device(): recv2 = lax.ppermute(send2, 'px', pairs2)  10.5 us
    all_to_all x1, starting transfers between devices, on_device(): lax.all_to_all(blocks, 'px', split_axis=0, concat_axis=0, tiled=True)  7.2 us
    ppermute x2, waiting for transfers between devices, on_device(): recv1 = lax.ppermute(send1, 'px', pairs1)  6.92 us
    ppermute x2, starting transfers between devices, on_device(): recv1 = lax.ppermute(send1, 'px', pairs1)  1.53 us
  transfers between devices with their start and end apart: 6, of which 3 were waited for; matrix products, arithmetic and copies ran while one was open for 0% of the time, Pallas kernels for 38%

profile of v7, /device:TPU:10, one launch (start us, length us, event | category | flops | bytes accessed | tf_op | source)
XLA Modules:
  0.0 68.6 jit_solution(16940431329352215845)
XLA Ops:
  0.0 1.2 %copy-done = f32[8,256,128]{2,1,0:T(8,128)S(1)} copy-done((f32[8,256,128]{2,1,0:T(8,128)S(1)}, f32[8,256,128]{2,1,0:T(8,128)}, u32[]{:S(2)}) %copy-start) | copy-done | bytes 1048600
  1.2 1.0 %shard_map.52 = f32[16,8,16,128]{3,2,1,0:T(8,128)} custom-call(f32[8,256,128]{2,1,0:T(8,128)S(1)} %copy-done), custom_call_target="tpu_custom_call" | custom-call | tf_op jit(solution)/shard_map/pallas_call | solution.py:442
  2.3 7.2 %all-to-all-start = ((f32[16,8,16,128]{3,2,1,0:T(8,128)}), f32[16,8,16,128]{3,2,1,0:T(8,128)S(1)}, u32[]{:S(2)}, u32[]{:S(2)}) async-start(f32[16,8,16,128]{3,2,1,0:T(8,128)} %shard_map.52), calls=%async_computation | async-start | bytes 2097152 | tf_op jit(solution)/shard_map/all_to_all | solution.py:491
  9.5 0.0 copy-done.1
  9.5 0.4 shard_map.46
  9.8 0.1 collective-permute-start
  9.9 1.3 %collective-permute-done.ylow_ref.yhigh_ref = f32[16,16,128]{2,1,0:T(8,128)S(1)} collective-permute-done((f32[16,16,128]{2,1,0:T(8,128)S(1)}, f32[16,16,128]{2,1,0:T(8,128)S(1)}, u32[]{:S(2)}, u32[]{:S(2)}) %collective-permute-start) | collective-permute-done | bytes 131104 | tf_op jit(solution)/shard_map/ppermute | solution.py:477
  11.3 0.2 shard_map.47
  11.5 0.6 collective-permute-start.1
  12.1 4.3 %collective-permute-start.2 = (f32[720,128]{1,0:T(8,128)S(1)}, f32[720,128]{1,0:T(8,128)S(1)}, u32[]{:S(2)}, u32[]{:S(2)}) collective-permute-start(f32[720,128]{1,0:T(8,128)S(1)} %get-tuple-element.22), channel_id=1, source_target_pairs={{2,4},{4,2},{6,8},{8,6},{10,12},{12,10},{14,16},{16,14},{18,20},{2... | collective-permute-start | bytes 1105928 | tf_op jit(solution)/shard_map/ppermute | solution.py:488
  16.4 4.5 %shard_map.48.inner = f32[10,160,128]{2,1,0:T(8,128)S(1)} custom-call(f32[3,16,128]{2,1,0:T(8,128)S(1)} %get-tuple-element.18.const_ref, f32[16,160,128]{2,1,0:T(8,128)S(1)} %get-tuple-element.23.own), custom_call_target="tpu_custom_call" | custom-call | tf_op jit(solution)/shard_map/pallas_call | solution.py:442
  20.9 6.9 %collective-permute-done.1.recv1_ref = f32[720,128]{1,0:T(8,128)S(1)} collective-permute-done((f32[720,128]{1,0:T(8,128)S(1)}, f32[720,128]{1,0:T(8,128)S(1)}, u32[]{:S(2)}, u32[]{:S(2)}) %collective-permute-start.1) | collective-permute-done | bytes 368672 | tf_op jit(solution)/shard_map/ppermute | solution.py:487
  27.8 11.6 %collective-permute-done.2.recv2_ref = f32[720,128]{1,0:T(8,128)S(1)} collective-permute-done((f32[720,128]{1,0:T(8,128)S(1)}, f32[720,128]{1,0:T(8,128)S(1)}, u32[]{:S(2)}, u32[]{:S(2)}) %collective-permute-start.2) | collective-permute-done | bytes 368672 | tf_op jit(solution)/shard_map/ppermute | solution.py:488
  39.4 8.8 %shard_map.49 = (f32[22,160,128]{2,1,0:T(8,128)S(1)}, f32[22,160,128]{2,1,0:T(8,128)S(1)}, f32[340,128]{1,0:T(8,128)S(1)}, f32[340,128]{1,0:T(8,128)S(1)}) custom-call(f32[3,16,128]{2,1,0:T(8,128)S(1)} %get-tuple-element.18.const_ref, f32[720,128]{1,0:T(8,128)S(1)} %collective-permute-done.1.recv1_ref, f32[720,128]{1,0:T(8,128)S(1)} %collective-permute-done.2.recv2_ref, ...), custom_call_target="tpu_custom_call" | custom-call | tf_op jit(solution)/shard_map/pallas_call | solution.py:442
  48.2 0.9 %collective-permute-start.3 = (f32[340,128]{1,0:T(8,128)S(1)}, f32[340,128]{1,0:T(8,128)S(1)}, u32[]{:S(2)}, u32[]{:S(2)}) collective-permute-start(f32[340,128]{1,0:T(8,128)S(1)} %get-tuple-element.24), channel_id=1, source_target_pairs={{0,2},{2,0},{4,6},{6,4},{8,10},{10,8},{12,14},{14,12},{16,18},{18,... | collective-permute-start | bytes 522248 | tf_op jit(solution)/shard_map/ppermute | solution.py:498
  49.1 6.2 %collective-permute-start.4 = (f32[340,128]{1,0:T(8,128)S(1)}, f32[340,128]{1,0:T(8,128)S(1)}, u32[]{:S(2)}, u32[]{:S(2)}) collective-permute-start(f32[340,128]{1,0:T(8,128)S(1)} %get-tuple-element.25), channel_id=1, source_target_pairs={{2,4},{4,2},{6,8},{8,6},{10,12},{12,10},{14,16},{16,14},{18,20},{2... | collective-permute-start | bytes 522248 | tf_op jit(solution)/shard_map/ppermute | solution.py:499
  55.4 8.5 %shard_map.50 = (f32[22,160,128]{2,1,0:T(8,128)S(1)}, f32[16,160,128]{2,1,0:T(8,128)S(1)}) custom-call(f32[3,16,128]{2,1,0:T(8,128)S(1)} %get-tuple-element.18.const_ref, f32[16,160,128]{2,1,0:T(8,128)S(1)} %get-tuple-element.23.own, f32[22,160,128]{2,1,0:T(8,128)S(1)} %get-tuple-element.26.one, ...), custom_call_target="tpu_custom_call", output_to_operand_aliasing={{0}: (3, {})} | custom-call | tf_op jit(solution)/shard_map/pallas_call | solution.py:442
  63.8 0.0 collective-permute-done.3.recv1_ref
  63.8 0.0 collective-permute-done.4.recv2_ref
  63.9 0.0 copy-start.2
  63.9 0.0 copy-start.3
  63.9 3.5 %shard_map.51 = (f32[2048,128]{1,0:T(8,128)S(1)}, f32[22,160,128]{2,1,0:T(8,128)S(1)}, f32[16,160,128]{2,1,0:T(8,128)S(1)}) custom-call(f32[3,16,128]{2,1,0:T(8,128)S(1)} %get-tuple-element.18.const_ref, f32[340,128]{1,0:T(8,128)S(1)} %collective-permute-done.3.recv1_ref, ...), custom_call_target="tpu_custom_call", output_to_operand_aliasing={{1}: (4, {}), {2}: (5, {})} | custom-call | tf_op jit(solution)/shard_map/pallas_call | solution.py:442
  67.4 0.0 all-to-all-done
  67.5 1.1 %shard_map.53 = f32[128,16,128]{2,1,0:T(8,128)} custom-call(f32[128,16,128]{2,1,0:T(8,128)S(1)} %bitcast.4, f32[128,16,128]{2,1,0:T(8,128)S(1)} %bitcast.3, f32[16,128]{1,0:T(8,128)S(1)} %copy-done.2, f32[16,128]{1,0:T(8,128)S(1)} %copy-done.3), custom_call_target="tpu_custom_call" | custom-call | tf_op jit(solution)/shard_map/pallas_call | solution.py:508
  (4 shorter events, 0.0 us)
Async XLA Ops:
  0.0 1.2 %copy-start = (f32[8,256,128]{2,1,0:T(8,128)S(1)}, f32[8,256,128]{2,1,0:T(8,128)}, u32[]{:S(2)}) copy-start(f32[8,256,128]{2,1,0:T(8,128)} %p_ref.1) | copy-start | bytes 3145732
  1.2 8.2 %copy-start.1 = (f32[128,16,128]{2,1,0:T(8,128)S(1)}, f32[128,16,128]{2,1,0:T(8,128)}, u32[]{:S(2)}) copy-start(f32[128,16,128]{2,1,0:T(8,128)} %param.4) | copy-start | bytes 3145732
  2.3 65.2 %all-to-all-start = ((f32[16,8,16,128]{3,2,1,0:T(8,128)}), f32[16,8,16,128]{3,2,1,0:T(8,128)S(1)}, u32[]{:S(2)}, u32[]{:S(2)}) async-start(f32[16,8,16,128]{3,2,1,0:T(8,128)} %shard_map.52), calls=%async_computation | async-start | bytes 2097152 | tf_op jit(solution)/shard_map/all_to_all | solution.py:491
  9.8 1.4 %collective-permute-start = (f32[16,16,128]{2,1,0:T(8,128)S(1)}, f32[16,16,128]{2,1,0:T(8,128)S(1)}, u32[]{:S(2)}, u32[]{:S(2)}) collective-permute-start(f32[16,16,128]{2,1,0:T(8,128)S(1)} %get-tuple-element.20), channel_id=1, source_target_pairs={{0,1},{1,0},{2,3},{3,2},{4,5},{5,4},{6,7},{7,6},{8,9},{9,8},{10,11... | collective-permute-start | bytes 393224 | tf_op jit(solution)/shard_map/ppermute | solution.py:477
  11.5 16.3 %collective-permute-start.1 = (f32[720,128]{1,0:T(8,128)S(1)}, f32[720,128]{1,0:T(8,128)S(1)}, u32[]{:S(2)}, u32[]{:S(2)}) collective-permute-start(f32[720,128]{1,0:T(8,128)S(1)} %get-tuple-element.21), channel_id=1, source_target_pairs={{0,2},{2,0},{4,6},{6,4},{8,10},{10,8},{12,14},{14,12},{16,18},{18,... | collective-permute-start | bytes 1105928 | tf_op jit(solution)/shard_map/ppermute | solution.py:487
  12.1 27.3 %collective-permute-start.2 = (f32[720,128]{1,0:T(8,128)S(1)}, f32[720,128]{1,0:T(8,128)S(1)}, u32[]{:S(2)}, u32[]{:S(2)}) collective-permute-start(f32[720,128]{1,0:T(8,128)S(1)} %get-tuple-element.22), channel_id=1, source_target_pairs={{2,4},{4,2},{6,8},{8,6},{10,12},{12,10},{14,16},{16,14},{18,20},{2... | collective-permute-start | bytes 1105928 | tf_op jit(solution)/shard_map/ppermute | solution.py:488
  48.2 15.6 %collective-permute-start.3 = (f32[340,128]{1,0:T(8,128)S(1)}, f32[340,128]{1,0:T(8,128)S(1)}, u32[]{:S(2)}, u32[]{:S(2)}) collective-permute-start(f32[340,128]{1,0:T(8,128)S(1)} %get-tuple-element.24), channel_id=1, source_target_pairs={{0,2},{2,0},{4,6},{6,4},{8,10},{10,8},{12,14},{14,12},{16,18},{18,... | collective-permute-start | bytes 522248 | tf_op jit(solution)/shard_map/ppermute | solution.py:498
  49.1 14.7 %collective-permute-start.4 = (f32[340,128]{1,0:T(8,128)S(1)}, f32[340,128]{1,0:T(8,128)S(1)}, u32[]{:S(2)}, u32[]{:S(2)}) collective-permute-start(f32[340,128]{1,0:T(8,128)S(1)} %get-tuple-element.25), channel_id=1, source_target_pairs={{2,4},{4,2},{6,8},{8,6},{10,12},{12,10},{14,16},{16,14},{18,20},{2... | collective-permute-start | bytes 522248 | tf_op jit(solution)/shard_map/ppermute | solution.py:499
  63.9 3.6 %copy-start.2 = (f32[16,128]{1,0:T(8,128)S(1)}, f32[16,128]{1,0:T(8,128)}, u32[]{:S(2)}) copy-start(f32[16,128]{1,0:T(8,128)} %reach_ref.1) | copy-start | bytes 24580
  63.9 3.6 %copy-start.3 = (f32[16,128]{1,0:T(8,128)S(1)}, f32[16,128]{1,0:T(8,128)}, u32[]{:S(2)}) copy-start(f32[16,128]{1,0:T(8,128)} %avoid_ref.1) | copy-start | bytes 24580
